TPU v7x, 256 devices: a whole 4x4x8 slice. The times are simulated.
256 devices in a mesh: depth: 8 (over z), imgy: 8 (over y, core), imgx: 4 (over x).
Axes of the slice: x: 4, y: 4, z: 8, core: 2. Of those that a mesh axis runs over, the one named last changes fastest.
Arguments:
- coefficients: float32 [512, 512, 512], P('depth', 'imgy', 'imgx'), may hold values from -6 to 6
- shifts: int32 [2, 512], P(None, 'depth'), may hold values from -63 to 63, as said below
- fraction: float32 [2, 512], P(None, 'depth'), may hold values from 0 to 1
- absorb: float32 [512], P('depth'), may hold values from 0.3 to 3
Outputs:
- image: float32 [4, 8, 64, 512], P(None, 'imgy', 'depth', 'imgx')
Inputs may be any that keep to these rules, and one draw needn't show every extreme that they name: `shifts`: each of the two rows is non-decreasing along the slices; slice 0 has the smallest value and slice 512 - 1 the largest.
All inputs are finite; a program needn't handle non-finite values.
Results may differ from a plain program's by a relative error of at most 0.0003.
Values sent between devices are 32-bit elements; how exact they have to be, the bound alone decides.
No kernel may reach another device: no remote copies, remote signals or barrier semaphores. Data moves between devices by JAX's collectives and lax.ppermute only.
A program may use at most 128 MiB of HBM per device.

v0:
```python
import jax
import jax.numpy as jnp
from jax import lax
from jax.sharding import PartitionSpec as P

BRICK = 64
LEVELS = 3


def with_halo(shard, sides, width):
    for axis, dim in sides:
        devices, length = (lax.axis_size(axis), shard.shape[dim])
        up = [(i, (i + 1) % devices) for i in range(devices - 1)]
        down = [(j, i) for i, j in up]
        last = lax.slice_in_dim(shard, length - width, length, axis=dim)
        leading = lax.slice_in_dim(shard, 0, width, axis=dim)
        before = lax.ppermute(last, axis, up)
        after = lax.ppermute(leading, axis, down)
        shard = jnp.concatenate([before, shard, after], axis=dim)
    return shard


def inverse_step(cube_block, dimension, half_span):
    low_part = lax.slice_in_dim(cube_block, 0, half_span, axis=dimension)
    high_part = lax.slice_in_dim(cube_block, half_span, 2 * half_span, axis=dimension)
    even_cells = low_part - 0.5 * high_part
    odd_cells = even_cells + high_part
    joined = jnp.stack([even_cells, odd_cells], axis=dimension + 1)
    return joined.reshape(cube_block.shape)


def column_table(width, half_span):
    source = lax.broadcasted_iota(jnp.int32, (width, width), 0)
    target = lax.broadcasted_iota(jnp.int32, (width, width), 1)
    local_col = target % BRICK
    brick_start = target - local_col
    pair_index = local_col // 2
    is_odd = local_col % 2
    inside = local_col < 2 * half_span
    low_index = brick_start + pair_index
    high_index = brick_start + half_span + pair_index
    high_weight = jnp.where(is_odd == 1, 0.5, -0.5).astype(jnp.float32)
    lifted = jnp.where(source == low_index, 1.0, 0.0).astype(jnp.float32) + jnp.where(
        source == high_index, high_weight, 0.0
    )
    same = jnp.where(source == target, 1.0, 0.0).astype(jnp.float32)
    return jnp.where(inside, lifted, same)


def inverse_lift(volume):
    slab_cells, row_cells, width = volume.shape
    row_bricks = row_cells // BRICK
    volume = volume.reshape(slab_cells, row_bricks, BRICK, width)
    column = lax.broadcasted_iota(jnp.int32, (width,), 0) % BRICK
    for level_index in reversed(range(LEVELS)):
        half_span = BRICK >> level_index + 1
        full_span = 2 * half_span
        corner_block = volume[:full_span, :, :full_span, :]
        lifted = inverse_step(corner_block, 0, half_span)
        lifted = inverse_step(lifted, 2, half_span)
        lifted = jnp.where((column < full_span)[None, None, None, :], lifted, corner_block)
        product = jnp.dot(
            lifted.reshape(full_span * row_bricks * full_span, width),
            column_table(width, half_span),
            precision=lax.Precision.HIGHEST,
            preferred_element_type=jnp.float32,
        )
        volume = volume.at[:full_span, :, :full_span, :].set(
            product.reshape(full_span, row_bricks, full_span, width)
        )
    return volume.reshape(slab_cells, row_cells, width)


def palette(sheared):
    return jnp.stack(
        [
            jax.nn.sigmoid(1.5 * sheared),
            jnp.exp(-0.5 * sheared * sheared),
            jax.nn.sigmoid(0.8 - sheared),
        ],
        axis=0,
    )


def shear_table(offsets, weights, out_cells, in_cells):
    count = offsets.shape[0]
    target = lax.broadcasted_iota(jnp.int32, (count, out_cells, in_cells), 1)
    source = lax.broadcasted_iota(jnp.int32, (count, out_cells, in_cells), 2)
    base = target + BRICK - offsets[:, None, None]
    near = jnp.where(source == base, 1.0 - weights[:, None, None], 0.0)
    far = jnp.where(source == base - 1, weights[:, None, None], 0.0)
    return near + far


def over_pair(front, behind):
    color_part = front[:3] + jnp.exp(-front[3])[None] * behind[:3]
    return jnp.concatenate([color_part, (front[3] + behind[3])[None]], axis=0)


def body(coefficients, shifts, fraction, absorb):
    slab_cells = coefficients.shape[0]
    row_cells = coefficients.shape[1]
    width = coefficients.shape[2]
    volume = inverse_lift(coefficients)
    padded = with_halo(volume, (("imgy", 1), ("imgx", 2)), BRICK)
    row_table = shear_table(shifts[0], fraction[0], row_cells, padded.shape[1])
    col_table = shear_table(shifts[1], fraction[1], width, padded.shape[2])
    row_moved = jnp.einsum(
        "zyp,zpq->zyq",
        row_table,
        padded,
        precision=lax.Precision.HIGHEST,
        preferred_element_type=jnp.float32,
    )
    sheared = jnp.einsum(
        "zyq,zxq->zyx",
        row_moved,
        col_table,
        precision=lax.Precision.HIGHEST,
        preferred_element_type=jnp.float32,
    )
    slices_total = slab_cells * lax.axis_size("depth")
    optical = absorb[:, None, None] * (2.0 / slices_total) * jax.nn.softplus(sheared)
    before = jnp.cumsum(optical, axis=0) - optical
    emission = (1.0 - jnp.exp(-optical))[None] * palette(sheared)
    radiance = jnp.sum(jnp.exp(-before)[None] * emission, axis=1)
    slab_depth = jnp.sum(optical, axis=0)
    pieces = jnp.concatenate([radiance, slab_depth[None]], axis=0)[None]
    incoming = lax.all_to_all(pieces, "depth", split_axis=2, concat_axis=0, tiled=True)

    def fold_over(running, piece):
        return (over_pair(running, piece), None)

    start_state = jnp.zeros(incoming.shape[1:], jnp.float32)
    merged, _ = lax.scan(fold_over, start_state, incoming)
    image = jnp.concatenate([merged[:3], (1.0 - jnp.exp(-merged[3]))[None]], axis=0)
    return image[:, None]


def solution(mesh):
    in_specs = (P("depth", "imgy", "imgx"), P(None, "depth"), P(None, "depth"), P("depth"))
    out_specs = P(None, "imgy", "depth", "imgx")
    return jax.shard_map(body, mesh=mesh, in_specs=in_specs, out_specs=out_specs, check_vma=False)
```

profile of v0, /device:TPU:20, one launch (start us, length us, event | category | flops | bytes accessed | tf_op | source)
XLA Modules:
  0.0 216.2 jit_solution(6759404046488984473)
XLA Ops:
  0.0 1.6 copy.63
  1.7 0.1 fusion.50
  1.8 0.3 fusion.45
  2.1 0.1 fusion.55
  2.3 0.4 copy.39
  2.7 0.1 fusion.47
  2.8 0.6 fusion.44
  3.4 0.2 fusion.48
  3.7 0.2 pad_maximum_fusion.2
  3.9 0.2 copy.40
  4.2 0.3 fusion.49
  4.5 0.2 pad_maximum_fusion.3
  4.6 1.9 copy.41
  6.6 1.9 fusion.35
  8.5 0.0 copy-start
  8.5 1.9 collective-permute-start
  10.4 3.6 %collective-permute-start.1 = (f32[64,64,128]{2,1,0:T(8,128)S(1)}, f32[64,64,128]{2,1,0:T(8,128)S(1)}, u32[]{:S(2)}, u32[]{:S(2)}) collective-permute-start(f32[64,64,128]{2,1,0:T(8,128)S(1)} %fusion.35), channel_id=1, source_target_pairs={{4,0},{8,4},{12,8},{16,12},{20,16},{24,20},{28,24},{5,1},{9,5},{13... | collective-permute-start | bytes 6291464 | tf_op jit(solution)/shard_map/ppermute | solution.py:18
  14.1 21.8 %collective-permute-done = f32[64,64,128]{2,1,0:T(8,128)S(1)} collective-permute-done((f32[64,64,128]{2,1,0:T(8,128)S(1)}, f32[64,64,128]{2,1,0:T(8,128)S(1)}, u32[]{:S(2)}, u32[]{:S(2)}) %collective-permute-start) | collective-permute-done | bytes 2097184 | tf_op jit(solution)/shard_map/ppermute | solution.py:17
  35.8 1.8 collective-permute-done.1
  37.6 0.0 copy-done
  37.6 0.0 copy-done.2
  37.6 1.3 copy-done.3
  38.9 0.4 pad_maximum_fusion.1
  39.4 6.9 %fusion.149 = (f32[64,192,64]{2,1,0:T(8,128)}, f32[64,192,64]{2,1,0:T(8,128)}) fusion(f32[64,192,128]{2,1,0:T(8,128)S(1)} %pad_maximum_fusion.1), kind=kLoop, calls=%fused_computation.218 | loop fusion | bytes 12582912 | tf_op jit(solution)/shard_map/slice | solution.py:15
  46.3 6.3 %copy.42 = f32[64,192,64]{1,2,0:T(8,128)} copy(f32[64,192,64]{2,1,0:T(8,128)} %get-tuple-element.87) | data formatting | bytes 6291456 | tf_op jit(solution)/shard_map/slice | solution.py:15
  52.6 3.1 %collective-permute-start.2 = (f32[64,192,64]{1,2,0:T(8,128)}, f32[64,192,64]{1,2,0:T(8,128)}, u32[]{:S(2)}, u32[]{:S(2)}) collective-permute-start(f32[64,192,64]{1,2,0:T(8,128)} %copy.42), channel_id=1, source_target_pairs={{0,1},{1,2},{2,3},{4,5},{5,6},{6,7},{8,9},{9,10},{10,11},{12,13},{... | collective-permute-start | bytes 9437192 | tf_op jit(solution)/shard_map/ppermute | solution.py:17
  55.7 0.0 copy-start.6
  55.7 0.0 copy-start.4
  55.7 0.0 copy-start.5
  55.7 6.3 %copy.43 = f32[64,192,64]{1,2,0:T(8,128)} copy(f32[64,192,64]{2,1,0:T(8,128)} %get-tuple-element.88) | data formatting | bytes 6291456 | tf_op jit(solution)/shard_map/slice | solution.py:16
  62.1 2.9 %collective-permute-start.3 = (f32[64,192,64]{1,2,0:T(8,128)}, f32[64,192,64]{1,2,0:T(8,128)}, u32[]{:S(2)}, u32[]{:S(2)}) collective-permute-start(f32[64,192,64]{1,2,0:T(8,128)} %copy.43), channel_id=1, source_target_pairs={{1,0},{2,1},{3,2},{5,4},{6,5},{7,6},{9,8},{10,9},{11,10},{13,12},{... | collective-permute-start | bytes 9437192 | tf_op jit(solution)/shard_map/ppermute | solution.py:18
  65.0 0.0 copy-done.4
  65.1 0.0 copy-done.5
  65.1 82.6 %collective-permute-done.2 = f32[64,192,64]{1,2,0:T(8,128)} collective-permute-done((f32[64,192,64]{1,2,0:T(8,128)}, f32[64,192,64]{1,2,0:T(8,128)}, u32[]{:S(2)}, u32[]{:S(2)}) %collective-permute-start.2) | collective-permute-done | bytes 3145760 | tf_op jit(solution)/shard_map/ppermute | solution.py:17
  147.7 6.1 %copy.44 = f32[64,192,64]{2,1,0:T(8,128)} copy(f32[64,192,64]{1,2,0:T(8,128)} %collective-permute-done.2) | data formatting | bytes 6291456 | tf_op jit(solution)/shard_map/ppermute | solution.py:17
  153.8 3.6 %collective-permute-done.3 = f32[64,192,64]{1,2,0:T(8,128)} collective-permute-done((f32[64,192,64]{1,2,0:T(8,128)}, f32[64,192,64]{1,2,0:T(8,128)}, u32[]{:S(2)}, u32[]{:S(2)}) %collective-permute-start.3) | collective-permute-done | bytes 3145760 | tf_op jit(solution)/shard_map/ppermute | solution.py:18
  157.4 6.1 %copy.45 = f32[64,192,64]{2,1,0:T(8,128)} copy(f32[64,192,64]{1,2,0:T(8,128)} %collective-permute-done.3) | data formatting | bytes 6291456 | tf_op jit(solution)/shard_map/ppermute | solution.py:18
  163.6 0.0 copy-done.1
  163.6 16.6 %fusion.3 = f32[64,64,256]{2,1,0:T(8,128)S(1)} fusion(f32[64,192,64]{2,1,0:T(8,128)} %copy.45, f32[64,64,128]{2,1,0:T(8,128)} %copy-done.3, f32[64,64,128]{2,1,0:T(8,128)S(1)} %copy-done.1, f32[64,64,128]{2,1,0:T(8,128)} %copy-done.2, f32[64,192,64]{2,1,0:T(8,128)} %copy.44, f32[64]{0:T(128)S(1)} %get-tuple-element.111, f32[64]{0:T(128)S(1)} %get-tuple-element.109, ...), kind=kOutput, calls=%fused_computation.8 | convolution fusion | flops 2434007040 | bytes 16778240 | tf_op jit(solution)/shard_map/zyp,zpq->zyq/dot_general | solution.py:108
  180.2 10.7 %fusion.14 = f32[64,64,128]{2,1,0:T(8,128)S(1)} fusion(f32[64,64,256]{2,1,0:T(8,128)S(1)} %fusion.3, f32[64]{0:T(128)S(1)} %get-tuple-element.110, f32[64]{0:T(128)S(1)} %get-tuple-element.108, s32[64]{0:T(128)S(1)} %get-tuple-element.106, s32[128]{0:T(128)S(1)} %iota_add_fusion), kind=kOutput, calls=%fused_computation.21 | convolution fusion | flops 1625292800 | bytes 6292736 | tf_op jit(solution)/shard_map/zyq,zxq->zyx/dot_general | solution.py:115
  190.9 2.6 %exponential_subtract_fusion = (f32[64,64,128]{2,1,0:T(8,128)S(1)}, f32[64,128]{1,0:T(8,128)S(1)}, f32[1,64,64,128]{3,2,1,0:T(8,128)S(1)}, f32[1,64,64,128]{3,2,1,0:T(8,128)S(1)}, f32[1,64,64,128]{3,2,1,0:T(8,128)S(1)}) fusion(f32[64,64,128]{2,1,0:T(8,128)S(1)} %fusion.14, f32[64]{0:T(128)S(1)} %broadcast_multiply_fusion), kind=kLoop, calls=%fused_computation.52 | loop fusion | flops 10477568 | bytes 10518784 | tf_op jit(solution)/shard_map/sub | solution.py:125
  193.5 1.6 negate_exponential_fusion
  195.1 1.3 fusion.20
  196.4 0.7 copy.46
  197.1 8.5 %all-to-all-start = ((f32[1,4,64,128]{3,1,0,2:T(4,128)}), f32[1,4,64,128]{3,1,0,2:T(4,128)S(1)}, u32[]{:S(2)}, u32[]{:S(2)}) async-start(f32[1,4,64,128]{3,1,0,2:T(4,128)} %copy.46), calls=%async_computation | async-start | bytes 262144 | tf_op jit(solution)/shard_map/all_to_all | solution.py:129
  205.6 9.4 %all-to-all-done = f32[1,4,64,128]{3,1,0,2:T(4,128)S(1)} async-done(((f32[1,4,64,128]{3,1,0,2:T(4,128)}), f32[1,4,64,128]{3,1,0,2:T(4,128)S(1)}, u32[]{:S(2)}, u32[]{:S(2)}) %all-to-all-start) | async-done | bytes 131104 | tf_op jit(solution)/shard_map/all_to_all | solution.py:129
  215.0 0.6 while.14
  215.6 0.6 maximum_bitcast_fusion.1
  (59 shorter events, 0.5 us)
Async XLA Ops:
  8.5 29.1 %copy-start = (f32[64,64,128]{2,1,0:T(8,128)}, f32[64,64,128]{2,1,0:T(8,128)S(1)}, u32[]{:S(2)}) copy-start(f32[64,64,128]{2,1,0:T(8,128)S(1)} %fusion.35) | copy-start | bytes 6291460
  8.5 27.4 %collective-permute-start = (f32[64,64,128]{2,1,0:T(8,128)S(1)}, f32[64,64,128]{2,1,0:T(8,128)S(1)}, u32[]{:S(2)}, u32[]{:S(2)}) collective-permute-start(f32[64,64,128]{2,1,0:T(8,128)S(1)} %fusion.35), channel_id=1, source_target_pairs={{0,4},{4,8},{8,12},{12,16},{16,20},{20,24},{24,28},{1,5},{5,9},{9,... | collective-permute-start | bytes 6291464 | tf_op jit(solution)/shard_map/ppermute | solution.py:17
  10.4 27.2 %collective-permute-start.1 = (f32[64,64,128]{2,1,0:T(8,128)S(1)}, f32[64,64,128]{2,1,0:T(8,128)S(1)}, u32[]{:S(2)}, u32[]{:S(2)}) collective-permute-start(f32[64,64,128]{2,1,0:T(8,128)S(1)} %fusion.35), channel_id=1, source_target_pairs={{4,0},{8,4},{12,8},{16,12},{20,16},{24,20},{28,24},{5,1},{9,5},{13... | collective-permute-start | bytes 6291464 | tf_op jit(solution)/shard_map/ppermute | solution.py:18
  35.8 1.8 copy-start.2
  37.6 1.3 copy-start.3
  52.6 95.1 %collective-permute-start.2 = (f32[64,192,64]{1,2,0:T(8,128)}, f32[64,192,64]{1,2,0:T(8,128)}, u32[]{:S(2)}, u32[]{:S(2)}) collective-permute-start(f32[64,192,64]{1,2,0:T(8,128)} %copy.42), channel_id=1, source_target_pairs={{0,1},{1,2},{2,3},{4,5},{5,6},{6,7},{8,9},{9,10},{10,11},{12,13},{... | collective-permute-start | bytes 9437192 | tf_op jit(solution)/shard_map/ppermute | solution.py:17
  55.7 9.3 %copy-start.6 = (f32[64]{0:T(128)S(1)}, f32[64]{0:T(128)}, u32[]{:S(2)}) copy-start(f32[64]{0:T(128)} %param.17) | copy-start | bytes 772
  55.7 9.3 %copy-start.4 = (f32[2,64]{1,0:T(2,128)S(1)}, f32[2,64]{1,0:T(2,128)}, u32[]{:S(2)}) copy-start(f32[2,64]{1,0:T(2,128)} %param.16) | copy-start | bytes 1540
  55.7 9.4 %copy-start.5 = (s32[2,64]{1,0:T(2,128)S(1)}, s32[2,64]{1,0:T(2,128)}, u32[]{:S(2)}) copy-start(s32[2,64]{1,0:T(2,128)} %param.15) | copy-start | bytes 1540
  62.1 95.3 %collective-permute-start.3 = (f32[64,192,64]{1,2,0:T(8,128)}, f32[64,192,64]{1,2,0:T(8,128)}, u32[]{:S(2)}, u32[]{:S(2)}) collective-permute-start(f32[64,192,64]{1,2,0:T(8,128)} %copy.43), channel_id=1, source_target_pairs={{1,0},{2,1},{3,2},{5,4},{6,5},{7,6},{9,8},{10,9},{11,10},{13,12},{... | collective-permute-start | bytes 9437192 | tf_op jit(solution)/shard_map/ppermute | solution.py:18
  153.8 9.8 %copy-start.1 = (f32[64,64,128]{2,1,0:T(8,128)S(1)}, f32[64,64,128]{2,1,0:T(8,128)}, u32[]{:S(2)}) copy-start(f32[64,64,128]{2,1,0:T(8,128)} %copy-done) | copy-start | bytes 6291460
  197.1 17.8 %all-to-all-start = ((f32[1,4,64,128]{3,1,0,2:T(4,128)}), f32[1,4,64,128]{3,1,0,2:T(4,128)S(1)}, u32[]{:S(2)}, u32[]{:S(2)}) async-start(f32[1,4,64,128]{3,1,0,2:T(4,128)} %copy.46), calls=%async_computation | async-start | bytes 262144 | tf_op jit(solution)/shard_map/all_to_all | solution.py:129
where the time goes:
time: 219 us; the launch traced here: 216 us
  waiting for transfers between devices  119 us (54%)
  local copies, waits for them, and re-layouts  38.3 us (17%)
  matrix products  30.1 us (14%)
  starting transfers between devices  20 us (9%)
  other arithmetic  7.95 us (4%)
    ppermute x2, waiting for transfers between devices, with_halo(): before = lax.ppermute(last, axis, up)  104 us
    dot_general x1, matrix products, body(): jnp.einsum('zyp,zpq->zyq', row_table, padded, precision=lax.Precision.HIG...  16.6 us
    slice x2, local copies, waits for them, and re-layouts, with_halo(): last = lax.slice_in_dim(shard, length - width, length, axis=dim)  13.2 us
    dot_general x1, matrix products, body(): jnp.einsum('zyq,zxq->zyx', row_moved, col_table, precision=lax.Precision....  10.7 us
    all_to_all x1, waiting for transfers between devices, body(): lax.all_to_all(pieces, 'depth', split_axis=2, concat_axis=0, tiled=True)  9.37 us
    all_to_all x1, starting transfers between devices, body(): lax.all_to_all(pieces, 'depth', split_axis=2, concat_axis=0, tiled=True)  8.47 us
    ppermute x2, starting transfers between devices, with_halo(): after = lax.ppermute(leading, axis, down)  6.55 us
    slice x1, local copies, waits for them, and re-layouts, with_halo(): leading = lax.slice_in_dim(shard, 0, width, axis=dim)  6.34 us
  transfers between devices with their start and end apart: 5, of which 5 were waited for; matrix products, arithmetic and copies ran while one was open for 6% of the time, Pallas kernels for 0%

commit v1 on v0

v1 whole, which is shorter than its diff:
```python
import functools
import math

import jax
import jax.numpy as jnp
from jax import lax
from jax.experimental import pallas as pl
from jax.experimental.pallas import tpu as pltpu
from jax.sharding import PartitionSpec as P

BRICK = 64
SLAB = 64
ROWS = 64
COLS = 128
STRIDE = 80
HEAD = 8
BLOCKS = 24
LN2 = math.log(2.0)
TINT0 = (0.5, 1.0, 1.0 / (1.0 + math.exp(-0.8)))
VMEM_SPEC = pl.BlockSpec(memory_space=pltpu.VMEM)
SMEM_SPEC = pl.BlockSpec(memory_space=pltpu.SMEM)
INTERPRET = False


def call(kernel, out_shape, in_specs, scratch=(), flops=1000, bytes_moved=1000):
    specs = jax.tree.map(lambda _: VMEM_SPEC, out_shape)
    return pl.pallas_call(
        kernel,
        out_shape=out_shape,
        in_specs=in_specs,
        out_specs=specs,
        scratch_shapes=list(scratch),
        interpret=INTERPRET,
        cost_estimate=pl.CostEstimate(flops=flops, bytes_accessed=bytes_moved, transcendentals=0),
    )


def f32(*shape):
    return jax.ShapeDtypeStruct(shape, jnp.float32)


def lane_table(half):
    source = lax.broadcasted_iota(jnp.int32, (2 * COLS, COLS), 0) % COLS
    target = lax.broadcasted_iota(jnp.int32, (2 * COLS, COLS), 1)
    local = target % BRICK
    start = target - local
    pair = local // 2
    weight = jnp.where(local % 2 == 1, 0.5, -0.5)
    inside = local < 2 * half
    low = jnp.where(inside & (source == start + pair), 1.0, 0.0)
    high = jnp.where(inside & (source == start + half + pair), weight, 0.0)
    return (low + high).astype(jnp.bfloat16)


def lane_lift(block, table):
    coarse = block.astype(jnp.bfloat16)
    rest = (block - coarse.astype(jnp.float32)).astype(jnp.bfloat16)
    both = jnp.concatenate([coarse, rest], axis=1)
    return jnp.dot(both, table, preferred_element_type=jnp.float32)


def lift_kernel(c_ref, d_ref, row_ref, col_ref, s2_ref, s1_ref, plane_ref):
    lane = lax.broadcasted_iota(jnp.int32, (1, COLS), 1)

    def level(half, below, out_ref, on_result, init, unroll):
        table = lane_table(half)

        def step(i, carry):
            if below is None:
                low = c_ref[i, : 2 * half, :]
            else:
                corner = jnp.where(lane % BRICK < half, below[i], c_ref[i, :half, :])
                low = jnp.concatenate([corner, c_ref[i, half : 2 * half, :]], axis=0)
            high = c_ref[i + half, : 2 * half, :]
            planes = []
            even = low - 0.5 * high
            for part in (even, even + high):
                row_even = part[:half] - 0.5 * part[half:]
                planes += [row_even, row_even + part[half:]]
            result = lane_lift(jnp.concatenate(planes, axis=0), table)
            for odd in range(2):
                for row_odd in range(2):
                    start = (2 * odd + row_odd) * half
                    out_ref[2 * i + odd, pl.ds(row_odd, half, stride=2), :] = result[start : start + half]
            return on_result(i, result, carry)

        return lax.fori_loop(0, half, step, init, unroll=unroll)

    def ignore(i, result, carry):
        return carry

    def boundary(i, result, plane):
        for odd in range(2):
            z = 2 * i + odd
            piece = result[64 * odd : 64 * odd + 64]
            row_ref[pl.ds(z, 1), :] = piece[63:64]
            plane = jnp.where(lane == z, pltpu.roll(piece, z + 1, 1), plane)
        return plane

    level(8, None, s2_ref, ignore, 0, 2)
    level(16, s2_ref, s1_ref, ignore, 0, 2)
    plane = level(32, s1_ref, d_ref, boundary, jnp.zeros((64, COLS), jnp.float32), 2)
    plane_ref[...] = plane
    for row_odd in range(2):
        col_ref[pl.ds(row_odd, 32, stride=2), :] = plane_ref[pl.ds(32 * row_odd, 32), :]
    row_ref[pl.ds(64, 8), :] = jnp.broadcast_to(plane[63:64], (8, COLS))


def optics(sheared, rate):
    size = jnp.abs(sheared)
    fall = jnp.exp(-size)
    tail = jnp.where(fall < 1e-3, fall * (1.0 - 0.5 * fall), jnp.log(1.0 + fall))
    return (
        rate * (jnp.maximum(sheared, 0.0) + tail),
        0.5 + 0.5 * jnp.tanh(0.75 * sheared),
        jnp.exp(-0.5 * sheared * sheared),
        0.5 + 0.5 * jnp.tanh(0.4 - 0.5 * sheared),
    )


def shade_kernel(
    scale, shift_ref, frac_ref, absorb_ref, span_ref, edge_ref, d_ref, halo_row_ref, halo_col_ref, corner_ref, last_ref,
    fvec_ref, up_ref, own_ref, down_ref, g_ref, v_ref, hu_ref,
):
    lane = lax.broadcasted_iota(jnp.int32, (8, COLS), 1)
    sub = lax.broadcasted_iota(jnp.int32, (8, COLS), 0)
    last_row = edge_ref[0] == 1
    last_col = edge_ref[1] == 1
    zero = jnp.zeros((8, COLS), jnp.float32)
    fy_lanes = fvec_ref[0:1, :]
    fx_lanes = fvec_ref[1:2, :]
    rate_lanes = fvec_ref[2:3, :] * scale

    for part in range(4):
        g_ref[part, pl.ds(0, 8), :] = zero
        v_ref[part, pl.ds(0, 8), :] = zero
        v_ref[part, pl.ds(80, 8), :] = zero

    for t in range(9):
        for which, plane, above in ((0, halo_col_ref, corner_ref[7:8, :]), (1, last_ref, halo_row_ref[64:65, :])):
            here = plane[8 * t : 8 * t + 8, :] if t < 8 else zero
            before = above if t == 0 else plane[8 * t - 1 : 8 * t, :]
            behind = jnp.where(sub == 0, before, pltpu.roll(here, 1, 0))
            mixed = here + fy_lanes * (behind - here)
            if which == 0:
                hu_ref[pl.ds(8 * t, 8), :] = mixed
            else:
                values = optics(fx_lanes * mixed, rate_lanes)
                for part in range(4):
                    value = values[part]
                    if t == 8:
                        value = jnp.where((sub == 0) & last_row, value, 0.0)
                    v_ref[part, pl.ds(8 + 8 * t, 8), :] = value

    def slice_step(z, carry):
        fy, fx, rate = frac_ref[0, z], frac_ref[1, z], absorb_ref[z] * scale
        k = shift_ref[1, z] + 64
        base = HEAD + STRIDE * z
        for t in range(9):
            if t == 0:
                here = d_ref[z, 0:8, :]
                behind = jnp.where(sub == 0, halo_row_ref[pl.ds(z, 1), :], pltpu.roll(here, 1, 0))
            elif t == 8:
                here = zero
                behind = jnp.where(sub == 0, d_ref[z, 63:64, :], 0.0)
            else:
                here = d_ref[z, 8 * t : 8 * t + 8, :]
                behind = d_ref[z, 8 * t - 1 : 8 * t + 7, :]
            mixed = here + fy * (behind - here)
            left = jnp.where(lane == 0, pltpu.roll(hu_ref[pl.ds(8 * t, 8), :], COLS - z, 1), pltpu.roll(mixed, 1, 1))
            sheared = pltpu.roll(mixed + fx * (left - mixed), k, 1)
            values = optics(sheared, rate)
            for part in range(4):
                value = values[part]
                if t == 8:
                    value = jnp.where((sub == 0) & last_row, value, 0.0)
                g_ref[part, pl.ds(pl.multiple_of(base + 8 * t, 8), 8), :] = value
        for part in range(4):
            g_ref[part, pl.ds(pl.multiple_of(base + 72, 8), 8), :] = zero
        return carry

    lax.fori_loop(0, SLAB, slice_step, 0, unroll=2)

    def composite(edge):
        for out, out_ref in enumerate((up_ref, own_ref, down_ref)):

            def block_step(block, carry):
                index = 8 * out + block

                def ray_step(group, state):
                    for offset in range(4):
                        z = 4 * group + offset
                        low = 8 * index - 64 - shift_ref[0, z]
                        valid = (low >= -7) & (low <= 64)
                        low = jnp.where(valid, low, 72)
                        k = shift_ref[1, z] + 64
                        row = HEAD + STRIDE * z + low
                        values = [g_ref[part, pl.ds(row, 8), :] for part in range(4)]
                        right = lane < k
                        left_values = [jnp.where(right, 0.0, values[0])] + values[1:]
                        right_values = [jnp.where(right, values[0], 0.0)] + values[1:]
                        if edge:
                            for part in range(4):
                                extra = v_ref[part, pl.ds(8 + low, 8), :]
                                extra = pltpu.roll(extra, (k - z + COLS) % COLS, 1)
                                right_values[part] = jnp.where(lane == k, extra, right_values[part])
                        new_state = []
                        for half, (optical, *tints) in enumerate((left_values, right_values)):
                            depth, through, *sums = state[half]
                            depth = depth + optical
                            after = jnp.exp(-depth)
                            weight = through - after
                            sums = [total + weight * tint for total, tint in zip(sums, tints)]
                            new_state.append((depth, after, *sums))
                        state = tuple(new_state)
                    return state

                start = (zero, zero + 1.0, zero, zero, zero)
                state = lax.fori_loop(span_ref[0, index], span_ref[1, index], ray_step, (start, start))
                rows = pl.ds(pl.multiple_of(8 * block, 8), 8)
                for half in range(2):
                    depth, _, *sums = state[half]
                    for channel in range(3):
                        out_ref[half, channel, rows, :] = sums[channel]
                    out_ref[half, 3, rows, :] = depth
                return carry

            lax.fori_loop(0, 8, block_step, 0)

    pl.when(last_col)(lambda: composite(True))
    pl.when(jnp.logical_not(last_col))(lambda: composite(False))


def over(front, behind):
    through = jnp.exp(-front[3])
    return [front[c] + through * behind[c] for c in range(3)] + [front[3] + behind[3]]


def channels(ref, *index):
    return [ref[(*index, c)] for c in range(4)]


def rows_kernel(own_ref, below_ref, above_ref, mine_ref, left_ref, right_ref):
    lane = lax.broadcasted_iota(jnp.int32, (1, COLS), 1)
    halves = []
    for half in range(2):
        merged = over(channels(own_ref, half), channels(above_ref, half))
        halves.append(over(channels(below_ref, half), merged))
    for c in range(4):
        low, high = halves[0][c], halves[1][c]
        low_turned, high_turned = pltpu.roll(low, 64, 1), pltpu.roll(high, 64, 1)
        mine_ref[c] = jnp.where(lane < 64, low_turned, high_turned)
        left_ref[c] = jnp.where(lane < 64, low[:32], low_turned[32:])
        right_ref[c] = jnp.where(lane < 64, high_turned[:32], high[32:])


def columns_kernel(scale, edge_ref, mine_ref, own_right_ref, from_right_ref, from_left_ref, zrow_ref, zcol_ref, out_ref):
    lane = lax.broadcasted_iota(jnp.int32, (1, COLS), 1)
    last_col = edge_ref[1] == 1

    def unpack(packed):
        turned = pltpu.roll(packed, 64, 1)
        return turned, packed

    front, behind, mine = [], [], []
    for c in range(4):
        piece = from_right_ref[c]
        turned = pltpu.roll(piece, 64, 1)
        upper = jnp.concatenate([turned, piece], axis=0)
        piece = from_left_ref[c]
        turned = pltpu.roll(piece, 64, 1)
        lower = jnp.concatenate([piece, turned], axis=0)
        own = mine_ref[c]
        front.append(jnp.where(lane < 64, own, upper))
        behind.append(jnp.where(lane < 64, lower, own))
    inner = over(front, behind)
    pre = jnp.maximum(zrow_ref[:, 0:1], zcol_ref[0:1, :])
    post = jnp.minimum(jnp.maximum(zrow_ref[:, 1:2], zcol_ref[1:2, :]), zcol_ref[2:3, :] - pre)
    post = jnp.maximum(post, 0.0)
    flat = []
    for amount in (pre, post):
        depth = (scale * LN2) * amount
        fade = 1.0 - jnp.exp(-depth)
        flat.append([TINT0[c] * fade for c in range(3)] + [depth])
    whole = over(flat[0], over(inner, flat[1]))
    pieces = out_ref.shape[0]
    height = ROWS // pieces
    for p in range(pieces):
        for c in range(4):
            out_ref[p, c] = whole[c][p * height : (p + 1) * height]


def fold_kernel(in_ref, out_ref):
    merged = channels(in_ref, 0)
    for slab in range(1, in_ref.shape[0]):
        merged = over(merged, channels(in_ref, slab))
    for c in range(3):
        out_ref[c] = merged[c]
    out_ref[3] = 1.0 - jnp.exp(-merged[3])


def body(coefficients, shifts, fraction, absorb):
    depth_count = lax.axis_size("depth")
    row_count = lax.axis_size("imgy")
    col_count = lax.axis_size("imgx")
    scale = 2.0 / (SLAB * depth_count)
    iy, ix = lax.axis_index("imgy"), lax.axis_index("imgx")

    volume, row_plane, col_plane = call(
        lift_kernel,
        (f32(SLAB, ROWS, COLS), f32(72, COLS), f32(ROWS, COLS)),
        [VMEM_SPEC],
        [
            pltpu.VMEM((16, 16, COLS), jnp.float32),
            pltpu.VMEM((32, 32, COLS), jnp.float32),
            pltpu.VMEM((64, COLS), jnp.float32),
        ],
        flops=300_000_000,
        bytes_moved=4 << 20,
    )(coefficients)

    row_up = [(i, i + 1) for i in range(row_count - 1)]
    row_down = [(i + 1, i) for i in range(row_count - 1)]
    col_up = [(i, i + 1) for i in range(col_count - 1)]
    col_down = [(i + 1, i) for i in range(col_count - 1)]
    both_up = [
        (y * col_count + x, (y + 1) * col_count + x + 1) for y in range(row_count - 1) for x in range(col_count - 1)
    ]
    halo_row = lax.ppermute(row_plane, "imgy", row_up)
    halo_col = lax.ppermute(col_plane, "imgx", col_up)
    corner = lax.ppermute(col_plane[56:64], ("imgy", "imgx"), both_up)

    shift_rows, shift_cols = shifts[0], shifts[1]
    starts = 8 * jnp.arange(BLOCKS, dtype=jnp.int32)
    first = jnp.sum(shift_rows[None, :] < starts[:, None] - 128, axis=1, dtype=jnp.int32)
    end = jnp.sum(shift_rows[None, :] <= starts[:, None] - 57, axis=1, dtype=jnp.int32)
    span = jnp.stack([first // 4, (end + 3) // 4])
    edge = jnp.stack([iy == row_count - 1, ix == col_count - 1]).astype(jnp.int32)
    vectors = jnp.pad(jnp.concatenate([fraction, absorb[None]], axis=0), ((0, 5), (0, COLS - SLAB)))

    sent = f32(2, 4, ROWS, COLS)
    up, own, down = call(
        functools.partial(shade_kernel, scale),
        (sent, sent, sent),
        [SMEM_SPEC] * 5 + [VMEM_SPEC] * 6,
        [
            pltpu.VMEM((4, HEAD + SLAB * STRIDE, COLS), jnp.float32),
            pltpu.VMEM((4, 88, COLS), jnp.float32),
            pltpu.VMEM((72, COLS), jnp.float32),
        ],
        flops=300_000_000,
        bytes_moved=4 << 20,
    )(shifts, fraction, absorb, span, edge, volume, halo_row, halo_col, corner, col_plane, vectors)

    below = lax.ppermute(up, "imgy", row_down)
    above = lax.ppermute(down, "imgy", row_up)
    packed = f32(4, ROWS // 2, COLS)
    mine, left, right = call(rows_kernel, (f32(4, ROWS, COLS), packed, packed), [VMEM_SPEC] * 3)(own, below, above)
    from_right = lax.ppermute(left, "imgx", col_down)
    from_left = lax.ppermute(right, "imgx", col_up)

    image_rows = iy * ROWS + jnp.arange(ROWS, dtype=jnp.int32)
    image_cols = ix * COLS + jnp.arange(COLS, dtype=jnp.int32)

    def outside(pixels, offsets, limit):
        position = pixels[:, None] - offsets[None, :]
        pre = jnp.sum(jnp.where(position > limit, absorb[None, :], 0.0), axis=1)
        post = jnp.sum(jnp.where(position < 0, absorb[None, :], 0.0), axis=1)
        return pre, post

    zrow = jnp.stack(outside(image_rows, shift_rows, ROWS * row_count), axis=1)
    zcol = jnp.stack(
        [*outside(image_cols, shift_cols, COLS * col_count), jnp.broadcast_to(jnp.sum(absorb), (COLS,))], axis=0
    )
    pieces = call(
        functools.partial(columns_kernel, scale),
        f32(depth_count, 4, ROWS // depth_count, COLS),
        [SMEM_SPEC] + [VMEM_SPEC] * 6,
    )(edge, mine, right, from_right, from_left, zrow, zcol)
    incoming = lax.all_to_all(pieces, "depth", split_axis=0, concat_axis=0, tiled=True)
    image = call(fold_kernel, f32(4, ROWS // depth_count, COLS), [VMEM_SPEC])(incoming)
    return image[:, None]


def solution(mesh):
    in_specs = (P("depth", "imgy", "imgx"), P(None, "depth"), P(None, "depth"), P("depth"))
    out_specs = P(None, "imgy", "depth", "imgx")
    return jax.shard_map(body, mesh=mesh, in_specs=in_specs, out_specs=out_specs, check_vma=False)
```

time: 219 us -> 86.6 us (0.40)
  waiting for transfers between devices: 119 us -> 6.35 us
  local copies, waits for them, and re-layouts: 38.3 us -> 4.06 us
  matrix products: 30.1 us -> 0 us
  Pallas kernels: 0 us -> 28.9 us
  blocking collectives: 0 us -> 17.8 us
  other arithmetic: 7.95 us -> 3.61 us
  starting transfers between devices: 20 us -> 24.2 us
    ppermute x4 -> x7, waiting for transfers between devices: 110 us -> 6.35 us  [the longest x1 3.71 us: body(): above = lax.ppermute(down, 'imgy', row_up)]
    dot_general x5 -> x0, matrix products: 30.1 us -> none  [the longest x1 16.6 us: body(): jnp.einsum('zyp,zpq->zyq', row_table, padded, precision=lax.Precision.HIG...]
    pallas_call x0 -> x5, Pallas kernels: none -> 28.9 us  [the longest x1 14.9 us: body(): call(functools.partial(shade_kernel, scale), (sent, sent, sent), [SMEM_SP...]
    slice x4 -> x1, local copies, waits for them, and re-layouts: 19.6 us -> 0.69 us  [body(): corner = lax.ppermute(col_plane[56:64], ('imgy', 'imgx'), both_up)]
    all_to_all x0 -> x1, blocking collectives: none -> 17.8 us  [body(): lax.all_to_all(pieces, 'depth', split_axis=0, concat_axis=0, tiled=True)]
    ppermute x4 -> x7, starting transfers between devices: 11.6 us -> 24.2 us  [the longest x1 9.42 us: body(): from_left = lax.ppermute(right, 'imgx', col_up)]
    ppermute x2 -> x0, local copies, waits for them, and re-layouts: 12.3 us -> none  [the longest x1 6.14 us: with_halo(): before = lax.ppermute(last, axis, up)]
    all_to_all x1 -> x0, waiting for transfers between devices: 9.37 us -> none  [body(): lax.all_to_all(pieces, 'depth', split_axis=2, concat_axis=0, tiled=True)]
  transfers between devices with their start and end apart: 5 -> 7, of which waited for: 5 -> 3; matrix products, arithmetic and copies ran while one was open for 6% -> 7% of each run, Pallas kernels for 0% -> 0%
where the time goes in v1:
time: 86.6 us; the launch traced here: 85.1 us
  Pallas kernels  28.9 us (33%)
  starting transfers between devices  24.2 us (28%)
  blocking collectives  17.8 us (21%)
  waiting for transfers between devices  6.35 us (7%)
  local copies, waits for them, and re-layouts  4.06 us (5%)
  other arithmetic  3.61 us (4%)
    all_to_all x1, blocking collectives, body(): lax.all_to_all(pieces, 'depth', split_axis=0, concat_axis=0, tiled=True)  17.8 us
    pallas_call x1, Pallas kernels, body(): call(functools.partial(shade_kernel, scale), (sent, sent, sent), [SMEM_SP...  14.9 us
    ppermute x1, starting transfers between devices, body(): from_left = lax.ppermute(right, 'imgx', col_up)  9.42 us
    pallas_call x1, Pallas kernels, body(): call(lift_kernel, (f32(SLAB, ROWS, COLS), f32(72, COLS), f32(ROWS, COLS))...  8.69 us
    ppermute x1, waiting for transfers between devices, body(): above = lax.ppermute(down, 'imgy', row_up)  3.71 us
    ppermute x1, starting transfers between devices, body(): from_right = lax.ppermute(left, 'imgx', col_down)  3.36 us
    ppermute x1, starting transfers between devices, body(): halo_col = lax.ppermute(col_plane, 'imgx', col_up)  3.09 us
    ppermute x1, starting transfers between devices, body(): below = lax.ppermute(up, 'imgy', row_down)  2.35 us
  transfers between devices with their start and end apart: 7, of which 3 were waited for; matrix products, arithmetic and copies ran while one was open for 7% of the time, Pallas kernels for 0%

profile of v1, /device:TPU:20, one launch (start us, length us, event | category | flops | bytes accessed | tf_op | source)
XLA Modules:
  0.0 85.1 jit_solution(13433902953227060978)
XLA Ops:
  0.0 0.0 copy-start.9
  0.0 0.0 copy-start.6
  0.0 0.0 copy-start.7
  0.0 0.0 copy-start.10
  0.0 8.7 %shard_map.46 = (f32[64,64,128]{2,1,0:T(8,128)}, f32[72,128]{1,0:T(8,128)}, f32[64,128]{1,0:T(8,128)}) custom-call(f32[64,64,128]{2,1,0:T(8,128)} %c_ref.1), custom_call_target="tpu_custom_call" | custom-call | flops 300000000 | bytes 4194304 | tf_op jit(solution)/shard_map/pallas_call | solution.py:309
  8.7 3.1 %collective-permute-start.1 = (f32[64,128]{1,0:T(8,128)}, f32[64,128]{1,0:T(8,128)S(1)}, u32[]{:S(2)}, u32[]{:S(2)}) collective-permute-start(f32[64,128]{1,0:T(8,128)} %get-tuple-element.16.last_ref), channel_id=1, source_target_pairs={{0,1},{1,2},{2,3},{4,5},{5,6},{6,7},{8,9},{9,10},{10,11},{12,13},{... | collective-permute-start | bytes 98312 | tf_op jit(solution)/shard_map/ppermute | solution.py:330
  11.8 0.7 slice.10
  12.5 1.9 %collective-permute-start.2 = (f32[8,128]{1,0:T(8,128)S(1)}, f32[8,128]{1,0:T(8,128)S(1)}, u32[]{:S(2)}, u32[]{:S(2)}) collective-permute-start(f32[8,128]{1,0:T(8,128)S(1)} %slice.10), channel_id=1, source_target_pairs={{0,5},{1,6},{2,7},{4,9},{5,10},{6,11},{8,13},{9,14},{10,15},{12,17... | collective-permute-start | bytes 12296 | tf_op jit(solution)/shard_map/ppermute | solution.py:331
  14.4 2.1 %collective-permute-start = (f32[72,128]{1,0:T(8,128)}, f32[72,128]{1,0:T(8,128)S(1)}, u32[]{:S(2)}, u32[]{:S(2)}) collective-permute-start(f32[72,128]{1,0:T(8,128)} %get-tuple-element.15), channel_id=1, source_target_pairs={{0,4},{4,8},{8,12},{12,16},{16,20},{20,24},{24,28},{1,5},{5,9},{9,... | collective-permute-start | bytes 110600 | tf_op jit(solution)/shard_map/ppermute | solution.py:329
  16.6 0.0 copy-done.9
  16.6 0.2 convert_reduce_fusion.1
  16.8 0.6 pad_add_fusion.span_ref
  17.4 0.0 copy-done.6
  17.4 0.0 copy-done.10
  17.4 0.6 select_maximum_fusion.fvec_ref
  18.0 0.1 select_reduce_fusion.1
  18.1 0.7 add_convert_fusion.edge_ref
  18.8 0.0 collective-permute-done.2.corner_ref
  18.8 0.0 copy-start.8
  18.8 0.0 collective-permute-done.1.halo_col_ref
  18.8 0.0 copy-start.5
  18.8 1.1 %collective-permute-done.halo_row_ref = f32[72,128]{1,0:T(8,128)S(1)} collective-permute-done((f32[72,128]{1,0:T(8,128)}, f32[72,128]{1,0:T(8,128)S(1)}, u32[]{:S(2)}, u32[]{:S(2)}) %collective-permute-start) | collective-permute-done | bytes 36896 | tf_op jit(solution)/shard_map/ppermute | solution.py:329
  19.9 0.0 copy-done.8
  19.9 0.0 copy-done.5
  19.9 0.6 copy-done.4
  20.5 14.9 %shard_map.47 = (f32[2,4,64,128]{3,2,1,0:T(8,128)}, f32[2,4,64,128]{3,2,1,0:T(8,128)}, f32[2,4,64,128]{3,2,1,0:T(8,128)}) custom-call(s32[2,64]{1,0:T(2,128)} %shift_ref.1, f32[2,64]{1,0:T(2,128)} %frac_ref.1, f32[64]{0:T(128)} %absorb_ref.1, s32[2,24]{1,0:T(2,128)} %pad_add_fusion.span_ref, s32[2]{0:T(128)} %add_convert_fusion.edge_ref, ...), custom_call_target="tpu_custom_call" | custom-call | flops 300000000 | bytes 4194304 | tf_op jit(solution)/shard_map/pallas_call | solution.py:342
  35.5 2.4 %collective-permute-start.3 = (f32[2,4,64,128]{3,2,1,0:T(8,128)}, f32[2,4,64,128]{3,2,1,0:T(8,128)S(1)}, u32[]{:S(2)}, u32[]{:S(2)}) collective-permute-start(f32[2,4,64,128]{3,2,1,0:T(8,128)} %get-tuple-element.18), channel_id=1, source_target_pairs={{4,0},{8,4},{12,8},{16,12},{20,16},{24,20},{28,24},{5,1},{9,5},{13... | collective-permute-start | bytes 786440 | tf_op jit(solution)/shard_map/ppermute | solution.py:355
  37.8 2.0 %collective-permute-start.4 = (f32[2,4,64,128]{3,2,1,0:T(8,128)}, f32[2,4,64,128]{3,2,1,0:T(8,128)S(1)}, u32[]{:S(2)}, u32[]{:S(2)}) collective-permute-start(f32[2,4,64,128]{3,2,1,0:T(8,128)} %get-tuple-element.19), channel_id=1, source_target_pairs={{0,4},{4,8},{8,12},{12,16},{16,20},{20,24},{24,28},{1,5},{5,9},{9,... | collective-permute-start | bytes 786440 | tf_op jit(solution)/shard_map/ppermute | solution.py:356
  39.8 0.0 copy-done.7
  39.8 0.2 select_reduce_fusion.3
  40.0 0.6 reduce_sum.72
  40.6 0.7 pad.7.clone
  41.3 0.7 maximum_maximum_fusion.zcol_ref
  41.9 0.0 collective-permute-done.3.below_ref
  42.0 3.7 %collective-permute-done.4.above_ref = f32[2,4,64,128]{3,2,1,0:T(8,128)S(1)} collective-permute-done((f32[2,4,64,128]{3,2,1,0:T(8,128)}, f32[2,4,64,128]{3,2,1,0:T(8,128)S(1)}, u32[]{:S(2)}, u32[]{:S(2)}) %collective-permute-start.4) | collective-permute-done | bytes 262176 | tf_op jit(solution)/shard_map/ppermute | solution.py:356
  45.7 0.0 copy-done
  45.7 0.7 copy-done.1
  46.4 1.9 %shard_map.48 = (f32[4,64,128]{2,1,0:T(8,128)}, f32[4,32,128]{2,1,0:T(8,128)}, f32[4,32,128]{2,1,0:T(8,128)}) custom-call(f32[2,4,64,128]{3,2,1,0:T(8,128)} %get-tuple-element.17.own_ref, f32[2,4,64,128]{3,2,1,0:T(8,128)} %copy-done, f32[2,4,64,128]{3,2,1,0:T(8,128)} %copy-done.1), custom_call_target="tpu_custom_call" | custom-call | flops 1000 | bytes 1000 | tf_op jit(solution)/shard_map/pallas_call | solution.py:358
  48.3 3.4 %collective-permute-start.5 = (f32[4,32,128]{2,1,0:T(8,128)}, f32[4,32,128]{2,1,0:T(8,128)S(1)}, u32[]{:S(2)}, u32[]{:S(2)}) collective-permute-start(f32[4,32,128]{2,1,0:T(8,128)} %get-tuple-element.22), channel_id=1, source_target_pairs={{1,0},{2,1},{3,2},{5,4},{6,5},{7,6},{9,8},{10,9},{11,10},{13,12},{... | collective-permute-start | bytes 196616 | tf_op jit(solution)/shard_map/ppermute | solution.py:359
  51.7 9.4 %collective-permute-start.6 = (f32[4,32,128]{2,1,0:T(8,128)}, f32[4,32,128]{2,1,0:T(8,128)S(1)}, u32[]{:S(2)}, u32[]{:S(2)}) collective-permute-start(f32[4,32,128]{2,1,0:T(8,128)} %get-tuple-element.21.own_right_ref), channel_id=1, source_target_pairs={{0,1},{1,2},{2,3},{4,5},{5,6},{6,7},{8,9},{9,10},{10,11},{12,13},{... | collective-permute-start | bytes 196616 | tf_op jit(solution)/shard_map/ppermute | solution.py:360
  61.1 0.7 copy.10.zrow_ref
  61.8 0.0 collective-permute-done.5.from_right_ref
  61.8 1.5 %collective-permute-done.6.from_left_ref = f32[4,32,128]{2,1,0:T(8,128)S(1)} collective-permute-done((f32[4,32,128]{2,1,0:T(8,128)}, f32[4,32,128]{2,1,0:T(8,128)S(1)}, u32[]{:S(2)}, u32[]{:S(2)}) %collective-permute-start.6) | collective-permute-done | bytes 65568 | tf_op jit(solution)/shard_map/ppermute | solution.py:360
  63.3 0.0 copy-done.2
  63.3 0.6 copy-done.3
  64.0 1.8 %shard_map.49 = f32[8,4,8,128]{3,2,1,0:T(8,128)} custom-call(s32[2]{0:T(128)} %add_convert_fusion.edge_ref, f32[4,64,128]{2,1,0:T(8,128)} %get-tuple-element.20.mine_ref, f32[4,32,128]{2,1,0:T(8,128)} %get-tuple-element.21.own_right_ref, f32[4,32,128]{2,1,0:T(8,128)} %copy-done.2, f32[4,32,128]{2,1,0:T(8,128)} %copy-done.3, f32[64,2]{1,0:T(8,128)} %copy.10.zrow_ref, ...), custom_call_target="tpu_custom_call" | custom-call | flops 1000 | bytes 1000 | tf_op jit(solution)/shard_map/pallas_call | solution.py:375
  65.7 17.8 %all_to_all.5.in_ref = f32[8,4,8,128]{3,2,1,0:T(8,128)} all-to-all(f32[8,4,8,128]{3,2,1,0:T(8,128)} %shard_map.49), channel_id=1, replica_groups=mesh['depth'=8,'imgy'=8,'imgx'=4] {'depth'}, dimensions={0} | all-to-all | bytes 262144 | tf_op jit(solution)/shard_map/all_to_all | solution.py:380
  83.5 1.5 %shard_map.50 = f32[4,8,128]{2,1,0:T(8,128)} custom-call(f32[8,4,8,128]{3,2,1,0:T(8,128)} %all_to_all.5.in_ref), custom_call_target="tpu_custom_call" | custom-call | flops 1000 | bytes 1000 | tf_op jit(solution)/shard_map/pallas_call | solution.py:381
  (12 shorter events, 0.1 us)
Async XLA Ops:
  0.0 16.6 %copy-start.9 = (s32[2,64]{1,0:T(2,128)S(1)}, s32[2,64]{1,0:T(2,128)}, u32[]{:S(2)}) copy-start(s32[2,64]{1,0:T(2,128)} %shift_ref.1) | copy-start | bytes 1540
  0.0 17.4 %copy-start.6 = (f32[64]{0:T(128)S(1)}, f32[64]{0:T(128)}, u32[]{:S(2)}) copy-start(f32[64]{0:T(128)} %absorb_ref.1) | copy-start | bytes 772
  0.0 39.8 %copy-start.7 = (f32[64]{0:T(128)S(1)}, f32[64]{0:T(128)}, u32[]{:S(2)}) copy-start(f32[64]{0:T(128)} %absorb_ref.1) | copy-start | bytes 772
  0.0 17.4 %copy-start.10 = (f32[2,64]{1,0:T(2,128)S(1)}, f32[2,64]{1,0:T(2,128)}, u32[]{:S(2)}) copy-start(f32[2,64]{1,0:T(2,128)} %frac_ref.1) | copy-start | bytes 1540
  8.7 10.1 %collective-permute-start.1 = (f32[64,128]{1,0:T(8,128)}, f32[64,128]{1,0:T(8,128)S(1)}, u32[]{:S(2)}, u32[]{:S(2)}) collective-permute-start(f32[64,128]{1,0:T(8,128)} %get-tuple-element.16.last_ref), channel_id=1, source_target_pairs={{0,1},{1,2},{2,3},{4,5},{5,6},{6,7},{8,9},{9,10},{10,11},{12,13},{... | collective-permute-start | bytes 98312 | tf_op jit(solution)/shard_map/ppermute | solution.py:330
  12.5 6.3 %collective-permute-start.2 = (f32[8,128]{1,0:T(8,128)S(1)}, f32[8,128]{1,0:T(8,128)S(1)}, u32[]{:S(2)}, u32[]{:S(2)}) collective-permute-start(f32[8,128]{1,0:T(8,128)S(1)} %slice.10), channel_id=1, source_target_pairs={{0,5},{1,6},{2,7},{4,9},{5,10},{6,11},{8,13},{9,14},{10,15},{12,17... | collective-permute-start | bytes 12296 | tf_op jit(solution)/shard_map/ppermute | solution.py:331
  14.4 5.5 %collective-permute-start = (f32[72,128]{1,0:T(8,128)}, f32[72,128]{1,0:T(8,128)S(1)}, u32[]{:S(2)}, u32[]{:S(2)}) collective-permute-start(f32[72,128]{1,0:T(8,128)} %get-tuple-element.15), channel_id=1, source_target_pairs={{0,4},{4,8},{8,12},{12,16},{16,20},{20,24},{24,28},{1,5},{5,9},{9,... | collective-permute-start | bytes 110600 | tf_op jit(solution)/shard_map/ppermute | solution.py:329
  18.8 1.1 %copy-start.8 = (f32[8,128]{1,0:T(8,128)}, f32[8,128]{1,0:T(8,128)S(1)}, u32[]{:S(2)}) copy-start(f32[8,128]{1,0:T(8,128)S(1)} %collective-permute-done.2.corner_ref) | copy-start | bytes 12292
  18.8 1.1 %copy-start.5 = (f32[64,128]{1,0:T(8,128)}, f32[64,128]{1,0:T(8,128)S(1)}, u32[]{:S(2)}) copy-start(f32[64,128]{1,0:T(8,128)S(1)} %collective-permute-done.1.halo_col_ref) | copy-start | bytes 98308
  19.9 0.6 copy-start.4
  35.5 6.5 %collective-permute-start.3 = (f32[2,4,64,128]{3,2,1,0:T(8,128)}, f32[2,4,64,128]{3,2,1,0:T(8,128)S(1)}, u32[]{:S(2)}, u32[]{:S(2)}) collective-permute-start(f32[2,4,64,128]{3,2,1,0:T(8,128)} %get-tuple-element.18), channel_id=1, source_target_pairs={{4,0},{8,4},{12,8},{16,12},{20,16},{24,20},{28,24},{5,1},{9,5},{13... | collective-permute-start | bytes 786440 | tf_op jit(solution)/shard_map/ppermute | solution.py:355
  37.8 7.9 %collective-permute-start.4 = (f32[2,4,64,128]{3,2,1,0:T(8,128)}, f32[2,4,64,128]{3,2,1,0:T(8,128)S(1)}, u32[]{:S(2)}, u32[]{:S(2)}) collective-permute-start(f32[2,4,64,128]{3,2,1,0:T(8,128)} %get-tuple-element.19), channel_id=1, source_target_pairs={{0,4},{4,8},{8,12},{12,16},{16,20},{20,24},{24,28},{1,5},{5,9},{9,... | collective-permute-start | bytes 786440 | tf_op jit(solution)/shard_map/ppermute | solution.py:356
  42.0 3.7 %copy-start = (f32[2,4,64,128]{3,2,1,0:T(8,128)}, f32[2,4,64,128]{3,2,1,0:T(8,128)S(1)}, u32[]{:S(2)}) copy-start(f32[2,4,64,128]{3,2,1,0:T(8,128)S(1)} %collective-permute-done.3.below_ref) | copy-start | bytes 786436
  45.7 0.7 copy-start.1
  48.3 13.5 %collective-permute-start.5 = (f32[4,32,128]{2,1,0:T(8,128)}, f32[4,32,128]{2,1,0:T(8,128)S(1)}, u32[]{:S(2)}, u32[]{:S(2)}) collective-permute-start(f32[4,32,128]{2,1,0:T(8,128)} %get-tuple-element.22), channel_id=1, source_target_pairs={{1,0},{2,1},{3,2},{5,4},{6,5},{7,6},{9,8},{10,9},{11,10},{13,12},{... | collective-permute-start | bytes 196616 | tf_op jit(solution)/shard_map/ppermute | solution.py:359
  51.7 11.6 %collective-permute-start.6 = (f32[4,32,128]{2,1,0:T(8,128)}, f32[4,32,128]{2,1,0:T(8,128)S(1)}, u32[]{:S(2)}, u32[]{:S(2)}) collective-permute-start(f32[4,32,128]{2,1,0:T(8,128)} %get-tuple-element.21.own_right_ref), channel_id=1, source_target_pairs={{0,1},{1,2},{2,3},{4,5},{5,6},{6,7},{8,9},{9,10},{10,11},{12,13},{... | collective-permute-start | bytes 196616 | tf_op jit(solution)/shard_map/ppermute | solution.py:360
  61.8 1.5 %copy-start.2 = (f32[4,32,128]{2,1,0:T(8,128)}, f32[4,32,128]{2,1,0:T(8,128)S(1)}, u32[]{:S(2)}) copy-start(f32[4,32,128]{2,1,0:T(8,128)S(1)} %collective-permute-done.5.from_right_ref) | copy-start | bytes 196612
  63.3 0.6 copy-start.3

commit v2 on v1

v2 whole, which is shorter than its diff:
```python
import functools
import math

import jax
import jax.numpy as jnp
from jax import lax
from jax.experimental import pallas as pl
from jax.experimental.pallas import tpu as pltpu
from jax.sharding import PartitionSpec as P

BRICK = 64
SLAB = 64
ROWS = 64
COLS = 128
EXT = 208
LN2 = math.log(2.0)
VMEM_SPEC = pl.BlockSpec(memory_space=pltpu.VMEM)
SMEM_SPEC = pl.BlockSpec(memory_space=pltpu.SMEM)
INTERPRET = False


def call(kernel, out_shape, in_specs, scratch=(), flops=1000, bytes_moved=1000):
    specs = jax.tree.map(lambda _: VMEM_SPEC, out_shape)
    return pl.pallas_call(
        kernel,
        out_shape=out_shape,
        in_specs=in_specs,
        out_specs=specs,
        scratch_shapes=list(scratch),
        interpret=INTERPRET,
        compiler_params=pltpu.CompilerParams(vmem_limit_bytes=24 << 20),
        cost_estimate=pl.CostEstimate(flops=flops, bytes_accessed=bytes_moved, transcendentals=0),
    )


def f32(*shape):
    return jax.ShapeDtypeStruct(shape, jnp.float32)


def lane_table(half):
    source = lax.broadcasted_iota(jnp.int32, (2 * COLS, COLS), 0) % COLS
    target = lax.broadcasted_iota(jnp.int32, (2 * COLS, COLS), 1)
    local = target % BRICK
    start = target - local
    pair = local // 2
    weight = jnp.where(local % 2 == 1, 0.5, -0.5)
    inside = local < 2 * half
    low = jnp.where(inside & (source == start + pair), 1.0, 0.0)
    high = jnp.where(inside & (source == start + half + pair), weight, 0.0)
    return (low + high).astype(jnp.bfloat16)


def lane_lift(block, table):
    coarse = block.astype(jnp.bfloat16)
    rest = (block - coarse.astype(jnp.float32)).astype(jnp.bfloat16)
    both = jnp.concatenate([coarse, rest], axis=1)
    return jnp.dot(both, table, preferred_element_type=jnp.float32)


def lift_kernel(c_ref, d_ref, row_ref, col_ref, s2_ref, s1_ref, plane_ref):
    lane = lax.broadcasted_iota(jnp.int32, (1, COLS), 1)

    def level(half, below, out_ref, on_result, init, unroll):
        table = lane_table(half)

        def step(i, carry):
            if below is None:
                low = c_ref[i, : 2 * half, :]
            else:
                corner = jnp.where(lane % BRICK < half, below[i], c_ref[i, :half, :])
                low = jnp.concatenate([corner, c_ref[i, half : 2 * half, :]], axis=0)
            high = c_ref[i + half, : 2 * half, :]
            planes = []
            even = low - 0.5 * high
            for part in (even, even + high):
                row_even = part[:half] - 0.5 * part[half:]
                planes += [row_even, row_even + part[half:]]
            result = lane_lift(jnp.concatenate(planes, axis=0), table)
            for odd in range(2):
                for row_odd in range(2):
                    start = (2 * odd + row_odd) * half
                    out_ref[2 * i + odd, pl.ds(row_odd, half, stride=2), :] = result[start : start + half]
            return on_result(i, result, carry)

        return lax.fori_loop(0, half, step, init, unroll=unroll)

    def ignore(i, result, carry):
        return carry

    def boundary(i, result, plane):
        for odd in range(2):
            z = 2 * i + odd
            piece = result[64 * odd : 64 * odd + 64]
            row_ref[pl.ds(z, 1), :] = piece[63:64]
            plane = jnp.where(lane == z, pltpu.roll(piece, z + 1, 1), plane)
        return plane

    level(8, None, s2_ref, ignore, 0, 2)
    level(16, s2_ref, s1_ref, ignore, 0, 2)
    plane = level(32, s1_ref, d_ref, boundary, jnp.zeros((64, COLS), jnp.float32), 2)
    plane_ref[...] = plane
    for row_odd in range(2):
        col_ref[pl.ds(row_odd, 32, stride=2), :] = plane_ref[pl.ds(32 * row_odd, 32), :]
    row_ref[pl.ds(64, 8), :] = jnp.broadcast_to(plane[63:64], (8, COLS))


def optics(sheared, rate):
    soft = jnp.maximum(sheared, 0.0) + jnp.log(1.0 + jnp.exp(-jnp.abs(sheared)))
    return (
        jnp.tanh(0.75 * sheared),
        jnp.exp(-0.5 * (sheared * sheared)),
        jnp.tanh(0.4 - 0.5 * sheared),
        jnp.exp(-rate * soft),
    )


def absorb_sample(acc_ref, half, rows, tints, keep):
    through = acc_ref[4 * half + 3, rows, :]
    after = through * keep
    weight = through - after
    acc_ref[4 * half + 3, rows, :] = after
    for channel in range(3):
        acc_ref[4 * half + channel, rows, :] += weight * tints[channel]


def shade_kernel(
    scale, shift_ref, frac_ref, absorb_ref, edge_ref, d_ref, halo_row_ref, halo_col_ref, corner_ref, last_ref,
    fvec_ref, up_ref, own_ref, down_ref, acc_ref, v_ref, hu_ref,
):
    lane = lax.broadcasted_iota(jnp.int32, (8, COLS), 1)
    sub = lax.broadcasted_iota(jnp.int32, (8, COLS), 0)
    first_lane = lane == 0
    last_row = edge_ref[0] == 1
    last_col = edge_ref[1] == 1
    zero = jnp.zeros((8, COLS), jnp.float32)
    fy_lanes = fvec_ref[0:1, :]
    fx_lanes = fvec_ref[1:2, :]
    rate_lanes = fvec_ref[2:3, :] * scale

    for index in range(8):
        acc_ref[index] = jnp.full((EXT, COLS), 1.0 if index % 4 == 3 else 0.0, jnp.float32)

    def lerp_plane(plane, above, t):
        here = plane[8 * t : 8 * t + 8, :] if t < 8 else zero
        before = above if t == 0 else plane[8 * t - 1 : 8 * t, :]
        behind = jnp.where(sub == 0, before, pltpu.roll(here, 1, 0))
        return here + fy_lanes * (behind - here)

    for t in range(9):
        hu_ref[pl.ds(8 * t, 8), :] = lerp_plane(halo_col_ref, corner_ref[7:8, :], t)

    def sheared_tile(z, t, fy, fx, k):
        if t == 0:
            here = d_ref[z, 0:8, :]
            behind = jnp.where(sub == 0, halo_row_ref[pl.ds(z, 1), :], pltpu.roll(here, 1, 0))
        elif t == 8:
            here = zero
            behind = jnp.where(sub == 0, d_ref[z, 63:64, :], 0.0)
        else:
            here = d_ref[z, 8 * t : 8 * t + 8, :]
            behind = d_ref[z, 8 * t - 1 : 8 * t + 7, :]
        mixed = here + fy * (behind - here)
        left = jnp.where(first_lane, pltpu.roll(hu_ref[pl.ds(8 * t, 8), :], COLS - z, 1), pltpu.roll(mixed, 1, 1))
        return pltpu.roll(mixed + fx * (left - mixed), k, 1)

    def shade_tile(z, t, fy, fx, k, rate, right):
        *tints, keep = optics(sheared_tile(z, t, fy, fx, k), rate)
        if t == 8:
            keep = jnp.where(sub == 0, keep, 1.0)
        rows = pl.ds(shift_ref[0, z] + 64 + 8 * t, 8)
        absorb_sample(acc_ref, 0, rows, tints, jnp.where(right, 1.0, keep))
        absorb_sample(acc_ref, 1, rows, tints, jnp.where(right, keep, 1.0))

    def slice_scalars(z):
        k = shift_ref[1, z] + 64
        return frac_ref[0, z], frac_ref[1, z], k, absorb_ref[z] * scale, lane < k

    @pl.when(last_col)
    def _():
        for t in range(9):
            *tints, keep = optics(fx_lanes * lerp_plane(last_ref, halo_row_ref[64:65, :], t), rate_lanes)
            if t == 8:
                keep = jnp.where((sub == 0) & last_row, keep, 1.0)
            for part, value in enumerate((*tints, keep)):
                v_ref[part, pl.ds(8 * t, 8), :] = value

        def column_step(group):
            for offset in range(2):
                z = 2 * group + offset
                k = shift_ref[1, z] + 64
                at = lane == k
                for t in range(9):
                    values = [
                        pltpu.roll(v_ref[part, pl.ds(8 * t, 8), :], (k - z + COLS) % COLS, 1) for part in range(4)
                    ]
                    rows = pl.ds(shift_ref[0, z] + 64 + 8 * t, 8)
                    absorb_sample(acc_ref, 1, rows, values[:3], jnp.where(at, values[3], 1.0))
            return group + 1

        lax.while_loop(
            lambda group: (group < SLAB // 2) & (shift_ref[1, jnp.minimum(2 * group, SLAB - 1)] < 0), column_step, 0
        )

    @pl.when(last_row)
    def _():
        def row_step(group):
            for offset in range(4):
                z = 4 * group + offset
                fy, fx, k, rate, right = slice_scalars(z)
                shade_tile(z, 8, fy, fx, k, rate, right)
            return group + 1

        lax.while_loop(
            lambda group: (group < SLAB // 4) & (shift_ref[0, jnp.minimum(4 * group, SLAB - 1)] < 0), row_step, 0
        )

    def slice_step(z, carry):
        fy, fx, k, rate, right = slice_scalars(z)
        for t in range(8):
            shade_tile(z, t, fy, fx, k, rate, right)
        return carry

    lax.fori_loop(0, SLAB, slice_step, 0, unroll=2)

    for out, out_ref in enumerate((up_ref, own_ref, down_ref)):
        for half in range(2):
            for channel in range(4):
                value = acc_ref[4 * half + channel, pl.ds(64 * out, 64), :]
                out_ref[half, channel] = 1.0 - value if channel == 3 else value


def over(front, behind):
    through = 1.0 - front[3]
    return [front[c] + through * behind[c] for c in range(4)]


def channels(ref, *index):
    return [ref[(*index, c)] for c in range(4)]


def rows_kernel(own_ref, below_ref, above_ref, mine_ref, left_ref, right_ref):
    lane = lax.broadcasted_iota(jnp.int32, (1, COLS), 1)
    halves = []
    for half in range(2):
        merged = over(channels(own_ref, half), channels(above_ref, half))
        halves.append(over(channels(below_ref, half), merged))
    for c in range(4):
        low, high = halves[0][c], halves[1][c]
        low_turned, high_turned = pltpu.roll(low, 64, 1), pltpu.roll(high, 64, 1)
        mine_ref[c] = jnp.where(lane < 64, low_turned, high_turned)
        left_ref[c] = jnp.where(lane < 64, low[:32], low_turned[32:])
        right_ref[c] = jnp.where(lane < 64, high_turned[:32], high[32:])


def columns_kernel(scale, mine_ref, from_right_ref, from_left_ref, zrow_ref, zcol_ref, out_ref):
    lane = lax.broadcasted_iota(jnp.int32, (1, COLS), 1)
    front, behind = [], []
    for c in range(4):
        piece = from_right_ref[c]
        upper = jnp.concatenate([pltpu.roll(piece, 64, 1), piece], axis=0)
        piece = from_left_ref[c]
        lower = jnp.concatenate([piece, pltpu.roll(piece, 64, 1)], axis=0)
        own = mine_ref[c]
        front.append(jnp.where(lane < 64, own, upper))
        behind.append(jnp.where(lane < 64, lower, own))
    inner = over(front, behind)
    pre = jnp.maximum(zrow_ref[:, 0:1], zcol_ref[0:1, :])
    post = jnp.minimum(jnp.maximum(zrow_ref[:, 1:2], zcol_ref[1:2, :]), zcol_ref[2:3, :] - pre)
    flat = []
    for amount in (pre, jnp.maximum(post, 0.0)):
        fade = 1.0 - jnp.exp((-scale * LN2) * amount)
        flat.append([jnp.zeros_like(fade), fade, math.tanh(0.4) * fade, fade])
    whole = over(flat[0], over(inner, flat[1]))
    pieces = out_ref.shape[0]
    height = ROWS // pieces
    for p in range(pieces):
        for c in range(4):
            out_ref[p, c] = whole[c][p * height : (p + 1) * height]


def fold_kernel(in_ref, out_ref):
    merged = channels(in_ref, 0)
    for slab in range(1, in_ref.shape[0]):
        merged = over(merged, channels(in_ref, slab))
    out_ref[0] = 0.5 * (merged[3] + merged[0])
    out_ref[1] = merged[1]
    out_ref[2] = 0.5 * (merged[3] + merged[2])
    out_ref[3] = merged[3]


def body(coefficients, shifts, fraction, absorb):
    depth_count = lax.axis_size("depth")
    row_count = lax.axis_size("imgy")
    col_count = lax.axis_size("imgx")
    scale = 2.0 / (SLAB * depth_count)
    iy, ix = lax.axis_index("imgy"), lax.axis_index("imgx")

    volume, row_plane, col_plane = call(
        lift_kernel,
        (f32(SLAB, ROWS, COLS), f32(72, COLS), f32(ROWS, COLS)),
        [VMEM_SPEC],
        [
            pltpu.VMEM((16, 16, COLS), jnp.float32),
            pltpu.VMEM((32, 32, COLS), jnp.float32),
            pltpu.VMEM((64, COLS), jnp.float32),
        ],
        flops=300_000_000,
        bytes_moved=4 << 20,
    )(coefficients)

    row_up = [(i, i + 1) for i in range(row_count - 1)]
    row_down = [(i + 1, i) for i in range(row_count - 1)]
    col_up = [(i, i + 1) for i in range(col_count - 1)]
    col_down = [(i + 1, i) for i in range(col_count - 1)]
    both_up = [
        (y * col_count + x, (y + 1) * col_count + x + 1) for y in range(row_count - 1) for x in range(col_count - 1)
    ]
    halo_row = lax.ppermute(row_plane, "imgy", row_up)
    halo_col = lax.ppermute(col_plane, "imgx", col_up)
    corner = lax.ppermute(col_plane[56:64], ("imgy", "imgx"), both_up)

    shift_rows, shift_cols = shifts[0], shifts[1]
    edge = jnp.stack([iy == row_count - 1, ix == col_count - 1]).astype(jnp.int32)
    vectors = jnp.pad(jnp.concatenate([fraction, absorb[None]], axis=0), ((0, 5), (0, COLS - SLAB)))

    sent = f32(2, 4, ROWS, COLS)
    up, own, down = call(
        functools.partial(shade_kernel, scale),
        (sent, sent, sent),
        [SMEM_SPEC] * 4 + [VMEM_SPEC] * 6,
        [
            pltpu.VMEM((8, EXT, COLS), jnp.float32),
            pltpu.VMEM((4, 72, COLS), jnp.float32),
            pltpu.VMEM((72, COLS), jnp.float32),
        ],
        flops=300_000_000,
        bytes_moved=4 << 20,
    )(shifts, fraction, absorb, edge, volume, halo_row, halo_col, corner, col_plane, vectors)

    below = lax.ppermute(up, "imgy", row_down)
    above = lax.ppermute(down, "imgy", row_up)
    packed = f32(4, ROWS // 2, COLS)
    mine, left, right = call(rows_kernel, (f32(4, ROWS, COLS), packed, packed), [VMEM_SPEC] * 3)(own, below, above)
    from_right = lax.ppermute(left, "imgx", col_down)
    from_left = lax.ppermute(right, "imgx", col_up)

    image_rows = iy * ROWS + jnp.arange(ROWS, dtype=jnp.int32)
    image_cols = ix * COLS + jnp.arange(COLS, dtype=jnp.int32)

    def outside(pixels, offsets, limit):
        position = pixels[:, None] - offsets[None, :]
        pre = jnp.sum(jnp.where(position > limit, absorb[None, :], 0.0), axis=1)
        post = jnp.sum(jnp.where(position < 0, absorb[None, :], 0.0), axis=1)
        return pre, post

    zrow = jnp.stack(outside(image_rows, shift_rows, ROWS * row_count), axis=1)
    zcol = jnp.stack(
        [*outside(image_cols, shift_cols, COLS * col_count), jnp.broadcast_to(jnp.sum(absorb), (COLS,))], axis=0
    )
    pieces = call(
        functools.partial(columns_kernel, scale),
        f32(depth_count, 4, ROWS // depth_count, COLS),
        [VMEM_SPEC] * 5,
    )(mine, from_right, from_left, zrow, zcol)
    incoming = lax.all_to_all(pieces, "depth", split_axis=0, concat_axis=0, tiled=True)
    image = call(fold_kernel, f32(4, ROWS // depth_count, COLS), [VMEM_SPEC])(incoming)
    return image[:, None]


def solution(mesh):
    in_specs = (P("depth", "imgy", "imgx"), P(None, "depth"), P(None, "depth"), P("depth"))
    out_specs = P(None, "imgy", "depth", "imgx")
    return jax.shard_map(body, mesh=mesh, in_specs=in_specs, out_specs=out_specs, check_vma=False)
```

time: 86.6 us -> 69.2 us (0.80); the launches traced: 85.1 us -> 68.6 us
  Pallas kernels: 28.9 us -> 20.1 us
  starting transfers between devices: 24.2 us -> 19.7 us
  other arithmetic: 3.61 us -> 1.06 us
  waiting for transfers between devices: 6.35 us -> 8.35 us
  local copies, waits for them, and re-layouts: 4.06 us -> 2.42 us
  blocking collectives: 17.8 us -> 16.7 us
    ppermute x1, starting transfers between devices: 9.42 us -> 4.88 us  [body(): from_left = lax.ppermute(right, 'imgx', col_up)]
    pallas_call x1, Pallas kernels: 8.69 us -> 5.79 us  [body(): call(lift_kernel, (f32(SLAB, ROWS, COLS), f32(72, COLS), f32(ROWS, COLS))...]
    pallas_call x1, Pallas kernels: 1.92 us -> 0.14 us  [body(): call(rows_kernel, (f32(4, ROWS, COLS), packed, packed), [VMEM_SPEC] * 3)]
    pallas_call x1, Pallas kernels: 1.78 us -> 0.13 us  [body(): call(functools.partial(columns_kernel, scale), f32(depth_count, 4, ROWS /...]
    pallas_call x1, Pallas kernels: 14.9 us -> 13.4 us  [body(): call(functools.partial(shade_kernel, scale), (sent, sent, sent), [SMEM_SP...]
    ppermute x1, waiting for transfers between devices: 0.01 us -> 1.5 us  [body(): corner = lax.ppermute(col_plane[56:64], ('imgy', 'imgx'), both_up)]
    all_to_all x1, blocking collectives: 17.8 us -> 16.7 us  [body(): lax.all_to_all(pieces, 'depth', split_axis=0, concat_axis=0, tiled=True)]
    pallas_call x1, Pallas kernels: 1.53 us -> 0.63 us  [body(): call(fold_kernel, f32(4, ROWS // depth_count, COLS), [VMEM_SPEC])(incoming)]
  transfers between devices with their start and end apart: 7 -> 7, of which waited for: 3 -> 5; matrix products, arithmetic and copies ran while one was open for 7% -> 3% of each run, Pallas kernels for 0% -> 0%
where the time goes in v2:
time: 69.2 us; the launch traced here: 68.6 us
  Pallas kernels  20.1 us (29%)
  starting transfers between devices  19.7 us (28%)
  blocking collectives  16.7 us (24%)
  waiting for transfers between devices  8.35 us (12%)
  local copies, waits for them, and re-layouts  2.42 us (3%)
  other arithmetic  1.06 us (2%)
    all_to_all x1, blocking collectives, body(): lax.all_to_all(pieces, 'depth', split_axis=0, concat_axis=0, tiled=True)  16.7 us
    pallas_call x1, Pallas kernels, body(): call(functools.partial(shade_kernel, scale), (sent, sent, sent), [SMEM_SP...  13.4 us
    pallas_call x1, Pallas kernels, body(): call(lift_kernel, (f32(SLAB, ROWS, COLS), f32(72, COLS), f32(ROWS, COLS))...  5.79 us
    ppermute x1, starting transfers between devices, body(): from_left = lax.ppermute(right, 'imgx', col_up)  4.88 us
    ppermute x1, waiting for transfers between devices, body(): above = lax.ppermute(down, 'imgy', row_up)  3.69 us
    ppermute x1, starting transfers between devices, body(): from_right = lax.ppermute(left, 'imgx', col_down)  3.37 us
    ppermute x1, starting transfers between devices, body(): halo_col = lax.ppermute(col_plane, 'imgx', col_up)  3.11 us
    ppermute x1, starting transfers between devices, body(): above = lax.ppermute(down, 'imgy', row_up)  2.41 us
  transfers between devices with their start and end apart: 7, of which 5 were waited for; matrix products, arithmetic and copies ran while one was open for 3% of the time, Pallas kernels for 0%

profile of v2, /device:TPU:20, one launch (start us, length us, event | category | flops | bytes accessed | tf_op | source)
XLA Modules:
  0.0 68.6 jit_solution(15492643596999404450)
XLA Ops:
  0.0 0.0 copy-start
  0.0 1.6 %copy-done = f32[64,64,128]{2,1,0:T(8,128)S(1)} copy-done((f32[64,64,128]{2,1,0:T(8,128)S(1)}, f32[64,64,128]{2,1,0:T(8,128)}, u32[]{:S(2)}) %copy-start) | copy-done | bytes 2097176
  1.6 0.0 copy-start.2
  1.6 0.0 copy-start.1
  1.6 0.0 copy-start.3
  1.6 5.8 %shard_map.46 = (f32[64,64,128]{2,1,0:T(8,128)S(1)}, f32[72,128]{1,0:T(8,128)S(1)}, f32[64,128]{1,0:T(8,128)S(1)}) custom-call(f32[64,64,128]{2,1,0:T(8,128)S(1)} %copy-done), custom_call_target="tpu_custom_call" | custom-call | flops 300000000 | bytes 4194304 | tf_op jit(solution)/shard_map/pallas_call | solution.py:298
  7.4 3.1 %collective-permute-start.1 = (f32[64,128]{1,0:T(8,128)S(1)}, f32[64,128]{1,0:T(8,128)S(1)}, u32[]{:S(2)}, u32[]{:S(2)}) collective-permute-start(f32[64,128]{1,0:T(8,128)S(1)} %get-tuple-element.16.last_ref), channel_id=1, source_target_pairs={{0,1},{1,2},{2,3},{4,5},{5,6},{6,7},{8,9},{9,10},{10,11},{12,13},{... | collective-permute-start | bytes 98312 | tf_op jit(solution)/shard_map/ppermute | solution.py:319
  10.5 1.9 %collective-permute-start.2 = (f32[8,128]{1,0:T(8,128)S(1)}, f32[8,128]{1,0:T(8,128)S(1)}, u32[]{:S(2)}, u32[]{:S(2)}) collective-permute-start(f32[8,128]{1,0:T(8,128)S(1)} %slice.9), channel_id=1, source_target_pairs={{0,5},{1,6},{2,7},{4,9},{5,10},{6,11},{8,13},{9,14},{10,15},{12,17... | collective-permute-start | bytes 12296 | tf_op jit(solution)/shard_map/ppermute | solution.py:320
  12.5 2.1 %collective-permute-start = (f32[72,128]{1,0:T(8,128)S(1)}, f32[72,128]{1,0:T(8,128)S(1)}, u32[]{:S(2)}, u32[]{:S(2)}) collective-permute-start(f32[72,128]{1,0:T(8,128)S(1)} %get-tuple-element.15), channel_id=1, source_target_pairs={{0,4},{4,8},{8,12},{12,16},{16,20},{20,24},{24,28},{1,5},{5,9},{9,... | collective-permute-start | bytes 110600 | tf_op jit(solution)/shard_map/ppermute | solution.py:318
  14.6 0.0 copy-done.2
  14.6 0.0 copy-done.1
  14.6 0.0 copy-done.3
  14.7 0.1 select_reduce_fusion.1
  14.8 0.1 add_convert_fusion.edge_ref
  14.8 1.5 %collective-permute-done.2.corner_ref = f32[8,128]{1,0:T(8,128)S(1)} collective-permute-done((f32[8,128]{1,0:T(8,128)S(1)}, f32[8,128]{1,0:T(8,128)S(1)}, u32[]{:S(2)}, u32[]{:S(2)}) %collective-permute-start.2) | collective-permute-done | bytes 4128 | tf_op jit(solution)/shard_map/ppermute | solution.py:320
  16.3 0.0 collective-permute-done.1.halo_col_ref
  16.4 1.4 %collective-permute-done.halo_row_ref = f32[72,128]{1,0:T(8,128)S(1)} collective-permute-done((f32[72,128]{1,0:T(8,128)S(1)}, f32[72,128]{1,0:T(8,128)S(1)}, u32[]{:S(2)}, u32[]{:S(2)}) %collective-permute-start) | collective-permute-done | bytes 36896 | tf_op jit(solution)/shard_map/ppermute | solution.py:318
  17.7 13.4 %shard_map.47 = (f32[2,4,64,128]{3,2,1,0:T(8,128)S(1)}, f32[2,4,64,128]{3,2,1,0:T(8,128)S(1)}, f32[2,4,64,128]{3,2,1,0:T(8,128)S(1)}) custom-call(s32[2,64]{1,0:T(2,128)S(1)} %copy-done.2, f32[2,64]{1,0:T(2,128)S(1)} %copy-done.3, f32[64]{0:T(128)S(1)} %copy-done.1, s32[2]{0:T(128)S(1)} %add_convert_fusion.edge_ref, ...), custom_call_target="tpu_custom_call" | custom-call | flops 300000000 | bytes 4194304 | tf_op jit(solution)/shard_map/pallas_call | solution.py:327
  31.1 1.9 %collective-permute-start.3 = (f32[2,4,64,128]{3,2,1,0:T(8,128)S(1)}, f32[2,4,64,128]{3,2,1,0:T(8,128)S(1)}, u32[]{:S(2)}, u32[]{:S(2)}) collective-permute-start(f32[2,4,64,128]{3,2,1,0:T(8,128)S(1)} %get-tuple-element.18), channel_id=1, source_target_pairs={{4,0},{8,4},{12,8},{16,12},{20,16},{24,20},{28,24},{5,1},{9,5},{13... | collective-permute-start | bytes 786440 | tf_op jit(solution)/shard_map/ppermute | solution.py:340
  33.1 2.4 %collective-permute-start.4 = (f32[2,4,64,128]{3,2,1,0:T(8,128)S(1)}, f32[2,4,64,128]{3,2,1,0:T(8,128)S(1)}, u32[]{:S(2)}, u32[]{:S(2)}) collective-permute-start(f32[2,4,64,128]{3,2,1,0:T(8,128)S(1)} %get-tuple-element.19), channel_id=1, source_target_pairs={{0,4},{4,8},{8,12},{12,16},{16,20},{20,24},{24,28},{1,5},{5,9},{9,... | collective-permute-start | bytes 786440 | tf_op jit(solution)/shard_map/ppermute | solution.py:341
  35.5 0.2 select_reduce_fusion.3
  35.7 0.6 reduce_sum.49
  36.3 0.7 %pad.7.clone = f32[3]{0:T(128)S(1)} pad(f32[1]{0:T(128)} %bitcast.12, f32[]{:T(128)} %constant.29), padding=2_0 | pad | bytes 20 | tf_op jit(solution)/shard_map/stack | solution.py:357
  37.0 0.1 maximum_maximum_fusion.zcol_ref
  37.1 0.0 collective-permute-done.3.below_ref
  37.1 3.7 %collective-permute-done.4.above_ref = f32[2,4,64,128]{3,2,1,0:T(8,128)S(1)} collective-permute-done((f32[2,4,64,128]{3,2,1,0:T(8,128)S(1)}, f32[2,4,64,128]{3,2,1,0:T(8,128)S(1)}, u32[]{:S(2)}, u32[]{:S(2)}) %collective-permute-start.4) | collective-permute-done | bytes 262176 | tf_op jit(solution)/shard_map/ppermute | solution.py:341
  40.8 0.1 shard_map.48
  40.9 3.4 %collective-permute-start.5 = (f32[4,32,128]{2,1,0:T(8,128)S(1)}, f32[4,32,128]{2,1,0:T(8,128)S(1)}, u32[]{:S(2)}, u32[]{:S(2)}) collective-permute-start(f32[4,32,128]{2,1,0:T(8,128)S(1)} %get-tuple-element.21), channel_id=1, source_target_pairs={{1,0},{2,1},{3,2},{5,4},{6,5},{7,6},{9,8},{10,9},{11,10},{13,12},{... | collective-permute-start | bytes 196616 | tf_op jit(solution)/shard_map/ppermute | solution.py:344
  44.3 4.9 %collective-permute-start.6 = (f32[4,32,128]{2,1,0:T(8,128)S(1)}, f32[4,32,128]{2,1,0:T(8,128)S(1)}, u32[]{:S(2)}, u32[]{:S(2)}) collective-permute-start(f32[4,32,128]{2,1,0:T(8,128)S(1)} %get-tuple-element.22), channel_id=1, source_target_pairs={{0,1},{1,2},{2,3},{4,5},{5,6},{6,7},{8,9},{9,10},{10,11},{12,13},{... | collective-permute-start | bytes 196616 | tf_op jit(solution)/shard_map/ppermute | solution.py:345
  49.2 0.1 copy.10.zrow_ref
  49.3 0.2 collective-permute-done.5.from_right_ref
  49.5 1.6 %collective-permute-done.6.from_left_ref = f32[4,32,128]{2,1,0:T(8,128)S(1)} collective-permute-done((f32[4,32,128]{2,1,0:T(8,128)S(1)}, f32[4,32,128]{2,1,0:T(8,128)S(1)}, u32[]{:S(2)}, u32[]{:S(2)}) %collective-permute-start.6) | collective-permute-done | bytes 65568 | tf_op jit(solution)/shard_map/ppermute | solution.py:345
  51.1 0.1 shard_map.49
  51.2 16.7 %all_to_all.5.in_ref = f32[8,4,8,128]{3,2,1,0:T(8,128)S(1)} all-to-all(f32[8,4,8,128]{3,2,1,0:T(8,128)S(1)} %shard_map.49), channel_id=1, replica_groups=mesh['depth'=8,'imgy'=8,'imgx'=4] {'depth'}, dimensions={0} | all-to-all | bytes 262144 | tf_op jit(solution)/shard_map/all_to_all | solution.py:365
  67.9 0.6 shard_map.50
  (6 shorter events, 0.0 us)
Async XLA Ops:
  0.0 1.6 %copy-start = (f32[64,64,128]{2,1,0:T(8,128)S(1)}, f32[64,64,128]{2,1,0:T(8,128)}, u32[]{:S(2)}) copy-start(f32[64,64,128]{2,1,0:T(8,128)} %c_ref.1) | copy-start | bytes 6291460
  1.6 13.0 %copy-start.2 = (s32[2,64]{1,0:T(2,128)S(1)}, s32[2,64]{1,0:T(2,128)}, u32[]{:S(2)}) copy-start(s32[2,64]{1,0:T(2,128)} %shift_ref.1) | copy-start | bytes 1540
  1.6 13.0 %copy-start.1 = (f32[64]{0:T(128)S(1)}, f32[64]{0:T(128)}, u32[]{:S(2)}) copy-start(f32[64]{0:T(128)} %absorb_ref.1) | copy-start | bytes 772
  1.6 13.0 %copy-start.3 = (f32[2,64]{1,0:T(2,128)S(1)}, f32[2,64]{1,0:T(2,128)}, u32[]{:S(2)}) copy-start(f32[2,64]{1,0:T(2,128)} %frac_ref.1) | copy-start | bytes 1540
  7.4 9.0 %collective-permute-start.1 = (f32[64,128]{1,0:T(8,128)S(1)}, f32[64,128]{1,0:T(8,128)S(1)}, u32[]{:S(2)}, u32[]{:S(2)}) collective-permute-start(f32[64,128]{1,0:T(8,128)S(1)} %get-tuple-element.16.last_ref), channel_id=1, source_target_pairs={{0,1},{1,2},{2,3},{4,5},{5,6},{6,7},{8,9},{9,10},{10,11},{12,13},{... | collective-permute-start | bytes 98312 | tf_op jit(solution)/shard_map/ppermute | solution.py:319
  10.5 5.8 %collective-permute-start.2 = (f32[8,128]{1,0:T(8,128)S(1)}, f32[8,128]{1,0:T(8,128)S(1)}, u32[]{:S(2)}, u32[]{:S(2)}) collective-permute-start(f32[8,128]{1,0:T(8,128)S(1)} %slice.9), channel_id=1, source_target_pairs={{0,5},{1,6},{2,7},{4,9},{5,10},{6,11},{8,13},{9,14},{10,15},{12,17... | collective-permute-start | bytes 12296 | tf_op jit(solution)/shard_map/ppermute | solution.py:320
  12.5 5.3 %collective-permute-start = (f32[72,128]{1,0:T(8,128)S(1)}, f32[72,128]{1,0:T(8,128)S(1)}, u32[]{:S(2)}, u32[]{:S(2)}) collective-permute-start(f32[72,128]{1,0:T(8,128)S(1)} %get-tuple-element.15), channel_id=1, source_target_pairs={{0,4},{4,8},{8,12},{12,16},{16,20},{20,24},{24,28},{1,5},{5,9},{9,... | collective-permute-start | bytes 110600 | tf_op jit(solution)/shard_map/ppermute | solution.py:318
  31.1 5.9 %collective-permute-start.3 = (f32[2,4,64,128]{3,2,1,0:T(8,128)S(1)}, f32[2,4,64,128]{3,2,1,0:T(8,128)S(1)}, u32[]{:S(2)}, u32[]{:S(2)}) collective-permute-start(f32[2,4,64,128]{3,2,1,0:T(8,128)S(1)} %get-tuple-element.18), channel_id=1, source_target_pairs={{4,0},{8,4},{12,8},{16,12},{20,16},{24,20},{28,24},{5,1},{9,5},{13... | collective-permute-start | bytes 786440 | tf_op jit(solution)/shard_map/ppermute | solution.py:340
  33.1 7.7 %collective-permute-start.4 = (f32[2,4,64,128]{3,2,1,0:T(8,128)S(1)}, f32[2,4,64,128]{3,2,1,0:T(8,128)S(1)}, u32[]{:S(2)}, u32[]{:S(2)}) collective-permute-start(f32[2,4,64,128]{3,2,1,0:T(8,128)S(1)} %get-tuple-element.19), channel_id=1, source_target_pairs={{0,4},{4,8},{8,12},{12,16},{16,20},{20,24},{24,28},{1,5},{5,9},{9,... | collective-permute-start | bytes 786440 | tf_op jit(solution)/shard_map/ppermute | solution.py:341
  40.9 8.6 %collective-permute-start.5 = (f32[4,32,128]{2,1,0:T(8,128)S(1)}, f32[4,32,128]{2,1,0:T(8,128)S(1)}, u32[]{:S(2)}, u32[]{:S(2)}) collective-permute-start(f32[4,32,128]{2,1,0:T(8,128)S(1)} %get-tuple-element.21), channel_id=1, source_target_pairs={{1,0},{2,1},{3,2},{5,4},{6,5},{7,6},{9,8},{10,9},{11,10},{13,12},{... | collective-permute-start | bytes 196616 | tf_op jit(solution)/shard_map/ppermute | solution.py:344
  44.3 6.8 %collective-permute-start.6 = (f32[4,32,128]{2,1,0:T(8,128)S(1)}, f32[4,32,128]{2,1,0:T(8,128)S(1)}, u32[]{:S(2)}, u32[]{:S(2)}) collective-permute-start(f32[4,32,128]{2,1,0:T(8,128)S(1)} %get-tuple-element.22), channel_id=1, source_target_pairs={{0,1},{1,2},{2,3},{4,5},{5,6},{6,7},{8,9},{9,10},{10,11},{12,13},{... | collective-permute-start | bytes 196616 | tf_op jit(solution)/shard_map/ppermute | solution.py:345

commit v3 on v2

--- a/solution.py
+++ b/solution.py
@@ -13,6 +13,9 @@
 ROWS = 64
 COLS = 128
 EXT = 208
+SLICE_UNROLL = 8
+ROW_UNROLL = 16
+COLUMN_UNROLL = 8
 LN2 = math.log(2.0)
 VMEM_SPEC = pl.BlockSpec(memory_space=pltpu.VMEM)
 SMEM_SPEC = pl.BlockSpec(memory_space=pltpu.SMEM)
@@ -95,9 +98,9 @@
             plane = jnp.where(lane == z, pltpu.roll(piece, z + 1, 1), plane)
         return plane
 
-    level(8, None, s2_ref, ignore, 0, 2)
-    level(16, s2_ref, s1_ref, ignore, 0, 2)
-    plane = level(32, s1_ref, d_ref, boundary, jnp.zeros((64, COLS), jnp.float32), 2)
+    level(8, None, s2_ref, ignore, 0, 8)
+    level(16, s2_ref, s1_ref, ignore, 0, 16)
+    plane = level(32, s1_ref, d_ref, boundary, jnp.zeros((64, COLS), jnp.float32), 16)
     plane_ref[...] = plane
     for row_odd in range(2):
         col_ref[pl.ds(row_odd, 32, stride=2), :] = plane_ref[pl.ds(32 * row_odd, 32), :]
@@ -114,22 +117,21 @@
     )
 
 
-def absorb_sample(acc_ref, half, rows, tints, keep):
-    through = acc_ref[4 * half + 3, rows, :]
+def absorb_sample(view, half, tints, keep):
+    through = view[4 * half + 3]
     after = through * keep
     weight = through - after
-    acc_ref[4 * half + 3, rows, :] = after
+    view[4 * half + 3] = after
     for channel in range(3):
-        acc_ref[4 * half + channel, rows, :] += weight * tints[channel]
+        view[4 * half + channel] = view[4 * half + channel] + weight * tints[channel]
 
 
 def shade_kernel(
     scale, shift_ref, frac_ref, absorb_ref, edge_ref, d_ref, halo_row_ref, halo_col_ref, corner_ref, last_ref,
-    fvec_ref, up_ref, own_ref, down_ref, acc_ref, v_ref, hu_ref,
+    fvec_ref, near_ref, own_ref, far_ref, acc_ref, v_ref, hu_ref,
 ):
-    lane = lax.broadcasted_iota(jnp.int32, (8, COLS), 1)
+    lane = lax.broadcasted_iota(jnp.int32, (1, COLS), 1)
     sub = lax.broadcasted_iota(jnp.int32, (8, COLS), 0)
-    first_lane = lane == 0
     last_row = edge_ref[0] == 1
     last_col = edge_ref[1] == 1
     zero = jnp.zeros((8, COLS), jnp.float32)
@@ -140,92 +142,82 @@
     for index in range(8):
         acc_ref[index] = jnp.full((EXT, COLS), 1.0 if index % 4 == 3 else 0.0, jnp.float32)
 
-    def lerp_plane(plane, above, t):
-        here = plane[8 * t : 8 * t + 8, :] if t < 8 else zero
-        before = above if t == 0 else plane[8 * t - 1 : 8 * t, :]
-        behind = jnp.where(sub == 0, before, pltpu.roll(here, 1, 0))
+    def lerp_plane(plane, above):
+        first = jnp.where(sub == 0, above, pltpu.roll(plane[0:8, :], 1, 0))
+        here = jnp.concatenate([plane[...], zero], axis=0)
+        behind = jnp.concatenate([first, plane[7:63, :], jnp.where(sub == 0, plane[63:64, :], 0.0)], axis=0)
         return here + fy_lanes * (behind - here)
 
-    for t in range(9):
-        hu_ref[pl.ds(8 * t, 8), :] = lerp_plane(halo_col_ref, corner_ref[7:8, :], t)
-
-    def sheared_tile(z, t, fy, fx, k):
-        if t == 0:
-            here = d_ref[z, 0:8, :]
-            behind = jnp.where(sub == 0, halo_row_ref[pl.ds(z, 1), :], pltpu.roll(here, 1, 0))
-        elif t == 8:
-            here = zero
-            behind = jnp.where(sub == 0, d_ref[z, 63:64, :], 0.0)
-        else:
-            here = d_ref[z, 8 * t : 8 * t + 8, :]
-            behind = d_ref[z, 8 * t - 1 : 8 * t + 7, :]
-        mixed = here + fy * (behind - here)
-        left = jnp.where(first_lane, pltpu.roll(hu_ref[pl.ds(8 * t, 8), :], COLS - z, 1), pltpu.roll(mixed, 1, 1))
-        return pltpu.roll(mixed + fx * (left - mixed), k, 1)
-
-    def shade_tile(z, t, fy, fx, k, rate, right):
-        *tints, keep = optics(sheared_tile(z, t, fy, fx, k), rate)
-        if t == 8:
-            keep = jnp.where(sub == 0, keep, 1.0)
-        rows = pl.ds(shift_ref[0, z] + 64 + 8 * t, 8)
-        absorb_sample(acc_ref, 0, rows, tints, jnp.where(right, 1.0, keep))
-        absorb_sample(acc_ref, 1, rows, tints, jnp.where(right, keep, 1.0))
-
-    def slice_scalars(z):
+    hu_ref[...] = lerp_plane(halo_col_ref, corner_ref[7:8, :])
+
+    def window(z, first_row, rows):
+        return acc_ref.at[:, pl.ds(shift_ref[0, z] + 64 + first_row, rows), :]
+
+    def shade(z, here, behind, halo, first_row, mask=None):
         k = shift_ref[1, z] + 64
-        return frac_ref[0, z], frac_ref[1, z], k, absorb_ref[z] * scale, lane < k
+        right = lane < k
+        mixed = here + frac_ref[0, z] * (behind - here)
+        left = jnp.where(lane == 0, pltpu.roll(halo, COLS - z, 1), pltpu.roll(mixed, 1, 1))
+        sheared = pltpu.roll(mixed + frac_ref[1, z] * (left - mixed), k, 1)
+        *tints, keep = optics(sheared, absorb_ref[z] * scale)
+        if mask is not None:
+            keep = jnp.where(mask, keep, 1.0)
+        view = window(z, first_row, here.shape[0])
+        absorb_sample(view, 0, tints, jnp.where(right, 1.0, keep))
+        absorb_sample(view, 1, tints, jnp.where(right, keep, 1.0))
 
     @pl.when(last_col)
     def _():
-        for t in range(9):
-            *tints, keep = optics(fx_lanes * lerp_plane(last_ref, halo_row_ref[64:65, :], t), rate_lanes)
-            if t == 8:
-                keep = jnp.where((sub == 0) & last_row, keep, 1.0)
-            for part, value in enumerate((*tints, keep)):
-                v_ref[part, pl.ds(8 * t, 8), :] = value
+        *tints, keep = optics(fx_lanes * lerp_plane(last_ref, halo_row_ref[64:65, :]), rate_lanes)
+        row = lax.broadcasted_iota(jnp.int32, (72, COLS), 0)
+        keep = jnp.where((row < 64) | ((row == 64) & last_row), keep, 1.0)
+        for part, value in enumerate((*tints, keep)):
+            v_ref[part] = value
 
         def column_step(group):
-            for offset in range(2):
-                z = 2 * group + offset
+            for offset in range(COLUMN_UNROLL):
+                z = COLUMN_UNROLL * group + offset
                 k = shift_ref[1, z] + 64
-                at = lane == k
-                for t in range(9):
-                    values = [
-                        pltpu.roll(v_ref[part, pl.ds(8 * t, 8), :], (k - z + COLS) % COLS, 1) for part in range(4)
-                    ]
-                    rows = pl.ds(shift_ref[0, z] + 64 + 8 * t, 8)
-                    absorb_sample(acc_ref, 1, rows, values[:3], jnp.where(at, values[3], 1.0))
+                *tints, keep = [pltpu.roll(v_ref[part], (k - z + COLS) % COLS, 1) for part in range(4)]
+                absorb_sample(window(z, 0, 72), 1, tints, jnp.where(lane == k, keep, 1.0))
             return group + 1
 
         lax.while_loop(
-            lambda group: (group < SLAB // 2) & (shift_ref[1, jnp.minimum(2 * group, SLAB - 1)] < 0), column_step, 0
+            lambda group: (group < SLAB // COLUMN_UNROLL)
+            & (shift_ref[1, jnp.minimum(COLUMN_UNROLL * group, SLAB - 1)] < 0),
+            column_step,
+            0,
         )
 
     @pl.when(last_row)
     def _():
         def row_step(group):
-            for offset in range(4):
-                z = 4 * group + offset
-                fy, fx, k, rate, right = slice_scalars(z)
-                shade_tile(z, 8, fy, fx, k, rate, right)
+            for offset in range(ROW_UNROLL):
+                z = ROW_UNROLL * group + offset
+                behind = jnp.where(sub == 0, d_ref[z, 63:64, :], 0.0)
+                shade(z, zero, behind, hu_ref[64:72, :], 64, sub == 0)
             return group + 1
 
         lax.while_loop(
-            lambda group: (group < SLAB // 4) & (shift_ref[0, jnp.minimum(4 * group, SLAB - 1)] < 0), row_step, 0
+            lambda group: (group < SLAB // ROW_UNROLL)
+            & (shift_ref[0, jnp.minimum(ROW_UNROLL * group, SLAB - 1)] < 0),
+            row_step,
+            0,
         )
 
     def slice_step(z, carry):
-        fy, fx, k, rate, right = slice_scalars(z)
-        for t in range(8):
-            shade_tile(z, t, fy, fx, k, rate, right)
+        first = jnp.where(sub == 0, halo_row_ref[pl.ds(z, 1), :], pltpu.roll(d_ref[z, 0:8, :], 1, 0))
+        behind = jnp.concatenate([first, d_ref[z, 7:63, :]], axis=0)
+        shade(z, d_ref[z], behind, hu_ref[0:64, :], 0)
         return carry
 
-    lax.fori_loop(0, SLAB, slice_step, 0, unroll=2)
-
-    for out, out_ref in enumerate((up_ref, own_ref, down_ref)):
+    lax.fori_loop(0, SLAB, slice_step, 0, unroll=SLICE_UNROLL)
+
+    odd = edge_ref[2]
+    for start, out_ref in ((128 - 128 * odd, near_ref), (64, own_ref), (128 * odd, far_ref)):
         for half in range(2):
             for channel in range(4):
-                value = acc_ref[4 * half + channel, pl.ds(64 * out, 64), :]
+                value = acc_ref[4 * half + channel, pl.ds(pl.multiple_of(start, 64), 64), :]
                 out_ref[half, channel] = 1.0 - value if channel == 3 else value
 
 
@@ -238,34 +230,42 @@
     return [ref[(*index, c)] for c in range(4)]
 
 
-def rows_kernel(own_ref, below_ref, above_ref, mine_ref, left_ref, right_ref):
+def rows_kernel(edge_ref, own_ref, near_ref, far_ref, mine_ref, near_out_ref, far_out_ref):
     lane = lax.broadcasted_iota(jnp.int32, (1, COLS), 1)
+    odd_row, odd_col = edge_ref[2] == 1, edge_ref[3] == 1
     halves = []
     for half in range(2):
-        merged = over(channels(own_ref, half), channels(above_ref, half))
-        halves.append(over(channels(below_ref, half), merged))
+        near, far = channels(near_ref, half), channels(far_ref, half)
+        below = [jnp.where(odd_row, f, n) for n, f in zip(near, far)]
+        above = [jnp.where(odd_row, n, f) for n, f in zip(near, far)]
+        halves.append(over(below, over(channels(own_ref, half), above)))
     for c in range(4):
         low, high = halves[0][c], halves[1][c]
         low_turned, high_turned = pltpu.roll(low, 64, 1), pltpu.roll(high, 64, 1)
         mine_ref[c] = jnp.where(lane < 64, low_turned, high_turned)
-        left_ref[c] = jnp.where(lane < 64, low[:32], low_turned[32:])
-        right_ref[c] = jnp.where(lane < 64, high_turned[:32], high[32:])
-
-
-def columns_kernel(scale, mine_ref, from_right_ref, from_left_ref, zrow_ref, zcol_ref, out_ref):
+        left = jnp.where(lane < 64, low[:32], low_turned[32:])
+        right = jnp.where(lane < 64, high_turned[:32], high[32:])
+        near_out_ref[c] = jnp.where(odd_col, left, right)
+        far_out_ref[c] = jnp.where(odd_col, right, left)
+
+
+def columns_kernel(scale, edge_ref, mine_ref, near_ref, far_ref, zrow_ref, zcol_ref, fvec_ref, out_ref):
     lane = lax.broadcasted_iota(jnp.int32, (1, COLS), 1)
+    odd_col = edge_ref[3] == 1
     front, behind = [], []
     for c in range(4):
-        piece = from_right_ref[c]
+        near, far = near_ref[c], far_ref[c]
+        piece = jnp.where(odd_col, far, near)
         upper = jnp.concatenate([pltpu.roll(piece, 64, 1), piece], axis=0)
-        piece = from_left_ref[c]
+        piece = jnp.where(odd_col, near, far)
         lower = jnp.concatenate([piece, pltpu.roll(piece, 64, 1)], axis=0)
         own = mine_ref[c]
         front.append(jnp.where(lane < 64, own, upper))
         behind.append(jnp.where(lane < 64, lower, own))
     inner = over(front, behind)
+    total = jnp.sum(fvec_ref[2:3, :], axis=1, keepdims=True)
     pre = jnp.maximum(zrow_ref[:, 0:1], zcol_ref[0:1, :])
-    post = jnp.minimum(jnp.maximum(zrow_ref[:, 1:2], zcol_ref[1:2, :]), zcol_ref[2:3, :] - pre)
+    post = jnp.minimum(jnp.maximum(zrow_ref[:, 1:2], zcol_ref[1:2, :]), total - pre)
     flat = []
     for amount in (pre, jnp.maximum(post, 0.0)):
         fade = 1.0 - jnp.exp((-scale * LN2) * amount)
@@ -286,6 +286,11 @@
     out_ref[1] = merged[1]
     out_ref[2] = 0.5 * (merged[3] + merged[2])
     out_ref[3] = merged[3]
+
+
+def matching(count, first):
+    pairs = [(i, i + 1) for i in range(first, count - 1, 2)]
+    return pairs + [(j, i) for i, j in pairs]
 
 
 def body(coefficients, shifts, fraction, absorb):
@@ -309,9 +314,7 @@
     )(coefficients)
 
     row_up = [(i, i + 1) for i in range(row_count - 1)]
-    row_down = [(i + 1, i) for i in range(row_count - 1)]
     col_up = [(i, i + 1) for i in range(col_count - 1)]
-    col_down = [(i + 1, i) for i in range(col_count - 1)]
     both_up = [
         (y * col_count + x, (y + 1) * col_count + x + 1) for y in range(row_count - 1) for x in range(col_count - 1)
     ]
@@ -320,11 +323,11 @@
     corner = lax.ppermute(col_plane[56:64], ("imgy", "imgx"), both_up)
 
     shift_rows, shift_cols = shifts[0], shifts[1]
-    edge = jnp.stack([iy == row_count - 1, ix == col_count - 1]).astype(jnp.int32)
+    edge = jnp.stack([iy == row_count - 1, ix == col_count - 1, iy % 2 == 1, ix % 2 == 1]).astype(jnp.int32)
     vectors = jnp.pad(jnp.concatenate([fraction, absorb[None]], axis=0), ((0, 5), (0, COLS - SLAB)))
 
     sent = f32(2, 4, ROWS, COLS)
-    up, own, down = call(
+    near, own, far = call(
         functools.partial(shade_kernel, scale),
         (sent, sent, sent),
         [SMEM_SPEC] * 4 + [VMEM_SPEC] * 6,
@@ -337,12 +340,14 @@
         bytes_moved=4 << 20,
     )(shifts, fraction, absorb, edge, volume, halo_row, halo_col, corner, col_plane, vectors)
 
-    below = lax.ppermute(up, "imgy", row_down)
-    above = lax.ppermute(down, "imgy", row_up)
+    near = lax.ppermute(near, "imgy", matching(row_count, 0))
+    far = lax.ppermute(far, "imgy", matching(row_count, 1))
     packed = f32(4, ROWS // 2, COLS)
-    mine, left, right = call(rows_kernel, (f32(4, ROWS, COLS), packed, packed), [VMEM_SPEC] * 3)(own, below, above)
-    from_right = lax.ppermute(left, "imgx", col_down)
-    from_left = lax.ppermute(right, "imgx", col_up)
+    mine, near, far = call(rows_kernel, (f32(4, ROWS, COLS), packed, packed), [SMEM_SPEC] + [VMEM_SPEC] * 3)(
+        edge, own, near, far
+    )
+    near = lax.ppermute(near, "imgx", matching(col_count, 0))
+    far = lax.ppermute(far, "imgx", matching(col_count, 1))
 
     image_rows = iy * ROWS + jnp.arange(ROWS, dtype=jnp.int32)
     image_cols = ix * COLS + jnp.arange(COLS, dtype=jnp.int32)
@@ -354,14 +359,12 @@
         return pre, post
 
     zrow = jnp.stack(outside(image_rows, shift_rows, ROWS * row_count), axis=1)
-    zcol = jnp.stack(
-        [*outside(image_cols, shift_cols, COLS * col_count), jnp.broadcast_to(jnp.sum(absorb), (COLS,))], axis=0
-    )
+    zcol = jnp.stack(outside(image_cols, shift_cols, COLS * col_count), axis=0)
     pieces = call(
         functools.partial(columns_kernel, scale),
         f32(depth_count, 4, ROWS // depth_count, COLS),
-        [VMEM_SPEC] * 5,
-    )(mine, from_right, from_left, zrow, zcol)
+        [SMEM_SPEC] + [VMEM_SPEC] * 6,
+    )(edge, mine, near, far, zrow, zcol, vectors)
     incoming = lax.all_to_all(pieces, "depth", split_axis=0, concat_axis=0, tiled=True)
     image = call(fold_kernel, f32(4, ROWS // depth_count, COLS), [VMEM_SPEC])(incoming)
     return image[:, None]

time: 69.2 us -> 53.9 us (0.78)
  the two profiles are of different devices: /device:TPU:20 before, /device:TPU:18 now
where the time goes in v3:
time: 53.9 us; the launch traced here: 53.7 us
  blocking collectives  17.3 us (32%)
  starting transfers between devices  16.3 us (30%)
  waiting for transfers between devices  9.19 us (17%)
  Pallas kernels  8.59 us (16%)
  local copies, waits for them, and re-layouts  1.71 us (3%)
    all_to_all x1, blocking collectives, body(): lax.all_to_all(pieces, 'depth', split_axis=0, concat_axis=0, tiled=True)  17.3 us
    pallas_call x1, Pallas kernels, body(): call(functools.partial(shade_kernel, scale), (sent, sent, sent), [SMEM_SP...  5.06 us
    ppermute x1, waiting for transfers between devices, body(): far = lax.ppermute(far, 'imgy', matching(row_count, 1))  5.01 us
    ppermute x1, starting transfers between devices, body(): far = lax.ppermute(far, 'imgx', matching(col_count, 1))  3.58 us
    ppermute x1, starting transfers between devices, body(): halo_row = lax.ppermute(row_plane, 'imgy', row_up)  3.57 us
    ppermute x1, starting transfers between devices, body(): halo_col = lax.ppermute(col_plane, 'imgx', col_up)  3.4 us
    ppermute x1, waiting for transfers between devices, body(): far = lax.ppermute(far, 'imgx', matching(col_count, 1))  2.51 us
    ppermute x1, starting transfers between devices, body(): far = lax.ppermute(far, 'imgy', matching(row_count, 1))  2.45 us
  transfers between devices with their start and end apart: 7, of which 4 were waited for; matrix products, arithmetic and copies ran while one was open for 1% of the time, Pallas kernels for 0%

profile of v3, /device:TPU:18, one launch (start us, length us, event | category | flops | bytes accessed | tf_op | source)
XLA Modules:
  0.0 53.7 jit_solution(861801034986771801)
XLA Ops:
  0.0 0.0 copy-start
  0.0 1.6 %copy-done = f32[64,64,128]{2,1,0:T(8,128)S(1)} copy-done((f32[64,64,128]{2,1,0:T(8,128)S(1)}, f32[64,64,128]{2,1,0:T(8,128)}, u32[]{:S(2)}) %copy-start) | copy-done | bytes 2097176
  1.6 0.0 copy-start.2
  1.6 0.0 copy-start.1
  1.6 0.0 copy-start.3
  1.6 1.5 %shard_map.46 = (f32[64,64,128]{2,1,0:T(8,128)S(1)}, f32[72,128]{1,0:T(8,128)S(1)}, f32[64,128]{1,0:T(8,128)S(1)}) custom-call(f32[64,64,128]{2,1,0:T(8,128)S(1)} %copy-done), custom_call_target="tpu_custom_call" | custom-call | flops 300000000 | bytes 4194304 | tf_op jit(solution)/shard_map/pallas_call | solution.py:303
  3.1 3.4 %collective-permute-start.1 = (f32[64,128]{1,0:T(8,128)S(1)}, f32[64,128]{1,0:T(8,128)S(1)}, u32[]{:S(2)}, u32[]{:S(2)}) collective-permute-start(f32[64,128]{1,0:T(8,128)S(1)} %get-tuple-element.16.last_ref), channel_id=1, source_target_pairs={{0,1},{1,2},{2,3},{4,5},{5,6},{6,7},{8,9},{9,10},{10,11},{12,13},{... | collective-permute-start | bytes 98312 | tf_op jit(solution)/shard_map/ppermute | solution.py:322
  6.5 2.3 %collective-permute-start.2 = (f32[8,128]{1,0:T(8,128)S(1)}, f32[8,128]{1,0:T(8,128)S(1)}, u32[]{:S(2)}, u32[]{:S(2)}) collective-permute-start(f32[8,128]{1,0:T(8,128)S(1)} %slice.9), channel_id=1, source_target_pairs={{0,5},{1,6},{2,7},{4,9},{5,10},{6,11},{8,13},{9,14},{10,15},{12,17... | collective-permute-start | bytes 12296 | tf_op jit(solution)/shard_map/ppermute | solution.py:323
  8.8 3.6 %collective-permute-start = (f32[72,128]{1,0:T(8,128)S(1)}, f32[72,128]{1,0:T(8,128)S(1)}, u32[]{:S(2)}, u32[]{:S(2)}) collective-permute-start(f32[72,128]{1,0:T(8,128)S(1)} %get-tuple-element.15), channel_id=1, source_target_pairs={{0,4},{4,8},{8,12},{12,16},{16,20},{20,24},{24,28},{1,5},{5,9},{9,... | collective-permute-start | bytes 110600 | tf_op jit(solution)/shard_map/ppermute | solution.py:321
  12.4 0.0 copy-done.2
  12.5 0.0 copy-done.1
  12.5 0.0 copy-done.3
  12.5 0.2 select_reduce_fusion.3
  12.7 0.1 add_convert_fusion.edge_ref
  12.8 0.0 collective-permute-done.2.corner_ref
  12.8 0.0 collective-permute-done.1.halo_col_ref
  12.8 1.6 %collective-permute-done.halo_row_ref = f32[72,128]{1,0:T(8,128)S(1)} collective-permute-done((f32[72,128]{1,0:T(8,128)S(1)}, f32[72,128]{1,0:T(8,128)S(1)}, u32[]{:S(2)}, u32[]{:S(2)}) %collective-permute-start) | collective-permute-done | bytes 36896 | tf_op jit(solution)/shard_map/ppermute | solution.py:321
  14.4 5.1 %shard_map.47 = (f32[2,4,64,128]{3,2,1,0:T(8,128)S(1)}, f32[2,4,64,128]{3,2,1,0:T(8,128)S(1)}, f32[2,4,64,128]{3,2,1,0:T(8,128)S(1)}) custom-call(s32[2,64]{1,0:T(2,128)S(1)} %copy-done.2, f32[2,64]{1,0:T(2,128)S(1)} %copy-done.3, f32[64]{0:T(128)S(1)} %copy-done.1, s32[4]{0:T(128)S(1)} %add_convert_fusion.edge_ref, ...), custom_call_target="tpu_custom_call" | custom-call | flops 300000000 | bytes 4194304 | tf_op jit(solution)/shard_map/pallas_call | solution.py:330
  19.5 0.1 collective-permute-start.3
  19.6 2.4 %collective-permute-start.4 = (f32[2,4,64,128]{3,2,1,0:T(8,128)S(1)}, f32[2,4,64,128]{3,2,1,0:T(8,128)S(1)}, u32[]{:S(2)}, u32[]{:S(2)}) collective-permute-start(f32[2,4,64,128]{3,2,1,0:T(8,128)S(1)} %get-tuple-element.19), channel_id=1, source_target_pairs={{4,8},{12,16},{20,24},{8,4},{16,12},{24,20},{5,9},{13,17},{21,25},... | collective-permute-start | bytes 786440 | tf_op jit(solution)/shard_map/ppermute | solution.py:344
  22.0 0.1 copy.10.zrow_ref
  22.1 0.1 select_reduce_fusion.1
  22.2 0.0 collective-permute-done.3.near_ref
  22.2 5.0 %collective-permute-done.4.far_ref = f32[2,4,64,128]{3,2,1,0:T(8,128)S(1)} collective-permute-done((f32[2,4,64,128]{3,2,1,0:T(8,128)S(1)}, f32[2,4,64,128]{3,2,1,0:T(8,128)S(1)}, u32[]{:S(2)}, u32[]{:S(2)}) %collective-permute-start.4) | collective-permute-done | bytes 262176 | tf_op jit(solution)/shard_map/ppermute | solution.py:344
  27.2 0.7 %shard_map.48 = (f32[4,64,128]{2,1,0:T(8,128)S(1)}, f32[4,32,128]{2,1,0:T(8,128)S(1)}, f32[4,32,128]{2,1,0:T(8,128)S(1)}) custom-call(s32[4]{0:T(128)S(1)} %add_convert_fusion.edge_ref, f32[2,4,64,128]{3,2,1,0:T(8,128)S(1)} %get-tuple-element.17.own_ref, f32[2,4,64,128]{3,2,1,0:T(8,128)S(1)} %collective-permute-done.3.near_ref, ...), custom_call_target="tpu_custom_call" | custom-call | flops 1000 | bytes 1000 | tf_op jit(solution)/shard_map/pallas_call | solution.py:346
  27.9 0.9 %collective-permute-start.5 = (f32[4,32,128]{2,1,0:T(8,128)S(1)}, f32[4,32,128]{2,1,0:T(8,128)S(1)}, u32[]{:S(2)}, u32[]{:S(2)}) collective-permute-start(f32[4,32,128]{2,1,0:T(8,128)S(1)} %get-tuple-element.21), channel_id=1, source_target_pairs={{0,1},{2,3},{1,0},{3,2},{4,5},{6,7},{5,4},{7,6},{8,9},{10,11},{9,8... | collective-permute-start | bytes 196616 | tf_op jit(solution)/shard_map/ppermute | solution.py:349
  28.9 3.6 %collective-permute-start.6 = (f32[4,32,128]{2,1,0:T(8,128)S(1)}, f32[4,32,128]{2,1,0:T(8,128)S(1)}, u32[]{:S(2)}, u32[]{:S(2)}) collective-permute-start(f32[4,32,128]{2,1,0:T(8,128)S(1)} %get-tuple-element.22), channel_id=1, source_target_pairs={{1,2},{2,1},{5,6},{6,5},{9,10},{10,9},{13,14},{14,13},{17,18},{18,... | collective-permute-start | bytes 196616 | tf_op jit(solution)/shard_map/ppermute | solution.py:350
  32.5 0.1 collective-permute-done.5.near_ref
  32.5 2.5 %collective-permute-done.6.far_ref = f32[4,32,128]{2,1,0:T(8,128)S(1)} collective-permute-done((f32[4,32,128]{2,1,0:T(8,128)S(1)}, f32[4,32,128]{2,1,0:T(8,128)S(1)}, u32[]{:S(2)}, u32[]{:S(2)}) %collective-permute-start.6) | collective-permute-done | bytes 65568 | tf_op jit(solution)/shard_map/ppermute | solution.py:350
  35.0 0.7 %shard_map.49 = f32[8,4,8,128]{3,2,1,0:T(8,128)S(1)} custom-call(s32[4]{0:T(128)S(1)} %add_convert_fusion.edge_ref, f32[4,64,128]{2,1,0:T(8,128)S(1)} %get-tuple-element.20.mine_ref, f32[4,32,128]{2,1,0:T(8,128)S(1)} %collective-permute-done.5.near_ref, f32[4,32,128]{2,1,0:T(8,128)S(1)} %collective-permute-done.6.far_ref, f32[64,2]{1,0:T(8,128)S(1)} %copy.10.zrow_ref, ...), custom_call_target="tpu_custom_call" | custom-call | flops 1000 | bytes 1000 | tf_op jit(solution)/shard_map/pallas_call | solution.py:363
  35.7 17.3 %all_to_all.5.in_ref = f32[8,4,8,128]{3,2,1,0:T(8,128)S(1)} all-to-all(f32[8,4,8,128]{3,2,1,0:T(8,128)S(1)} %shard_map.49), channel_id=1, replica_groups=mesh['depth'=8,'imgy'=8,'imgx'=4] {'depth'}, dimensions={0} | all-to-all | bytes 262144 | tf_op jit(solution)/shard_map/all_to_all | solution.py:368
  53.0 0.6 %shard_map.50 = f32[4,8,128]{2,1,0:T(8,128)} custom-call(f32[8,4,8,128]{3,2,1,0:T(8,128)S(1)} %all_to_all.5.in_ref), custom_call_target="tpu_custom_call" | custom-call | flops 1000 | bytes 1000 | tf_op jit(solution)/shard_map/pallas_call | solution.py:369
  (7 shorter events, 0.0 us)
Async XLA Ops:
  0.0 1.6 %copy-start = (f32[64,64,128]{2,1,0:T(8,128)S(1)}, f32[64,64,128]{2,1,0:T(8,128)}, u32[]{:S(2)}) copy-start(f32[64,64,128]{2,1,0:T(8,128)} %c_ref.1) | copy-start | bytes 6291460
  1.6 10.9 %copy-start.2 = (s32[2,64]{1,0:T(2,128)S(1)}, s32[2,64]{1,0:T(2,128)}, u32[]{:S(2)}) copy-start(s32[2,64]{1,0:T(2,128)} %shift_ref.1) | copy-start | bytes 1540
  1.6 10.9 %copy-start.1 = (f32[64]{0:T(128)S(1)}, f32[64]{0:T(128)}, u32[]{:S(2)}) copy-start(f32[64]{0:T(128)} %absorb_ref.1) | copy-start | bytes 772
  1.6 10.9 %copy-start.3 = (f32[2,64]{1,0:T(2,128)S(1)}, f32[2,64]{1,0:T(2,128)}, u32[]{:S(2)}) copy-start(f32[2,64]{1,0:T(2,128)} %frac_ref.1) | copy-start | bytes 1540
  3.1 9.6 %collective-permute-start.1 = (f32[64,128]{1,0:T(8,128)S(1)}, f32[64,128]{1,0:T(8,128)S(1)}, u32[]{:S(2)}, u32[]{:S(2)}) collective-permute-start(f32[64,128]{1,0:T(8,128)S(1)} %get-tuple-element.16.last_ref), channel_id=1, source_target_pairs={{0,1},{1,2},{2,3},{4,5},{5,6},{6,7},{8,9},{9,10},{10,11},{12,13},{... | collective-permute-start | bytes 98312 | tf_op jit(solution)/shard_map/ppermute | solution.py:322
  6.5 6.2 %collective-permute-start.2 = (f32[8,128]{1,0:T(8,128)S(1)}, f32[8,128]{1,0:T(8,128)S(1)}, u32[]{:S(2)}, u32[]{:S(2)}) collective-permute-start(f32[8,128]{1,0:T(8,128)S(1)} %slice.9), channel_id=1, source_target_pairs={{0,5},{1,6},{2,7},{4,9},{5,10},{6,11},{8,13},{9,14},{10,15},{12,17... | collective-permute-start | bytes 12296 | tf_op jit(solution)/shard_map/ppermute | solution.py:323
  8.8 5.6 %collective-permute-start = (f32[72,128]{1,0:T(8,128)S(1)}, f32[72,128]{1,0:T(8,128)S(1)}, u32[]{:S(2)}, u32[]{:S(2)}) collective-permute-start(f32[72,128]{1,0:T(8,128)S(1)} %get-tuple-element.15), channel_id=1, source_target_pairs={{0,4},{4,8},{8,12},{12,16},{16,20},{20,24},{24,28},{1,5},{5,9},{9,... | collective-permute-start | bytes 110600 | tf_op jit(solution)/shard_map/ppermute | solution.py:321
  19.5 2.8 %collective-permute-start.3 = (f32[2,4,64,128]{3,2,1,0:T(8,128)S(1)}, f32[2,4,64,128]{3,2,1,0:T(8,128)S(1)}, u32[]{:S(2)}, u32[]{:S(2)}) collective-permute-start(f32[2,4,64,128]{3,2,1,0:T(8,128)S(1)} %get-tuple-element.18), channel_id=1, source_target_pairs={{0,4},{8,12},{16,20},{24,28},{4,0},{12,8},{20,16},{28,24},{1,5},{9... | collective-permute-start | bytes 786440 | tf_op jit(solution)/shard_map/ppermute | solution.py:343
  19.6 7.7 %collective-permute-start.4 = (f32[2,4,64,128]{3,2,1,0:T(8,128)S(1)}, f32[2,4,64,128]{3,2,1,0:T(8,128)S(1)}, u32[]{:S(2)}, u32[]{:S(2)}) collective-permute-start(f32[2,4,64,128]{3,2,1,0:T(8,128)S(1)} %get-tuple-element.19), channel_id=1, source_target_pairs={{4,8},{12,16},{20,24},{8,4},{16,12},{24,20},{5,9},{13,17},{21,25},... | collective-permute-start | bytes 786440 | tf_op jit(solution)/shard_map/ppermute | solution.py:344
  27.9 4.6 %collective-permute-start.5 = (f32[4,32,128]{2,1,0:T(8,128)S(1)}, f32[4,32,128]{2,1,0:T(8,128)S(1)}, u32[]{:S(2)}, u32[]{:S(2)}) collective-permute-start(f32[4,32,128]{2,1,0:T(8,128)S(1)} %get-tuple-element.21), channel_id=1, source_target_pairs={{0,1},{2,3},{1,0},{3,2},{4,5},{6,7},{5,4},{7,6},{8,9},{10,11},{9,8... | collective-permute-start | bytes 196616 | tf_op jit(solution)/shard_map/ppermute | solution.py:349
  28.9 6.2 %collective-permute-start.6 = (f32[4,32,128]{2,1,0:T(8,128)S(1)}, f32[4,32,128]{2,1,0:T(8,128)S(1)}, u32[]{:S(2)}, u32[]{:S(2)}) collective-permute-start(f32[4,32,128]{2,1,0:T(8,128)S(1)} %get-tuple-element.22), channel_id=1, source_target_pairs={{1,2},{2,1},{5,6},{6,5},{9,10},{10,9},{13,14},{14,13},{17,18},{18,... | collective-permute-start | bytes 196616 | tf_op jit(solution)/shard_map/ppermute | solution.py:350

commit v4 on v3

v4 whole, which is shorter than its diff:
```python
import functools
import math

import jax
import jax.numpy as jnp
from jax import lax
from jax.experimental import pallas as pl
from jax.experimental.pallas import tpu as pltpu
from jax.sharding import PartitionSpec as P

BRICK = 64
SLAB = 64
ROWS = 64
COLS = 128
EXT = 208
SLICE_UNROLL = 8
LN2 = math.log(2.0)
VMEM_SPEC = pl.BlockSpec(memory_space=pltpu.VMEM)
SMEM_SPEC = pl.BlockSpec(memory_space=pltpu.SMEM)
INTERPRET = False


def call(kernel, out_shape, in_specs, scratch=(), flops=1000, bytes_moved=1000):
    specs = jax.tree.map(lambda _: VMEM_SPEC, out_shape)
    return pl.pallas_call(
        kernel,
        out_shape=out_shape,
        in_specs=in_specs,
        out_specs=specs,
        scratch_shapes=list(scratch),
        interpret=INTERPRET,
        compiler_params=pltpu.CompilerParams(vmem_limit_bytes=24 << 20),
        cost_estimate=pl.CostEstimate(flops=flops, bytes_accessed=bytes_moved, transcendentals=0),
    )


def f32(*shape):
    return jax.ShapeDtypeStruct(shape, jnp.float32)


def lane_table(half):
    source = lax.broadcasted_iota(jnp.int32, (2 * COLS, COLS), 0) % COLS
    target = lax.broadcasted_iota(jnp.int32, (2 * COLS, COLS), 1)
    local = target % BRICK
    start = target - local
    pair = local // 2
    weight = jnp.where(local % 2 == 1, 0.5, -0.5)
    inside = local < 2 * half
    low = jnp.where(inside & (source == start + pair), 1.0, 0.0)
    high = jnp.where(inside & (source == start + half + pair), weight, 0.0)
    return (low + high).astype(jnp.bfloat16)


def lane_lift(block, table):
    coarse = block.astype(jnp.bfloat16)
    rest = (block - coarse.astype(jnp.float32)).astype(jnp.bfloat16)
    both = jnp.concatenate([coarse, rest], axis=1)
    return jnp.dot(both, table, preferred_element_type=jnp.float32)


def softplus(sheared):
    return jnp.maximum(sheared, 0.0) + jnp.log(1.0 + jnp.exp(-jnp.abs(sheared)))


def tint(sheared):
    return jnp.tanh(0.75 * sheared), jnp.exp(-0.5 * (sheared * sheared)), jnp.tanh(0.4 - 0.5 * sheared)


def absorb_sample(view, half, tints, keep):
    through = view[4 * half + 3]
    after = through * keep
    weight = through - after
    view[4 * half + 3] = after
    for channel in range(3):
        view[4 * half + channel] = view[4 * half + channel] + weight * tints[channel]


def tile_kernel(
    scale, shift_ref, frac_ref, absorb_ref, edge_ref, c_ref, near_ref, own_ref, far_ref, rows_ref, cols_ref,
    s2_ref, s1_ref, d_ref, plane_ref, acc_ref,
):
    lane = lax.broadcasted_iota(jnp.int32, (1, COLS), 1)
    sub = lax.broadcasted_iota(jnp.int32, (8, COLS), 0)

    def level(half, below, out_ref, on_result, init, unroll):
        table = lane_table(half)

        def step(i, carry):
            if below is None:
                low = c_ref[i, : 2 * half, :]
            else:
                corner = jnp.where(lane % BRICK < half, below[i], c_ref[i, :half, :])
                low = jnp.concatenate([corner, c_ref[i, half : 2 * half, :]], axis=0)
            high = c_ref[i + half, : 2 * half, :]
            planes = []
            even = low - 0.5 * high
            for part in (even, even + high):
                row_even = part[:half] - 0.5 * part[half:]
                planes += [row_even, row_even + part[half:]]
            result = lane_lift(jnp.concatenate(planes, axis=0), table)
            for odd in range(2):
                for row_odd in range(2):
                    start = (2 * odd + row_odd) * half
                    out_ref[2 * i + odd, pl.ds(row_odd, half, stride=2), :] = result[start : start + half]
            return on_result(i, result, carry)

        return lax.fori_loop(0, half, step, init, unroll=unroll)

    def ignore(i, result, carry):
        return carry

    def boundary(i, result, plane):
        for odd in range(2):
            z = 2 * i + odd
            piece = result[64 * odd : 64 * odd + 64]
            rows_ref[pl.ds(z, 1), :] = piece[63:64]
            rows_ref[pl.ds(64 + z, 1), :] = piece[0:1]
            plane = jnp.where(lane == z, pltpu.roll(piece, z + 1, 1), plane)
            plane = jnp.where(lane == z + 64, pltpu.roll(piece, z + 64, 1), plane)
        return plane

    level(8, None, s2_ref, ignore, 0, 8)
    level(16, s2_ref, s1_ref, ignore, 0, 16)
    plane_ref[...] = level(32, s1_ref, d_ref, boundary, jnp.zeros((64, COLS), jnp.float32), 16)
    for row_odd in range(2):
        cols_ref[pl.ds(row_odd, 32, stride=2), :] = plane_ref[pl.ds(32 * row_odd, 32), :]

    for index in range(8):
        acc_ref[index] = jnp.full((EXT, COLS), 1.0 if index % 4 == 3 else 0.0, jnp.float32)

    def slice_step(z, carry):
        k = shift_ref[1, z] + 64
        here = d_ref[z]
        behind = jnp.concatenate([pltpu.roll(d_ref[z, 0:8, :], 1, 0), d_ref[z, 7:63, :]], axis=0)
        mixed = here + frac_ref[0, z] * (behind - here)
        left = pltpu.roll(mixed, 1, 1)
        sheared = pltpu.roll(mixed + frac_ref[1, z] * (left - mixed), k, 1)
        tints = tint(sheared)
        keep = jnp.exp((-absorb_ref[z] * scale) * softplus(sheared))
        keep = jnp.concatenate([jnp.where(sub == 0, 1.0, keep[0:8]), keep[8:]], axis=0)
        view = acc_ref.at[:, pl.ds(shift_ref[0, z] + 64, 64), :]
        absorb_sample(view, 0, tints, jnp.where(lane > k, keep, 1.0))
        absorb_sample(view, 1, tints, jnp.where(lane < k, keep, 1.0))
        return carry

    lax.fori_loop(0, SLAB, slice_step, 0, unroll=SLICE_UNROLL)

    odd = edge_ref[0]
    for start, out_ref in ((128 - 128 * odd, near_ref), (64, own_ref), (128 * odd, far_ref)):
        for half in range(2):
            for channel in range(4):
                value = acc_ref[4 * half + channel, pl.ds(pl.multiple_of(start, 64), 64), :]
                value = 1.0 - value if channel == 3 else value
                out_ref[pl.ds(64 * (4 * half + channel), 64), :] = value
    near_ref[pl.ds(512, 64), :] = rows_ref[pl.ds(pl.multiple_of(64 * odd, 64), 64), :]
    far_ref[pl.ds(512, 64), :] = rows_ref[pl.ds(pl.multiple_of(64 - 64 * odd, 64), 64), :]
    near_ref[pl.ds(576, 64), :] = cols_ref[...]
    far_ref[pl.ds(576, 64), :] = cols_ref[...]


def over(front, behind):
    through = 1.0 - front[3]
    return [front[c] + through * behind[c] for c in range(4)]


def channels(ref, *index):
    return [ref[(*index, c)] for c in range(4)]


def turn_rows(plane, amounts):
    sub = lax.broadcasted_iota(jnp.int32, (8, COLS), 0)
    tiles = []
    for t in range(plane.shape[0] // 8):
        tile = plane[8 * t : 8 * t + 8]
        turned = pltpu.roll(tile, amounts(8 * t), 1)
        for r in range(1, 8):
            turned = jnp.where(sub == r, pltpu.roll(tile, amounts(8 * t + r), 1), turned)
        tiles.append(turned)
    return jnp.concatenate(tiles, axis=0)


def exact_dot(a, b):
    return jnp.dot(a, b, precision=lax.Precision.HIGHEST, preferred_element_type=jnp.float32)


def line_composite(sheared, opticals, key_row, key_col):
    first = lax.broadcasted_iota(jnp.int32, (SLAB, SLAB), 0)
    second = lax.broadcasted_iota(jnp.int32, (SLAB, SLAB), 1)
    ahead = jnp.where((second < first) & (key_row == key_col), 1.0, 0.0)
    target = lax.broadcasted_iota(jnp.int32, (2 * SLAB, SLAB), 0).astype(jnp.float32)
    chosen = jnp.where(target == key_row + 64.0, 1.0, 0.0)
    before = exact_dot(ahead, jnp.concatenate(opticals, axis=1))
    tints = tint(sheared)
    pieces = []
    for half, optical in enumerate(opticals):
        front = before[:, COLS * half : COLS * half + COLS]
        weight = jnp.exp(-front) - jnp.exp(-(front + optical))
        pieces += [weight * tints[0], weight * tints[1], weight * tints[2], weight]
    total = exact_dot(chosen, jnp.concatenate(pieces, axis=1))
    return [total[:, COLS * p : COLS * p + COLS] for p in range(len(pieces))]


def rows_kernel(
    scale, shift_ref, edge_ref, own_ref, near_ref, far_ref, rows_ref, cols_ref, fvec_ref, fcol_ref,
    mine_ref, near_out_ref, far_out_ref, u_ref,
):
    lane = lax.broadcasted_iota(jnp.int32, (1, COLS), 1)
    odd_row, odd_col = edge_ref[0] == 1, edge_ref[1] == 1
    fy, fx, rate = fcol_ref[:, 0:1], fcol_ref[:, 1:2], fcol_ref[:, 2:3] * scale
    oy, ox = fcol_ref[:, 3:4], fcol_ref[:, 4:5]

    def received(start, size):
        near, far = near_ref[pl.ds(start, size), :], far_ref[pl.ds(start, size), :]
        return jnp.where(odd_row, far, near), jnp.where(odd_row, near, far)

    below_row, above_row = received(512, 64)
    here = jnp.where(oy < 0.0, below_row, rows_ref[pl.ds(64, 64), :])
    behind = jnp.where(oy < 0.0, rows_ref[pl.ds(0, 64), :], above_row)
    mixed = here + fy * (behind - here)
    sheared = mixed + fx * (pltpu.roll(mixed, 1, 1) - mixed)
    sheared = turn_rows(sheared, lambda z: shift_ref[1, z] + 64)
    optical = rate * softplus(sheared)
    place = lane.astype(jnp.float32)
    opticals = [jnp.where(place > ox + 64.0, optical, 0.0), jnp.where(place < ox + 64.0, optical, 0.0)]
    line = line_composite(sheared, opticals, fvec_ref[3:4, 0:SLAB], oy)

    halves = []
    for half in range(2):
        pairs = [received(64 * (4 * half + c), 64) for c in range(4)]
        own = [own_ref[pl.ds(64 * (4 * half + c), 64), :] for c in range(4)]
        lower = [line[4 * half + c][:64] for c in range(4)]
        upper = [line[4 * half + c][64:] for c in range(4)]
        merged = over(own, over(upper, [above for _, above in pairs]))
        halves.append(over([below for below, _ in pairs], over(lower, merged)))
    for c in range(4):
        low, high = halves[0][c], halves[1][c]
        low_turned, high_turned = pltpu.roll(low, 64, 1), pltpu.roll(high, 64, 1)
        mine_ref[c] = jnp.where(lane < 64, low_turned, high_turned)
        left = jnp.where(lane < 64, low[:32], low_turned[32:])
        right = jnp.where(lane < 64, high_turned[:32], high[32:])
        near_out_ref[pl.ds(32 * c, 32), :] = jnp.where(odd_col, left, right)
        far_out_ref[pl.ds(32 * c, 32), :] = jnp.where(odd_col, right, left)

    below_col, above_col = received(576, 64)
    negative = jnp.concatenate([fvec_ref[3:4, 0:SLAB]] * 2, axis=1) < 0.0
    pair = jnp.concatenate(
        [jnp.where(negative, cols_ref[...], above_col), jnp.where(negative, below_col, cols_ref[...])], axis=0
    )

    def amount(z):
        offset = shift_ref[0, z % SLAB]
        return jnp.where(offset < 0, offset + COLS, offset + 64)

    here = turn_rows(jnp.transpose(pair), amount)
    columns = here + jnp.concatenate([fy, fy], axis=0) * (pltpu.roll(here, 1, 1) - here)
    u_ref[...] = columns
    near_out_ref[pl.ds(128, 64), :] = jnp.where(odd_col, columns[64:], columns[:64])
    far_out_ref[pl.ds(128, 64), :] = jnp.where(odd_col, columns[:64], columns[64:])


def columns_kernel(scale, limit, edge_ref, mine_ref, near_ref, far_ref, u_ref, zrow_ref, zcol_ref, fvec_ref, fcol_ref, out_ref):
    lane = lax.broadcasted_iota(jnp.int32, (1, COLS), 1)
    odd_col = edge_ref[1] == 1
    fx, rate, oy, ox = fcol_ref[:, 1:2], fcol_ref[:, 2:3] * scale, fcol_ref[:, 3:4], fcol_ref[:, 4:5]

    def received(start, size):
        near, far = near_ref[pl.ds(start, size), :], far_ref[pl.ds(start, size), :]
        return jnp.where(odd_col, far, near), jnp.where(odd_col, near, far)

    right_first, left_last = received(128, 64)
    here = jnp.where(ox < 0.0, right_first, u_ref[pl.ds(64, 64), :])
    behind = jnp.where(ox < 0.0, u_ref[pl.ds(0, 64), :], left_last)
    sheared = here + fx * (behind - here)
    row = (lane + edge_ref[2]).astype(jnp.float32) - oy
    optical = jnp.where((row >= 0.0) & (row <= limit), rate * softplus(sheared), 0.0)
    line = line_composite(sheared, [optical], fvec_ref[4:5, 0:SLAB], ox)
    line = [pltpu.roll(jnp.transpose(part)[:64], 64, 1) for part in line]

    front, behind = [], []
    for c in range(4):
        right, left = received(32 * c, 32)
        upper = jnp.concatenate([pltpu.roll(right, 64, 1), right], axis=0)
        lower = jnp.concatenate([left, pltpu.roll(left, 64, 1)], axis=0)
        own = mine_ref[c]
        front.append(jnp.where(lane < 64, own, upper))
        behind.append(jnp.where(lane < 64, lower, own))
    inner = over(front, over(line, behind))
    total = jnp.sum(fvec_ref[2:3, :], axis=1, keepdims=True)
    pre = jnp.maximum(zrow_ref[:, 0:1], zcol_ref[0:1, :])
    post = jnp.minimum(jnp.maximum(zrow_ref[:, 1:2], zcol_ref[1:2, :]), total - pre)
    flat = []
    for amount in (pre, jnp.maximum(post, 0.0)):
        fade = 1.0 - jnp.exp((-scale * LN2) * amount)
        flat.append([jnp.zeros_like(fade), fade, math.tanh(0.4) * fade, fade])
    whole = over(flat[0], over(inner, flat[1]))
    pieces = out_ref.shape[0]
    height = ROWS // pieces
    for p in range(pieces):
        for c in range(4):
            out_ref[p, c] = whole[c][p * height : (p + 1) * height]


def fold_kernel(in_ref, out_ref):
    merged = channels(in_ref, 0)
    for slab in range(1, in_ref.shape[0]):
        merged = over(merged, channels(in_ref, slab))
    out_ref[0] = 0.5 * (merged[3] + merged[0])
    out_ref[1] = merged[1]
    out_ref[2] = 0.5 * (merged[3] + merged[2])
    out_ref[3] = merged[3]


def matching(count, first):
    pairs = [(i, i + 1) for i in range(first, count - 1, 2)]
    return pairs + [(j, i) for i, j in pairs]


def body(coefficients, shifts, fraction, absorb):
    depth_count = lax.axis_size("depth")
    row_count = lax.axis_size("imgy")
    col_count = lax.axis_size("imgx")
    scale = 2.0 / (SLAB * depth_count)
    iy, ix = lax.axis_index("imgy"), lax.axis_index("imgx")

    shift_rows, shift_cols = shifts[0], shifts[1]
    edge = jnp.stack([iy % 2, ix % 2, iy * ROWS]).astype(jnp.int32)
    lines = jnp.concatenate([fraction, absorb[None], shifts.astype(jnp.float32)], axis=0)
    vectors = jnp.pad(lines, ((0, 3), (0, COLS - SLAB)))
    columns = jnp.pad(lines.T, ((0, 0), (0, 3)))

    sent = f32(640, COLS)
    near, own, far, row_planes, col_planes = call(
        functools.partial(tile_kernel, scale),
        (sent, f32(512, COLS), sent, f32(128, COLS), f32(64, COLS)),
        [SMEM_SPEC] * 4 + [VMEM_SPEC],
        [
            pltpu.VMEM((16, 16, COLS), jnp.float32),
            pltpu.VMEM((32, 32, COLS), jnp.float32),
            pltpu.VMEM((64, 64, COLS), jnp.float32),
            pltpu.VMEM((64, COLS), jnp.float32),
            pltpu.VMEM((8, EXT, COLS), jnp.float32),
        ],
        flops=300_000_000,
        bytes_moved=4 << 20,
    )(shifts, fraction, absorb, edge, coefficients)

    near = lax.ppermute(near, "imgy", matching(row_count, 0))
    far = lax.ppermute(far, "imgy", matching(row_count, 1))
    packed = f32(192, COLS)
    mine, near, far, sheared_cols = call(
        functools.partial(rows_kernel, scale),
        (f32(4, ROWS, COLS), packed, packed, f32(128, COLS)),
        [SMEM_SPEC] * 2 + [VMEM_SPEC] * 7,
    )(shifts, edge, own, near, far, row_planes, col_planes, vectors, columns)
    near = lax.ppermute(near, "imgx", matching(col_count, 0))
    far = lax.ppermute(far, "imgx", matching(col_count, 1))

    image_rows = iy * ROWS + jnp.arange(ROWS, dtype=jnp.int32)
    image_cols = ix * COLS + jnp.arange(COLS, dtype=jnp.int32)

    def outside(pixels, offsets, limit):
        position = pixels[:, None] - offsets[None, :]
        pre = jnp.sum(jnp.where(position > limit, absorb[None, :], 0.0), axis=1)
        post = jnp.sum(jnp.where(position < 0, absorb[None, :], 0.0), axis=1)
        return pre, post

    zrow = jnp.stack(outside(image_rows, shift_rows, ROWS * row_count), axis=1)
    zcol = jnp.stack(outside(image_cols, shift_cols, COLS * col_count), axis=0)
    pieces = call(
        functools.partial(columns_kernel, scale, float(ROWS * row_count)),
        f32(depth_count, 4, ROWS // depth_count, COLS),
        [SMEM_SPEC] + [VMEM_SPEC] * 8,
    )(edge, mine, near, far, sheared_cols, zrow, zcol, vectors, columns)
    incoming = lax.all_to_all(pieces, "depth", split_axis=0, concat_axis=0, tiled=True)
    image = call(fold_kernel, f32(4, ROWS // depth_count, COLS), [VMEM_SPEC])(incoming)
    return image[:, None]


def solution(mesh):
    in_specs = (P("depth", "imgy", "imgx"), P(None, "depth"), P(None, "depth"), P("depth"))
    out_specs = P(None, "imgy", "depth", "imgx")
    return jax.shard_map(body, mesh=mesh, in_specs=in_specs, out_specs=out_specs, check_vma=False)
```

time: 53.9 us -> 48.4 us (0.90)
  the two profiles are of different devices: /device:TPU:18 before, /device:TPU:20 now
where the time goes in v4:
time: 48.4 us; the launch traced here: 48.2 us
  blocking collectives  17.3 us (36%)
  Pallas kernels  10.6 us (22%)
  waiting for transfers between devices  10.2 us (21%)
  starting transfers between devices  5.73 us (12%)
  local copies, waits for them, and re-layouts  3.82 us (8%)
    all_to_all x1, blocking collectives, body(): lax.all_to_all(pieces, 'depth', split_axis=0, concat_axis=0, tiled=True)  17.3 us
    pallas_call x1, Pallas kernels, body(): call(functools.partial(tile_kernel, scale), (sent, f32(512, COLS), sent,...  6.8 us
    ppermute x1, waiting for transfers between devices, body(): far = lax.ppermute(far, 'imgy', matching(row_count, 1))  5.36 us
    unnamed x12, local copies, waits for them, and re-layouts  3.61 us
    ppermute x1, waiting for transfers between devices, body(): far = lax.ppermute(far, 'imgx', matching(col_count, 1))  2.8 us
    ppermute x1, starting transfers between devices, body(): far = lax.ppermute(far, 'imgy', matching(row_count, 1))  2.45 us
    ppermute x1, waiting for transfers between devices, body(): near = lax.ppermute(near, 'imgx', matching(col_count, 0))  2.06 us
    ppermute x1, starting transfers between devices, body(): far = lax.ppermute(far, 'imgx', matching(col_count, 1))  1.91 us
  transfers between devices with their start and end apart: 4, of which 3 were waited for; matrix products, arithmetic and copies ran while one was open for 1% of the time, Pallas kernels for 0%

profile of v4, /device:TPU:20, one launch (start us, length us, event | category | flops | bytes accessed | tf_op | source)
XLA Modules:
  0.0 48.2 jit_solution(7952111685210696458)
XLA Ops:
  0.0 0.0 copy-start.2
  0.0 0.0 copy-start.4
  0.0 0.1 pad_add_fusion.edge_ref
  0.1 0.0 copy-start
  0.1 1.6 %copy-done = f32[64,64,128]{2,1,0:T(8,128)S(1)} copy-done((f32[64,64,128]{2,1,0:T(8,128)S(1)}, f32[64,64,128]{2,1,0:T(8,128)}, u32[]{:S(2)}) %copy-start) | copy-done | bytes 2097176
  1.7 0.0 copy-start.1
  1.7 0.7 %copy-done.1 = s32[2,64]{1,0:T(2,128)S(1)} copy-done((s32[2,64]{1,0:T(2,128)S(1)}, s32[2,64]{1,0:T(2,128)}, u32[]{:S(2)}) %copy-start.1) | copy-done | bytes 536
  2.4 0.0 copy-start.3
  2.4 0.7 %copy-done.3 = f32[64]{0:T(128)S(1)} copy-done((f32[64]{0:T(128)S(1)}, f32[64]{0:T(128)}, u32[]{:S(2)}) %copy-start.3) | copy-done | bytes 280
  3.0 0.0 copy-start.5
  3.0 0.7 %copy-done.5 = f32[2,64]{1,0:T(2,128)S(1)} copy-done((f32[2,64]{1,0:T(2,128)S(1)}, f32[2,64]{1,0:T(2,128)}, u32[]{:S(2)}) %copy-start.5) | copy-done | bytes 536
  3.7 6.8 %shard_map.46 = (f32[640,128]{1,0:T(8,128)S(1)}, f32[512,128]{1,0:T(8,128)S(1)}, f32[640,128]{1,0:T(8,128)S(1)}, f32[128,128]{1,0:T(8,128)S(1)}, f32[64,128]{1,0:T(8,128)S(1)}) custom-call(s32[2,64]{1,0:T(2,128)S(1)} %copy-done.1, f32[2,64]{1,0:T(2,128)S(1)} %copy-done.5, f32[64]{0:T(128)S(1)} %copy-done.3, s32[3]{0:T(128)S(1)} %pad_add_fusion.edge_ref, ...), custom_call_target="tpu_custom_call" | custom-call | flops 300000000 | bytes 4194304 | tf_op jit(solution)/shard_map/pallas_call | solution.py:332
  10.5 0.1 collective-permute-start
  10.6 2.4 %collective-permute-start.1 = (f32[640,128]{1,0:T(8,128)S(1)}, f32[640,128]{1,0:T(8,128)S(1)}, u32[]{:S(2)}, u32[]{:S(2)}) collective-permute-start(f32[640,128]{1,0:T(8,128)S(1)} %get-tuple-element.16), channel_id=1, source_target_pairs={{4,8},{12,16},{20,24},{8,4},{16,12},{24,20},{5,9},{13,17},{21,25},... | collective-permute-start | bytes 983048 | tf_op jit(solution)/shard_map/ppermute | solution.py:348
  13.1 0.1 copy.16
  13.2 0.0 copy-done.4
  13.2 0.2 select_reduce_fusion.3
  13.4 0.1 copy.17.zrow_ref
  13.5 0.1 select_reduce_fusion.1
  13.6 0.0 collective-permute-done.near_ref
  13.6 5.4 %collective-permute-done.1.far_ref = f32[640,128]{1,0:T(8,128)S(1)} collective-permute-done((f32[640,128]{1,0:T(8,128)S(1)}, f32[640,128]{1,0:T(8,128)S(1)}, u32[]{:S(2)}, u32[]{:S(2)}) %collective-permute-start.1) | collective-permute-done | bytes 327712 | tf_op jit(solution)/shard_map/ppermute | solution.py:348
  19.0 0.0 copy-done.2
  19.0 1.8 %shard_map.47 = (f32[4,64,128]{2,1,0:T(8,128)S(1)}, f32[192,128]{1,0:T(8,128)S(1)}, f32[192,128]{1,0:T(8,128)S(1)}, f32[128,128]{1,0:T(8,128)S(1)}) custom-call(s32[2,64]{1,0:T(2,128)S(1)} %copy-done.2, s32[3]{0:T(128)S(1)} %pad_add_fusion.edge_ref, f32[512,128]{1,0:T(8,128)S(1)} %get-tuple-element.14.own_ref, f32[640,128]{1,0:T(8,128)S(1)} %collective-permute-done.near_ref, ...), custom_call_target="tpu_custom_call" | custom-call | flops 1000 | bytes 1000 | tf_op jit(solution)/shard_map/pallas_call | solution.py:350
  20.8 1.3 %collective-permute-start.2 = (f32[192,128]{1,0:T(8,128)S(1)}, f32[192,128]{1,0:T(8,128)S(1)}, u32[]{:S(2)}, u32[]{:S(2)}) collective-permute-start(f32[192,128]{1,0:T(8,128)S(1)} %get-tuple-element.20), channel_id=1, source_target_pairs={{0,1},{2,3},{1,0},{3,2},{4,5},{6,7},{5,4},{7,6},{8,9},{10,11},{9,8... | collective-permute-start | bytes 294920 | tf_op jit(solution)/shard_map/ppermute | solution.py:355
  22.1 1.9 %collective-permute-start.3 = (f32[192,128]{1,0:T(8,128)S(1)}, f32[192,128]{1,0:T(8,128)S(1)}, u32[]{:S(2)}, u32[]{:S(2)}) collective-permute-start(f32[192,128]{1,0:T(8,128)S(1)} %get-tuple-element.21), channel_id=1, source_target_pairs={{1,2},{2,1},{5,6},{6,5},{9,10},{10,9},{13,14},{14,13},{17,18},{18,... | collective-permute-start | bytes 294920 | tf_op jit(solution)/shard_map/ppermute | solution.py:356
  24.0 2.1 %collective-permute-done.2.near_ref = f32[192,128]{1,0:T(8,128)S(1)} collective-permute-done((f32[192,128]{1,0:T(8,128)S(1)}, f32[192,128]{1,0:T(8,128)S(1)}, u32[]{:S(2)}, u32[]{:S(2)}) %collective-permute-start.2) | collective-permute-done | bytes 98336 | tf_op jit(solution)/shard_map/ppermute | solution.py:355
  26.0 2.8 %collective-permute-done.3.far_ref = f32[192,128]{1,0:T(8,128)S(1)} collective-permute-done((f32[192,128]{1,0:T(8,128)S(1)}, f32[192,128]{1,0:T(8,128)S(1)}, u32[]{:S(2)}, u32[]{:S(2)}) %collective-permute-start.3) | collective-permute-done | bytes 98336 | tf_op jit(solution)/shard_map/ppermute | solution.py:356
  28.8 1.4 %shard_map.48 = f32[8,4,8,128]{3,2,1,0:T(8,128)S(1)} custom-call(s32[3]{0:T(128)S(1)} %pad_add_fusion.edge_ref, f32[4,64,128]{2,1,0:T(8,128)S(1)} %get-tuple-element.19.mine_ref, f32[192,128]{1,0:T(8,128)S(1)} %collective-permute-done.2.near_ref, f32[192,128]{1,0:T(8,128)S(1)} %collective-permute-done.3.far_ref, f32[128,128]{1,0:T(8,128)S(1)} %get-tuple-element.22.u_ref, ...), custom_call_target="tpu_custom_call" | custom-call | flops 1000 | bytes 1000 | tf_op jit(solution)/shard_map/pallas_call | solution.py:369
  30.2 17.3 %all_to_all.5.in_ref = f32[8,4,8,128]{3,2,1,0:T(8,128)S(1)} all-to-all(f32[8,4,8,128]{3,2,1,0:T(8,128)S(1)} %shard_map.48), channel_id=1, replica_groups=mesh['depth'=8,'imgy'=8,'imgx'=4] {'depth'}, dimensions={0} | all-to-all | bytes 262144 | tf_op jit(solution)/shard_map/all_to_all | solution.py:374
  47.6 0.6 %shard_map.49 = f32[4,8,128]{2,1,0:T(8,128)} custom-call(f32[8,4,8,128]{3,2,1,0:T(8,128)S(1)} %all_to_all.5.in_ref), custom_call_target="tpu_custom_call" | custom-call | flops 1000 | bytes 1000 | tf_op jit(solution)/shard_map/pallas_call | solution.py:375
  (9 shorter events, 0.1 us)
Async XLA Ops:
  0.0 19.0 %copy-start.2 = (s32[2,64]{1,0:T(2,128)S(1)}, s32[2,64]{1,0:T(2,128)}, u32[]{:S(2)}) copy-start(s32[2,64]{1,0:T(2,128)} %shift_ref.3) | copy-start | bytes 1540
  0.0 13.2 %copy-start.4 = (f32[64]{0:T(128)S(1)}, f32[64]{0:T(128)}, u32[]{:S(2)}) copy-start(f32[64]{0:T(128)} %absorb_ref.1) | copy-start | bytes 772
  0.1 1.6 %copy-start = (f32[64,64,128]{2,1,0:T(8,128)S(1)}, f32[64,64,128]{2,1,0:T(8,128)}, u32[]{:S(2)}) copy-start(f32[64,64,128]{2,1,0:T(8,128)} %c_ref.1) | copy-start | bytes 6291460
  1.7 0.7 %copy-start.1 = (s32[2,64]{1,0:T(2,128)S(1)}, s32[2,64]{1,0:T(2,128)}, u32[]{:S(2)}) copy-start(s32[2,64]{1,0:T(2,128)} %shift_ref.3) | copy-start | bytes 1540
  2.4 0.7 %copy-start.3 = (f32[64]{0:T(128)S(1)}, f32[64]{0:T(128)}, u32[]{:S(2)}) copy-start(f32[64]{0:T(128)} %absorb_ref.1) | copy-start | bytes 772
  3.0 0.7 %copy-start.5 = (f32[2,64]{1,0:T(2,128)S(1)}, f32[2,64]{1,0:T(2,128)}, u32[]{:S(2)}) copy-start(f32[2,64]{1,0:T(2,128)} %frac_ref.1) | copy-start | bytes 1540
  10.5 3.1 %collective-permute-start = (f32[640,128]{1,0:T(8,128)S(1)}, f32[640,128]{1,0:T(8,128)S(1)}, u32[]{:S(2)}, u32[]{:S(2)}) collective-permute-start(f32[640,128]{1,0:T(8,128)S(1)} %get-tuple-element.15), channel_id=1, source_target_pairs={{0,4},{8,12},{16,20},{24,28},{4,0},{12,8},{20,16},{28,24},{1,5},{9... | collective-permute-start | bytes 983048 | tf_op jit(solution)/shard_map/ppermute | solution.py:347
  10.6 8.4 %collective-permute-start.1 = (f32[640,128]{1,0:T(8,128)S(1)}, f32[640,128]{1,0:T(8,128)S(1)}, u32[]{:S(2)}, u32[]{:S(2)}) collective-permute-start(f32[640,128]{1,0:T(8,128)S(1)} %get-tuple-element.16), channel_id=1, source_target_pairs={{4,8},{12,16},{20,24},{8,4},{16,12},{24,20},{5,9},{13,17},{21,25},... | collective-permute-start | bytes 983048 | tf_op jit(solution)/shard_map/ppermute | solution.py:348
  20.8 5.3 %collective-permute-start.2 = (f32[192,128]{1,0:T(8,128)S(1)}, f32[192,128]{1,0:T(8,128)S(1)}, u32[]{:S(2)}, u32[]{:S(2)}) collective-permute-start(f32[192,128]{1,0:T(8,128)S(1)} %get-tuple-element.20), channel_id=1, source_target_pairs={{0,1},{2,3},{1,0},{3,2},{4,5},{6,7},{5,4},{7,6},{8,9},{10,11},{9,8... | collective-permute-start | bytes 294920 | tf_op jit(solution)/shard_map/ppermute | solution.py:355
  22.1 6.8 %collective-permute-start.3 = (f32[192,128]{1,0:T(8,128)S(1)}, f32[192,128]{1,0:T(8,128)S(1)}, u32[]{:S(2)}, u32[]{:S(2)}) collective-permute-start(f32[192,128]{1,0:T(8,128)S(1)} %get-tuple-element.21), channel_id=1, source_target_pairs={{1,2},{2,1},{5,6},{6,5},{9,10},{10,9},{13,14},{14,13},{17,18},{18,... | collective-permute-start | bytes 294920 | tf_op jit(solution)/shard_map/ppermute | solution.py:356

commit v5 on v4

--- a/solution.py
+++ b/solution.py
@@ -17,6 +17,8 @@
 LN2 = math.log(2.0)
 VMEM_SPEC = pl.BlockSpec(memory_space=pltpu.VMEM)
 SMEM_SPEC = pl.BlockSpec(memory_space=pltpu.SMEM)
+HBM_SPEC = pl.BlockSpec(memory_space=pltpu.HBM)
+CHUNK = 16
 INTERPRET = False
 
 
@@ -76,13 +78,27 @@
 
 
 def tile_kernel(
-    scale, shift_ref, frac_ref, absorb_ref, edge_ref, c_ref, near_ref, own_ref, far_ref, rows_ref, cols_ref,
-    s2_ref, s1_ref, d_ref, plane_ref, acc_ref,
+    scale, edge_ref, shift_hbm, frac_hbm, absorb_hbm, c_hbm, near_ref, own_ref, far_ref, rows_ref, cols_ref,
+    shift_ref, frac_ref, absorb_ref, c_ref, s2_ref, s1_ref, d_ref, plane_ref, acc_ref, sems,
 ):
+    loads = [
+        pltpu.make_async_copy(c_hbm.at[pl.ds(CHUNK * i, CHUNK)], c_ref.at[pl.ds(CHUNK * i, CHUNK)], sems.at[i])
+        for i in range(SLAB // CHUNK)
+    ]
+    scalars = [
+        pltpu.make_async_copy(shift_hbm, shift_ref, sems.at[4]),
+        pltpu.make_async_copy(frac_hbm, frac_ref, sems.at[5]),
+        pltpu.make_async_copy(absorb_hbm, absorb_ref, sems.at[6]),
+    ]
+    for copy in loads + scalars:
+        copy.start()
+    for index in range(8):
+        acc_ref[index] = jnp.full((EXT, COLS), 1.0 if index % 4 == 3 else 0.0, jnp.float32)
+
     lane = lax.broadcasted_iota(jnp.int32, (1, COLS), 1)
     sub = lax.broadcasted_iota(jnp.int32, (8, COLS), 0)
 
-    def level(half, below, out_ref, on_result, init, unroll):
+    def level(half, below, out_ref, on_result, init, unroll, span=None):
         table = lane_table(half)
 
         def step(i, carry):
@@ -104,7 +120,8 @@
                     out_ref[2 * i + odd, pl.ds(row_odd, half, stride=2), :] = result[start : start + half]
             return on_result(i, result, carry)
 
-        return lax.fori_loop(0, half, step, init, unroll=unroll)
+        first, last = span or (0, half)
+        return lax.fori_loop(first, last, step, init, unroll=unroll)
 
     def ignore(i, result, carry):
         return carry
@@ -119,14 +136,19 @@
             plane = jnp.where(lane == z + 64, pltpu.roll(piece, z + 64, 1), plane)
         return plane
 
+    loads[0].wait()
     level(8, None, s2_ref, ignore, 0, 8)
+    loads[1].wait()
     level(16, s2_ref, s1_ref, ignore, 0, 16)
-    plane_ref[...] = level(32, s1_ref, d_ref, boundary, jnp.zeros((64, COLS), jnp.float32), 16)
+    loads[2].wait()
+    plane = level(32, s1_ref, d_ref, boundary, jnp.zeros((64, COLS), jnp.float32), 16, (0, 16))
+    loads[3].wait()
+    plane_ref[...] = level(32, s1_ref, d_ref, boundary, plane, 16, (16, 32))
     for row_odd in range(2):
         cols_ref[pl.ds(row_odd, 32, stride=2), :] = plane_ref[pl.ds(32 * row_odd, 32), :]
 
-    for index in range(8):
-        acc_ref[index] = jnp.full((EXT, COLS), 1.0 if index % 4 == 3 else 0.0, jnp.float32)
+    for copy in scalars:
+        copy.wait()
 
     def slice_step(z, carry):
         k = shift_ref[1, z] + 64
@@ -332,28 +354,33 @@
     near, own, far, row_planes, col_planes = call(
         functools.partial(tile_kernel, scale),
         (sent, f32(512, COLS), sent, f32(128, COLS), f32(64, COLS)),
-        [SMEM_SPEC] * 4 + [VMEM_SPEC],
+        [SMEM_SPEC] + [HBM_SPEC] * 4,
         [
+            pltpu.SMEM((2, SLAB), jnp.int32),
+            pltpu.SMEM((2, SLAB), jnp.float32),
+            pltpu.SMEM((SLAB,), jnp.float32),
+            pltpu.VMEM((SLAB, ROWS, COLS), jnp.float32),
             pltpu.VMEM((16, 16, COLS), jnp.float32),
             pltpu.VMEM((32, 32, COLS), jnp.float32),
             pltpu.VMEM((64, 64, COLS), jnp.float32),
             pltpu.VMEM((64, COLS), jnp.float32),
             pltpu.VMEM((8, EXT, COLS), jnp.float32),
+            pltpu.SemaphoreType.DMA((7,)),
         ],
         flops=300_000_000,
         bytes_moved=4 << 20,
-    )(shifts, fraction, absorb, edge, coefficients)
-
+    )(edge, *[pltpu.with_memory_space_constraint(a, pltpu.HBM) for a in (shifts, fraction, absorb, coefficients)])
+
+    far = lax.ppermute(far, "imgy", matching(row_count, 1))
     near = lax.ppermute(near, "imgy", matching(row_count, 0))
-    far = lax.ppermute(far, "imgy", matching(row_count, 1))
     packed = f32(192, COLS)
     mine, near, far, sheared_cols = call(
         functools.partial(rows_kernel, scale),
         (f32(4, ROWS, COLS), packed, packed, f32(128, COLS)),
         [SMEM_SPEC] * 2 + [VMEM_SPEC] * 7,
     )(shifts, edge, own, near, far, row_planes, col_planes, vectors, columns)
+    far = lax.ppermute(far, "imgx", matching(col_count, 1))
     near = lax.ppermute(near, "imgx", matching(col_count, 0))
-    far = lax.ppermute(far, "imgx", matching(col_count, 1))
 
     image_rows = iy * ROWS + jnp.arange(ROWS, dtype=jnp.int32)
     image_cols = ix * COLS + jnp.arange(COLS, dtype=jnp.int32)

time: 48.4 us -> 45.9 us (0.948)
  local copies, waits for them, and re-layouts: 3.82 us -> 0.22 us
  Pallas kernels: 10.6 us -> 11.7 us
    unnamed x12 -> x6, local copies, waits for them, and re-layouts: 3.61 us -> 0.01 us
    pallas_call x1, Pallas kernels: 6.8 us -> 7.94 us  [body(): call(functools.partial(tile_kernel, scale), (sent, f32(512, COLS), sent,...]
where the time goes in v5:
time: 45.9 us; the launch traced here: 45.7 us
  blocking collectives  17.3 us (38%)
  Pallas kernels  11.7 us (25%)
  waiting for transfers between devices  10.2 us (22%)
  starting transfers between devices  5.74 us (13%)
    all_to_all x1, blocking collectives, body(): lax.all_to_all(pieces, 'depth', split_axis=0, concat_axis=0, tiled=True)  17.3 us
    pallas_call x1, Pallas kernels, body(): call(functools.partial(tile_kernel, scale), (sent, f32(512, COLS), sent,...  7.94 us
    ppermute x1, waiting for transfers between devices, body(): far = lax.ppermute(far, 'imgy', matching(row_count, 1))  5.33 us
    ppermute x1, waiting for transfers between devices, body(): far = lax.ppermute(far, 'imgx', matching(col_count, 1))  2.81 us
    ppermute x1, starting transfers between devices, body(): far = lax.ppermute(far, 'imgy', matching(row_count, 1))  2.45 us
    ppermute x1, waiting for transfers between devices, body(): near = lax.ppermute(near, 'imgx', matching(col_count, 0))  2.05 us
    ppermute x1, starting transfers between devices, body(): far = lax.ppermute(far, 'imgx', matching(col_count, 1))  1.91 us
    pallas_call x1, Pallas kernels, body(): call(functools.partial(rows_kernel, scale), (f32(4, ROWS, COLS), packed,...  1.78 us
  transfers between devices with their start and end apart: 4, of which 3 were waited for; matrix products, arithmetic and copies ran while one was open for 1% of the time, Pallas kernels for 0%

profile of v5, /device:TPU:20, one launch (start us, length us, event | category | flops | bytes accessed | tf_op | source)
XLA Modules:
  0.0 45.7 jit_solution(11101256344005236496)
XLA Ops:
  0.0 0.0 copy-start
  0.0 0.0 copy-start.2
  0.0 0.0 copy-start.1
  0.0 0.1 pad_add_fusion.edge_ref
  0.1 7.9 %shard_map.46 = (f32[640,128]{1,0:T(8,128)S(1)}, f32[512,128]{1,0:T(8,128)S(1)}, f32[640,128]{1,0:T(8,128)S(1)}, f32[128,128]{1,0:T(8,128)S(1)}, f32[64,128]{1,0:T(8,128)S(1)}) custom-call(s32[3]{0:T(128)S(1)} %pad_add_fusion.edge_ref, s32[2,64]{1,0:T(2,128)} %shift_ref.1, f32[2,64]{1,0:T(2,128)} %frac_hbm.1, f32[64]{0:T(128)} %absorb_hbm.1, ...), custom_call_target="tpu_custom_call" | custom-call | flops 300000000 | bytes 4194304 | tf_op jit(solution)/shard_map/pallas_call | solution.py:354
  8.1 0.1 collective-permute-start
  8.2 2.4 %collective-permute-start.1 = (f32[640,128]{1,0:T(8,128)S(1)}, f32[640,128]{1,0:T(8,128)S(1)}, u32[]{:S(2)}, u32[]{:S(2)}) collective-permute-start(f32[640,128]{1,0:T(8,128)S(1)} %get-tuple-element.16), channel_id=1, source_target_pairs={{4,8},{12,16},{20,24},{8,4},{16,12},{24,20},{5,9},{13,17},{21,25},... | collective-permute-start | bytes 983048 | tf_op jit(solution)/shard_map/ppermute | solution.py:374
  10.6 0.0 copy-done
  10.7 0.0 copy-done.2
  10.7 0.0 copy-done.1
  10.7 0.1 copy.16
  10.8 0.2 select_reduce_fusion.3
  11.0 0.1 copy.17.zrow_ref
  11.1 0.1 select_reduce_fusion.1
  11.2 0.0 collective-permute-done.near_ref
  11.2 5.3 %collective-permute-done.1.far_ref = f32[640,128]{1,0:T(8,128)S(1)} collective-permute-done((f32[640,128]{1,0:T(8,128)S(1)}, f32[640,128]{1,0:T(8,128)S(1)}, u32[]{:S(2)}, u32[]{:S(2)}) %collective-permute-start.1) | collective-permute-done | bytes 327712 | tf_op jit(solution)/shard_map/ppermute | solution.py:374
  16.6 1.8 %shard_map.47 = (f32[4,64,128]{2,1,0:T(8,128)S(1)}, f32[192,128]{1,0:T(8,128)S(1)}, f32[192,128]{1,0:T(8,128)S(1)}, f32[128,128]{1,0:T(8,128)S(1)}) custom-call(s32[2,64]{1,0:T(2,128)S(1)} %copy-done, s32[3]{0:T(128)S(1)} %pad_add_fusion.edge_ref, f32[512,128]{1,0:T(8,128)S(1)} %get-tuple-element.14.own_ref, f32[640,128]{1,0:T(8,128)S(1)} %collective-permute-done.near_ref, ...), custom_call_target="tpu_custom_call" | custom-call | flops 1000 | bytes 1000 | tf_op jit(solution)/shard_map/pallas_call | solution.py:377
  18.3 1.3 %collective-permute-start.2 = (f32[192,128]{1,0:T(8,128)S(1)}, f32[192,128]{1,0:T(8,128)S(1)}, u32[]{:S(2)}, u32[]{:S(2)}) collective-permute-start(f32[192,128]{1,0:T(8,128)S(1)} %get-tuple-element.20), channel_id=1, source_target_pairs={{0,1},{2,3},{1,0},{3,2},{4,5},{6,7},{5,4},{7,6},{8,9},{10,11},{9,8... | collective-permute-start | bytes 294920 | tf_op jit(solution)/shard_map/ppermute | solution.py:383
  19.6 1.9 %collective-permute-start.3 = (f32[192,128]{1,0:T(8,128)S(1)}, f32[192,128]{1,0:T(8,128)S(1)}, u32[]{:S(2)}, u32[]{:S(2)}) collective-permute-start(f32[192,128]{1,0:T(8,128)S(1)} %get-tuple-element.21), channel_id=1, source_target_pairs={{1,2},{2,1},{5,6},{6,5},{9,10},{10,9},{13,14},{14,13},{17,18},{18,... | collective-permute-start | bytes 294920 | tf_op jit(solution)/shard_map/ppermute | solution.py:382
  21.6 2.0 %collective-permute-done.2.near_ref = f32[192,128]{1,0:T(8,128)S(1)} collective-permute-done((f32[192,128]{1,0:T(8,128)S(1)}, f32[192,128]{1,0:T(8,128)S(1)}, u32[]{:S(2)}, u32[]{:S(2)}) %collective-permute-start.2) | collective-permute-done | bytes 98336 | tf_op jit(solution)/shard_map/ppermute | solution.py:383
  23.6 2.8 %collective-permute-done.3.far_ref = f32[192,128]{1,0:T(8,128)S(1)} collective-permute-done((f32[192,128]{1,0:T(8,128)S(1)}, f32[192,128]{1,0:T(8,128)S(1)}, u32[]{:S(2)}, u32[]{:S(2)}) %collective-permute-start.3) | collective-permute-done | bytes 98336 | tf_op jit(solution)/shard_map/ppermute | solution.py:382
  26.4 1.4 %shard_map.48 = f32[8,4,8,128]{3,2,1,0:T(8,128)S(1)} custom-call(s32[3]{0:T(128)S(1)} %pad_add_fusion.edge_ref, f32[4,64,128]{2,1,0:T(8,128)S(1)} %get-tuple-element.19.mine_ref, f32[192,128]{1,0:T(8,128)S(1)} %collective-permute-done.2.near_ref, f32[192,128]{1,0:T(8,128)S(1)} %collective-permute-done.3.far_ref, f32[128,128]{1,0:T(8,128)S(1)} %get-tuple-element.22.u_ref, ...), custom_call_target="tpu_custom_call" | custom-call | flops 1000 | bytes 1000 | tf_op jit(solution)/shard_map/pallas_call | solution.py:396
  27.8 17.3 %all_to_all.5.in_ref = f32[8,4,8,128]{3,2,1,0:T(8,128)S(1)} all-to-all(f32[8,4,8,128]{3,2,1,0:T(8,128)S(1)} %shard_map.48), channel_id=1, replica_groups=mesh['depth'=8,'imgy'=8,'imgx'=4] {'depth'}, dimensions={0} | all-to-all | bytes 262144 | tf_op jit(solution)/shard_map/all_to_all | solution.py:401
  45.1 0.6 %shard_map.49 = f32[4,8,128]{2,1,0:T(8,128)} custom-call(f32[8,4,8,128]{3,2,1,0:T(8,128)S(1)} %all_to_all.5.in_ref), custom_call_target="tpu_custom_call" | custom-call | flops 1000 | bytes 1000 | tf_op jit(solution)/shard_map/pallas_call | solution.py:402
  (9 shorter events, 0.1 us)
Async XLA Ops:
  0.0 10.6 %copy-start = (s32[2,64]{1,0:T(2,128)S(1)}, s32[2,64]{1,0:T(2,128)}, u32[]{:S(2)}) copy-start(s32[2,64]{1,0:T(2,128)} %shift_ref.1) | copy-start | bytes 1540
  0.0 10.7 %copy-start.2 = (f32[2,64]{1,0:T(2,128)S(1)}, f32[2,64]{1,0:T(2,128)}, u32[]{:S(2)}) copy-start(f32[2,64]{1,0:T(2,128)} %frac_hbm.1) | copy-start | bytes 1540
  0.0 10.7 %copy-start.1 = (f32[64]{0:T(128)S(1)}, f32[64]{0:T(128)}, u32[]{:S(2)}) copy-start(f32[64]{0:T(128)} %absorb_hbm.1) | copy-start | bytes 772
  8.1 3.2 %collective-permute-start = (f32[640,128]{1,0:T(8,128)S(1)}, f32[640,128]{1,0:T(8,128)S(1)}, u32[]{:S(2)}, u32[]{:S(2)}) collective-permute-start(f32[640,128]{1,0:T(8,128)S(1)} %get-tuple-element.15), channel_id=1, source_target_pairs={{0,4},{8,12},{16,20},{24,28},{4,0},{12,8},{20,16},{28,24},{1,5},{9... | collective-permute-start | bytes 983048 | tf_op jit(solution)/shard_map/ppermute | solution.py:375
  8.2 8.4 %collective-permute-start.1 = (f32[640,128]{1,0:T(8,128)S(1)}, f32[640,128]{1,0:T(8,128)S(1)}, u32[]{:S(2)}, u32[]{:S(2)}) collective-permute-start(f32[640,128]{1,0:T(8,128)S(1)} %get-tuple-element.16), channel_id=1, source_target_pairs={{4,8},{12,16},{20,24},{8,4},{16,12},{24,20},{5,9},{13,17},{21,25},... | collective-permute-start | bytes 983048 | tf_op jit(solution)/shard_map/ppermute | solution.py:374
  18.3 5.3 %collective-permute-start.2 = (f32[192,128]{1,0:T(8,128)S(1)}, f32[192,128]{1,0:T(8,128)S(1)}, u32[]{:S(2)}, u32[]{:S(2)}) collective-permute-start(f32[192,128]{1,0:T(8,128)S(1)} %get-tuple-element.20), channel_id=1, source_target_pairs={{0,1},{2,3},{1,0},{3,2},{4,5},{6,7},{5,4},{7,6},{8,9},{10,11},{9,8... | collective-permute-start | bytes 294920 | tf_op jit(solution)/shard_map/ppermute | solution.py:383
  19.6 6.8 %collective-permute-start.3 = (f32[192,128]{1,0:T(8,128)S(1)}, f32[192,128]{1,0:T(8,128)S(1)}, u32[]{:S(2)}, u32[]{:S(2)}) collective-permute-start(f32[192,128]{1,0:T(8,128)S(1)} %get-tuple-element.21), channel_id=1, source_target_pairs={{1,2},{2,1},{5,6},{6,5},{9,10},{10,9},{13,14},{14,13},{17,18},{18,... | collective-permute-start | bytes 294920 | tf_op jit(solution)/shard_map/ppermute | solution.py:382

commit v6 on v5

--- a/solution.py
+++ b/solution.py
@@ -15,6 +15,7 @@
 EXT = 208
 SLICE_UNROLL = 8
 LN2 = math.log(2.0)
+LOG2E = 1.0 / math.log(2.0)
 VMEM_SPEC = pl.BlockSpec(memory_space=pltpu.VMEM)
 SMEM_SPEC = pl.BlockSpec(memory_space=pltpu.SMEM)
 HBM_SPEC = pl.BlockSpec(memory_space=pltpu.HBM)
@@ -66,15 +67,6 @@
 
 def tint(sheared):
     return jnp.tanh(0.75 * sheared), jnp.exp(-0.5 * (sheared * sheared)), jnp.tanh(0.4 - 0.5 * sheared)
-
-
-def absorb_sample(view, half, tints, keep):
-    through = view[4 * half + 3]
-    after = through * keep
-    weight = through - after
-    view[4 * half + 3] = after
-    for channel in range(3):
-        view[4 * half + channel] = view[4 * half + channel] + weight * tints[channel]
 
 
 def tile_kernel(
@@ -150,6 +142,8 @@
     for copy in scalars:
         copy.wait()
 
+    inside = lax.broadcasted_iota(jnp.int32, (ROWS, COLS), 0) > 0
+
     def slice_step(z, carry):
         k = shift_ref[1, z] + 64
         here = d_ref[z]
@@ -157,12 +151,20 @@
         mixed = here + frac_ref[0, z] * (behind - here)
         left = pltpu.roll(mixed, 1, 1)
         sheared = pltpu.roll(mixed + frac_ref[1, z] * (left - mixed), k, 1)
-        tints = tint(sheared)
-        keep = jnp.exp((-absorb_ref[z] * scale) * softplus(sheared))
-        keep = jnp.concatenate([jnp.where(sub == 0, 1.0, keep[0:8]), keep[8:]], axis=0)
+        twos = LOG2E * sheared
+        positive = jnp.maximum(twos, 0.0)
+        soft = positive + jnp.log2(1.0 + jnp.exp2((twos - positive) - positive))
+        keep = jnp.exp2((-absorb_ref[z] * scale) * soft)
+        tints = jnp.tanh(0.75 * sheared), jnp.exp2((-0.5 * twos) * sheared), jnp.tanh(0.4 - 0.5 * sheared)
         view = acc_ref.at[:, pl.ds(shift_ref[0, z] + 64, 64), :]
-        absorb_sample(view, 0, tints, jnp.where(lane > k, keep, 1.0))
-        absorb_sample(view, 1, tints, jnp.where(lane < k, keep, 1.0))
+        right = lane < k
+        value = [jnp.where(right, view[4 + c], view[c]) for c in range(4)]
+        after = value[3] * keep
+        weight = value[3] - after
+        value = [value[c] + weight * tints[c] for c in range(3)] + [after]
+        for c in range(4):
+            pltpu.store(view.at[c], value[c], mask=inside & (lane > k))
+            pltpu.store(view.at[4 + c], value[c], mask=inside & right)
         return carry
 
     lax.fori_loop(0, SLAB, slice_step, 0, unroll=SLICE_UNROLL)
@@ -201,8 +203,14 @@
     return jnp.concatenate(tiles, axis=0)
 
 
-def exact_dot(a, b):
-    return jnp.dot(a, b, precision=lax.Precision.HIGHEST, preferred_element_type=jnp.float32)
+def select_dot(chosen, values):
+    coarse = values.astype(jnp.bfloat16)
+    rest = values - coarse.astype(jnp.float32)
+    fine = rest.astype(jnp.bfloat16)
+    left = chosen.astype(jnp.bfloat16)
+    return jnp.dot(left, coarse, preferred_element_type=jnp.float32) + jnp.dot(
+        left, fine, preferred_element_type=jnp.float32
+    )
 
 
 def line_composite(sheared, opticals, key_row, key_col):
@@ -211,14 +219,14 @@
     ahead = jnp.where((second < first) & (key_row == key_col), 1.0, 0.0)
     target = lax.broadcasted_iota(jnp.int32, (2 * SLAB, SLAB), 0).astype(jnp.float32)
     chosen = jnp.where(target == key_row + 64.0, 1.0, 0.0)
-    before = exact_dot(ahead, jnp.concatenate(opticals, axis=1))
+    before = select_dot(ahead, jnp.concatenate(opticals, axis=1))
     tints = tint(sheared)
     pieces = []
     for half, optical in enumerate(opticals):
         front = before[:, COLS * half : COLS * half + COLS]
         weight = jnp.exp(-front) - jnp.exp(-(front + optical))
         pieces += [weight * tints[0], weight * tints[1], weight * tints[2], weight]
-    total = exact_dot(chosen, jnp.concatenate(pieces, axis=1))
+    total = select_dot(chosen, jnp.concatenate(pieces, axis=1))
     return [total[:, COLS * p : COLS * p + COLS] for p in range(len(pieces))]
 
 
@@ -276,8 +284,11 @@
     here = turn_rows(jnp.transpose(pair), amount)
     columns = here + jnp.concatenate([fy, fy], axis=0) * (pltpu.roll(here, 1, 1) - here)
     u_ref[...] = columns
-    near_out_ref[pl.ds(128, 64), :] = jnp.where(odd_col, columns[64:], columns[:64])
-    far_out_ref[pl.ds(128, 64), :] = jnp.where(odd_col, columns[:64], columns[64:])
+    turned = pltpu.roll(columns, 64, 1)
+    last = jnp.where(lane < 64, columns[:32], turned[32:64])
+    first = jnp.where(lane < 64, columns[64:96], turned[96:])
+    near_out_ref[pl.ds(128, 32), :] = jnp.where(odd_col, first, last)
+    far_out_ref[pl.ds(128, 32), :] = jnp.where(odd_col, last, first)
 
 
 def columns_kernel(scale, limit, edge_ref, mine_ref, near_ref, far_ref, u_ref, zrow_ref, zcol_ref, fvec_ref, fcol_ref, out_ref):
@@ -289,7 +300,9 @@
         near, far = near_ref[pl.ds(start, size), :], far_ref[pl.ds(start, size), :]
         return jnp.where(odd_col, far, near), jnp.where(odd_col, near, far)
 
-    right_first, left_last = received(128, 64)
+    right_first, left_last = [
+        jnp.concatenate([part, pltpu.roll(part, 64, 1)], axis=0) for part in received(128, 32)
+    ]
     here = jnp.where(ox < 0.0, right_first, u_ref[pl.ds(64, 64), :])
     behind = jnp.where(ox < 0.0, u_ref[pl.ds(0, 64), :], left_last)
     sheared = here + fx * (behind - here)
@@ -373,7 +386,7 @@
 
     far = lax.ppermute(far, "imgy", matching(row_count, 1))
     near = lax.ppermute(near, "imgy", matching(row_count, 0))
-    packed = f32(192, COLS)
+    packed = f32(160, COLS)
     mine, near, far, sheared_cols = call(
         functools.partial(rows_kernel, scale),
         (f32(4, ROWS, COLS), packed, packed, f32(128, COLS)),

time: 45.9 us -> 44.5 us (0.969)
  Pallas kernels: 11.7 us -> 10.6 us
    pallas_call x1, Pallas kernels: 7.94 us -> 7.33 us  [body(): call(functools.partial(tile_kernel, scale), (sent, f32(512, COLS), sent,...]
where the time goes in v6:
time: 44.5 us; the launch traced here: 44.3 us
  blocking collectives  17.3 us (39%)
  Pallas kernels  10.6 us (24%)
  waiting for transfers between devices  9.84 us (22%)
  starting transfers between devices  5.72 us (13%)
    all_to_all x1, blocking collectives, body(): lax.all_to_all(pieces, 'depth', split_axis=0, concat_axis=0, tiled=True)  17.3 us
    pallas_call x1, Pallas kernels, body(): call(functools.partial(tile_kernel, scale), (sent, f32(512, COLS), sent,...  7.33 us
    ppermute x1, waiting for transfers between devices, body(): far = lax.ppermute(far, 'imgy', matching(row_count, 1))  5.34 us
    ppermute x1, waiting for transfers between devices, body(): far = lax.ppermute(far, 'imgx', matching(col_count, 1))  2.79 us
    ppermute x1, starting transfers between devices, body(): far = lax.ppermute(far, 'imgy', matching(row_count, 1))  2.44 us
    ppermute x1, starting transfers between devices, body(): far = lax.ppermute(far, 'imgx', matching(col_count, 1))  1.91 us
    ppermute x1, waiting for transfers between devices, body(): near = lax.ppermute(near, 'imgx', matching(col_count, 0))  1.71 us
    pallas_call x1, Pallas kernels, body(): call(functools.partial(rows_kernel, scale), (f32(4, ROWS, COLS), packed,...  1.46 us
  transfers between devices with their start and end apart: 4, of which 3 were waited for; matrix products, arithmetic and copies ran while one was open for 1% of the time, Pallas kernels for 0%

profile of v6, /device:TPU:20, one launch (start us, length us, event | category | flops | bytes accessed | tf_op | source)
XLA Modules:
  0.0 44.3 jit_solution(16609007995539045563)
XLA Ops:
  0.0 0.0 copy-start
  0.0 0.0 copy-start.2
  0.0 0.0 copy-start.1
  0.0 0.1 pad_add_fusion.edge_ref
  0.1 7.3 %shard_map.46 = (f32[640,128]{1,0:T(8,128)S(1)}, f32[512,128]{1,0:T(8,128)S(1)}, f32[640,128]{1,0:T(8,128)S(1)}, f32[128,128]{1,0:T(8,128)S(1)}, f32[64,128]{1,0:T(8,128)S(1)}) custom-call(s32[3]{0:T(128)S(1)} %pad_add_fusion.edge_ref, s32[2,64]{1,0:T(2,128)} %shift_ref.1, f32[2,64]{1,0:T(2,128)} %frac_hbm.1, f32[64]{0:T(128)} %absorb_hbm.1, ...), custom_call_target="tpu_custom_call" | custom-call | flops 300000000 | bytes 4194304 | tf_op jit(solution)/shard_map/pallas_call | solution.py:367
  7.4 0.1 collective-permute-start
  7.5 2.4 %collective-permute-start.1 = (f32[640,128]{1,0:T(8,128)S(1)}, f32[640,128]{1,0:T(8,128)S(1)}, u32[]{:S(2)}, u32[]{:S(2)}) collective-permute-start(f32[640,128]{1,0:T(8,128)S(1)} %get-tuple-element.16), channel_id=1, source_target_pairs={{4,8},{12,16},{20,24},{8,4},{16,12},{24,20},{5,9},{13,17},{21,25},... | collective-permute-start | bytes 983048 | tf_op jit(solution)/shard_map/ppermute | solution.py:387
  10.0 0.0 copy-done
  10.0 0.0 copy-done.2
  10.0 0.0 copy-done.1
  10.1 0.1 copy.16
  10.2 0.2 select_reduce_fusion.3
  10.4 0.1 copy.17.zrow_ref
  10.5 0.1 select_reduce_fusion.1
  10.6 0.0 collective-permute-done.near_ref
  10.6 5.3 %collective-permute-done.1.far_ref = f32[640,128]{1,0:T(8,128)S(1)} collective-permute-done((f32[640,128]{1,0:T(8,128)S(1)}, f32[640,128]{1,0:T(8,128)S(1)}, u32[]{:S(2)}, u32[]{:S(2)}) %collective-permute-start.1) | collective-permute-done | bytes 327712 | tf_op jit(solution)/shard_map/ppermute | solution.py:387
  15.9 1.5 %shard_map.47 = (f32[4,64,128]{2,1,0:T(8,128)S(1)}, f32[160,128]{1,0:T(8,128)S(1)}, f32[160,128]{1,0:T(8,128)S(1)}, f32[128,128]{1,0:T(8,128)S(1)}) custom-call(s32[2,64]{1,0:T(2,128)S(1)} %copy-done, s32[3]{0:T(128)S(1)} %pad_add_fusion.edge_ref, f32[512,128]{1,0:T(8,128)S(1)} %get-tuple-element.14.own_ref, f32[640,128]{1,0:T(8,128)S(1)} %collective-permute-done.near_ref, ...), custom_call_target="tpu_custom_call" | custom-call | flops 1000 | bytes 1000 | tf_op jit(solution)/shard_map/pallas_call | solution.py:390
  17.4 1.3 %collective-permute-start.2 = (f32[160,128]{1,0:T(8,128)S(1)}, f32[160,128]{1,0:T(8,128)S(1)}, u32[]{:S(2)}, u32[]{:S(2)}) collective-permute-start(f32[160,128]{1,0:T(8,128)S(1)} %get-tuple-element.20), channel_id=1, source_target_pairs={{0,1},{2,3},{1,0},{3,2},{4,5},{6,7},{5,4},{7,6},{8,9},{10,11},{9,8... | collective-permute-start | bytes 245768 | tf_op jit(solution)/shard_map/ppermute | solution.py:396
  18.7 1.9 %collective-permute-start.3 = (f32[160,128]{1,0:T(8,128)S(1)}, f32[160,128]{1,0:T(8,128)S(1)}, u32[]{:S(2)}, u32[]{:S(2)}) collective-permute-start(f32[160,128]{1,0:T(8,128)S(1)} %get-tuple-element.21), channel_id=1, source_target_pairs={{1,2},{2,1},{5,6},{6,5},{9,10},{10,9},{13,14},{14,13},{17,18},{18,... | collective-permute-start | bytes 245768 | tf_op jit(solution)/shard_map/ppermute | solution.py:395
  20.6 1.7 %collective-permute-done.2.near_ref = f32[160,128]{1,0:T(8,128)S(1)} collective-permute-done((f32[160,128]{1,0:T(8,128)S(1)}, f32[160,128]{1,0:T(8,128)S(1)}, u32[]{:S(2)}, u32[]{:S(2)}) %collective-permute-start.2) | collective-permute-done | bytes 81952 | tf_op jit(solution)/shard_map/ppermute | solution.py:396
  22.3 2.8 %collective-permute-done.3.far_ref = f32[160,128]{1,0:T(8,128)S(1)} collective-permute-done((f32[160,128]{1,0:T(8,128)S(1)}, f32[160,128]{1,0:T(8,128)S(1)}, u32[]{:S(2)}, u32[]{:S(2)}) %collective-permute-start.3) | collective-permute-done | bytes 81952 | tf_op jit(solution)/shard_map/ppermute | solution.py:395
  25.1 1.2 %shard_map.48 = f32[8,4,8,128]{3,2,1,0:T(8,128)S(1)} custom-call(s32[3]{0:T(128)S(1)} %pad_add_fusion.edge_ref, f32[4,64,128]{2,1,0:T(8,128)S(1)} %get-tuple-element.19.mine_ref, f32[160,128]{1,0:T(8,128)S(1)} %collective-permute-done.2.near_ref, f32[160,128]{1,0:T(8,128)S(1)} %collective-permute-done.3.far_ref, f32[128,128]{1,0:T(8,128)S(1)} %get-tuple-element.22.u_ref, ...), custom_call_target="tpu_custom_call" | custom-call | flops 1000 | bytes 1000 | tf_op jit(solution)/shard_map/pallas_call | solution.py:409
  26.3 17.3 %all_to_all.5.in_ref = f32[8,4,8,128]{3,2,1,0:T(8,128)S(1)} all-to-all(f32[8,4,8,128]{3,2,1,0:T(8,128)S(1)} %shard_map.48), channel_id=1, replica_groups=mesh['depth'=8,'imgy'=8,'imgx'=4] {'depth'}, dimensions={0} | all-to-all | bytes 262144 | tf_op jit(solution)/shard_map/all_to_all | solution.py:414
  43.7 0.6 %shard_map.49 = f32[4,8,128]{2,1,0:T(8,128)} custom-call(f32[8,4,8,128]{3,2,1,0:T(8,128)S(1)} %all_to_all.5.in_ref), custom_call_target="tpu_custom_call" | custom-call | flops 1000 | bytes 1000 | tf_op jit(solution)/shard_map/pallas_call | solution.py:415
  (9 shorter events, 0.1 us)
Async XLA Ops:
  0.0 10.0 %copy-start = (s32[2,64]{1,0:T(2,128)S(1)}, s32[2,64]{1,0:T(2,128)}, u32[]{:S(2)}) copy-start(s32[2,64]{1,0:T(2,128)} %shift_ref.1) | copy-start | bytes 1540
  0.0 10.0 %copy-start.2 = (f32[2,64]{1,0:T(2,128)S(1)}, f32[2,64]{1,0:T(2,128)}, u32[]{:S(2)}) copy-start(f32[2,64]{1,0:T(2,128)} %frac_hbm.1) | copy-start | bytes 1540
  0.0 10.0 %copy-start.1 = (f32[64]{0:T(128)S(1)}, f32[64]{0:T(128)}, u32[]{:S(2)}) copy-start(f32[64]{0:T(128)} %absorb_hbm.1) | copy-start | bytes 772
  7.4 3.1 %collective-permute-start = (f32[640,128]{1,0:T(8,128)S(1)}, f32[640,128]{1,0:T(8,128)S(1)}, u32[]{:S(2)}, u32[]{:S(2)}) collective-permute-start(f32[640,128]{1,0:T(8,128)S(1)} %get-tuple-element.15), channel_id=1, source_target_pairs={{0,4},{8,12},{16,20},{24,28},{4,0},{12,8},{20,16},{28,24},{1,5},{9... | collective-permute-start | bytes 983048 | tf_op jit(solution)/shard_map/ppermute | solution.py:388
  7.5 8.4 %collective-permute-start.1 = (f32[640,128]{1,0:T(8,128)S(1)}, f32[640,128]{1,0:T(8,128)S(1)}, u32[]{:S(2)}, u32[]{:S(2)}) collective-permute-start(f32[640,128]{1,0:T(8,128)S(1)} %get-tuple-element.16), channel_id=1, source_target_pairs={{4,8},{12,16},{20,24},{8,4},{16,12},{24,20},{5,9},{13,17},{21,25},... | collective-permute-start | bytes 983048 | tf_op jit(solution)/shard_map/ppermute | solution.py:387
  17.4 4.9 %collective-permute-start.2 = (f32[160,128]{1,0:T(8,128)S(1)}, f32[160,128]{1,0:T(8,128)S(1)}, u32[]{:S(2)}, u32[]{:S(2)}) collective-permute-start(f32[160,128]{1,0:T(8,128)S(1)} %get-tuple-element.20), channel_id=1, source_target_pairs={{0,1},{2,3},{1,0},{3,2},{4,5},{6,7},{5,4},{7,6},{8,9},{10,11},{9,8... | collective-permute-start | bytes 245768 | tf_op jit(solution)/shard_map/ppermute | solution.py:396
  18.7 6.4 %collective-permute-start.3 = (f32[160,128]{1,0:T(8,128)S(1)}, f32[160,128]{1,0:T(8,128)S(1)}, u32[]{:S(2)}, u32[]{:S(2)}) collective-permute-start(f32[160,128]{1,0:T(8,128)S(1)} %get-tuple-element.21), channel_id=1, source_target_pairs={{1,2},{2,1},{5,6},{6,5},{9,10},{10,9},{13,14},{14,13},{17,18},{18,... | collective-permute-start | bytes 245768 | tf_op jit(solution)/shard_map/ppermute | solution.py:395

commit v7 on v6

--- a/solution.py
+++ b/solution.py
@@ -13,7 +13,7 @@
 ROWS = 64
 COLS = 128
 EXT = 208
-SLICE_UNROLL = 8
+SLICE_UNROLL = 16
 LN2 = math.log(2.0)
 LOG2E = 1.0 / math.log(2.0)
 VMEM_SPEC = pl.BlockSpec(memory_space=pltpu.VMEM)
@@ -73,14 +73,16 @@
     scale, edge_ref, shift_hbm, frac_hbm, absorb_hbm, c_hbm, near_ref, own_ref, far_ref, rows_ref, cols_ref,
     shift_ref, frac_ref, absorb_ref, c_ref, s2_ref, s1_ref, d_ref, plane_ref, acc_ref, sems,
 ):
-    loads = [
-        pltpu.make_async_copy(c_hbm.at[pl.ds(CHUNK * i, CHUNK)], c_ref.at[pl.ds(CHUNK * i, CHUNK)], sems.at[i])
-        for i in range(SLAB // CHUNK)
-    ]
+    def load(index, planes, rows):
+        block = (pl.ds(*planes), pl.ds(*rows))
+        return pltpu.make_async_copy(c_hbm.at[block], c_ref.at[block], sems.at[index])
+
+    loads = [load(0, (0, 16), (0, 16)), load(1, (16, 16), (0, 32)), load(2, (0, 16), (16, 16))]
+    loads += [load(3, (0, 16), (32, 32)), load(4, (32, 16), (0, 64)), load(5, (16, 16), (32, 32)), load(6, (48, 16), (0, 64))]
     scalars = [
-        pltpu.make_async_copy(shift_hbm, shift_ref, sems.at[4]),
-        pltpu.make_async_copy(frac_hbm, frac_ref, sems.at[5]),
-        pltpu.make_async_copy(absorb_hbm, absorb_ref, sems.at[6]),
+        pltpu.make_async_copy(shift_hbm, shift_ref, sems.at[7]),
+        pltpu.make_async_copy(frac_hbm, frac_ref, sems.at[8]),
+        pltpu.make_async_copy(absorb_hbm, absorb_ref, sems.at[9]),
     ]
     for copy in loads + scalars:
         copy.start()
@@ -124,17 +126,19 @@
             piece = result[64 * odd : 64 * odd + 64]
             rows_ref[pl.ds(z, 1), :] = piece[63:64]
             rows_ref[pl.ds(64 + z, 1), :] = piece[0:1]
-            plane = jnp.where(lane == z, pltpu.roll(piece, z + 1, 1), plane)
-            plane = jnp.where(lane == z + 64, pltpu.roll(piece, z + 64, 1), plane)
+            plane = jnp.where(lane // 2 == z, pltpu.roll(piece, 2 * z + 1, 1), plane)
         return plane
 
     loads[0].wait()
     level(8, None, s2_ref, ignore, 0, 8)
     loads[1].wait()
+    loads[2].wait()
     level(16, s2_ref, s1_ref, ignore, 0, 16)
-    loads[2].wait()
+    loads[3].wait()
+    loads[4].wait()
     plane = level(32, s1_ref, d_ref, boundary, jnp.zeros((64, COLS), jnp.float32), 16, (0, 16))
-    loads[3].wait()
+    loads[5].wait()
+    loads[6].wait()
     plane_ref[...] = level(32, s1_ref, d_ref, boundary, plane, 16, (16, 32))
     for row_odd in range(2):
         cols_ref[pl.ds(row_odd, 32, stride=2), :] = plane_ref[pl.ds(32 * row_odd, 32), :]
@@ -231,7 +235,7 @@
 
 
 def rows_kernel(
-    scale, shift_ref, edge_ref, own_ref, near_ref, far_ref, rows_ref, cols_ref, fvec_ref, fcol_ref,
+    scale, shift_ref, edge_ref, own_ref, near_ref, far_ref, rows_ref, cols_ref, fvec_ref, fcol_ref, fy_ref,
     mine_ref, near_out_ref, far_out_ref, u_ref,
 ):
     lane = lax.broadcasted_iota(jnp.int32, (1, COLS), 1)
@@ -272,21 +276,23 @@
         far_out_ref[pl.ds(32 * c, 32), :] = jnp.where(odd_col, right, left)
 
     below_col, above_col = received(576, 64)
-    negative = jnp.concatenate([fvec_ref[3:4, 0:SLAB]] * 2, axis=1) < 0.0
+    negative = fvec_ref[5:6, :] < 0.0
     pair = jnp.concatenate(
         [jnp.where(negative, cols_ref[...], above_col), jnp.where(negative, below_col, cols_ref[...])], axis=0
     )
 
     def amount(z):
-        offset = shift_ref[0, z % SLAB]
+        offset = shift_ref[0, z // 2]
         return jnp.where(offset < 0, offset + COLS, offset + 64)
 
     here = turn_rows(jnp.transpose(pair), amount)
-    columns = here + jnp.concatenate([fy, fy], axis=0) * (pltpu.roll(here, 1, 1) - here)
-    u_ref[...] = columns
-    turned = pltpu.roll(columns, 64, 1)
-    last = jnp.where(lane < 64, columns[:32], turned[32:64])
-    first = jnp.where(lane < 64, columns[64:96], turned[96:])
+    u_ref[...] = here + fy_ref[:, 0:1] * (pltpu.roll(here, 1, 1) - here)
+
+    def pack(column):
+        upper = u_ref[pl.ds(column, 32, stride=2), :]
+        return jnp.where(lane < 64, upper, pltpu.roll(u_ref[pl.ds(64 + column, 32, stride=2), :], 64, 1))
+
+    last, first = pack(0), pack(1)
     near_out_ref[pl.ds(128, 32), :] = jnp.where(odd_col, first, last)
     far_out_ref[pl.ds(128, 32), :] = jnp.where(odd_col, last, first)
 
@@ -303,8 +309,8 @@
     right_first, left_last = [
         jnp.concatenate([part, pltpu.roll(part, 64, 1)], axis=0) for part in received(128, 32)
     ]
-    here = jnp.where(ox < 0.0, right_first, u_ref[pl.ds(64, 64), :])
-    behind = jnp.where(ox < 0.0, u_ref[pl.ds(0, 64), :], left_last)
+    here = jnp.where(ox < 0.0, right_first, u_ref[pl.ds(1, 64, stride=2), :])
+    behind = jnp.where(ox < 0.0, u_ref[pl.ds(0, 64, stride=2), :], left_last)
     sheared = here + fx * (behind - here)
     row = (lane + edge_ref[2]).astype(jnp.float32) - oy
     optical = jnp.where((row >= 0.0) & (row <= limit), rate * softplus(sheared), 0.0)
@@ -345,6 +351,21 @@
     out_ref[3] = merged[3]
 
 
+def tile_scratch():
+    return [
+        pltpu.SMEM((2, SLAB), jnp.int32),
+        pltpu.SMEM((2, SLAB), jnp.float32),
+        pltpu.SMEM((SLAB,), jnp.float32),
+        pltpu.VMEM((SLAB, ROWS, COLS), jnp.float32),
+        pltpu.VMEM((16, 16, COLS), jnp.float32),
+        pltpu.VMEM((32, 32, COLS), jnp.float32),
+        pltpu.VMEM((64, 64, COLS), jnp.float32),
+        pltpu.VMEM((64, COLS), jnp.float32),
+        pltpu.VMEM((8, EXT, COLS), jnp.float32),
+        pltpu.SemaphoreType.DMA((10,)),
+    ]
+
+
 def matching(count, first):
     pairs = [(i, i + 1) for i in range(first, count - 1, 2)]
     return pairs + [(j, i) for i, j in pairs]
@@ -360,7 +381,9 @@
     shift_rows, shift_cols = shifts[0], shifts[1]
     edge = jnp.stack([iy % 2, ix % 2, iy * ROWS]).astype(jnp.int32)
     lines = jnp.concatenate([fraction, absorb[None], shifts.astype(jnp.float32)], axis=0)
-    vectors = jnp.pad(lines, ((0, 3), (0, COLS - SLAB)))
+    twice = jnp.repeat(lines[3:4], 2, axis=1)
+    vectors = jnp.concatenate([jnp.pad(lines, ((0, 0), (0, COLS - SLAB))), twice, jnp.zeros((2, COLS))], axis=0)
+    fy_twice = jnp.repeat(fraction[0], 2)[:, None]
     columns = jnp.pad(lines.T, ((0, 0), (0, 3)))
 
     sent = f32(640, COLS)
@@ -368,18 +391,7 @@
         functools.partial(tile_kernel, scale),
         (sent, f32(512, COLS), sent, f32(128, COLS), f32(64, COLS)),
         [SMEM_SPEC] + [HBM_SPEC] * 4,
-        [
-            pltpu.SMEM((2, SLAB), jnp.int32),
-            pltpu.SMEM((2, SLAB), jnp.float32),
-            pltpu.SMEM((SLAB,), jnp.float32),
-            pltpu.VMEM((SLAB, ROWS, COLS), jnp.float32),
-            pltpu.VMEM((16, 16, COLS), jnp.float32),
-            pltpu.VMEM((32, 32, COLS), jnp.float32),
-            pltpu.VMEM((64, 64, COLS), jnp.float32),
-            pltpu.VMEM((64, COLS), jnp.float32),
-            pltpu.VMEM((8, EXT, COLS), jnp.float32),
-            pltpu.SemaphoreType.DMA((7,)),
-        ],
+        tile_scratch(),
         flops=300_000_000,
         bytes_moved=4 << 20,
     )(edge, *[pltpu.with_memory_space_constraint(a, pltpu.HBM) for a in (shifts, fraction, absorb, coefficients)])
@@ -390,8 +402,8 @@
     mine, near, far, sheared_cols = call(
         functools.partial(rows_kernel, scale),
         (f32(4, ROWS, COLS), packed, packed, f32(128, COLS)),
-        [SMEM_SPEC] * 2 + [VMEM_SPEC] * 7,
-    )(shifts, edge, own, near, far, row_planes, col_planes, vectors, columns)
+        [SMEM_SPEC] * 2 + [VMEM_SPEC] * 8,
+    )(shifts, edge, own, near, far, row_planes, col_planes, vectors, columns, fy_twice)
     far = lax.ppermute(far, "imgx", matching(col_count, 1))
     near = lax.ppermute(near, "imgx", matching(col_count, 0))
 

time: 44.5 us -> 43.5 us (0.978)
  Pallas kernels: 10.6 us -> 9.66 us
  waiting for transfers between devices: 9.84 us -> 9.3 us
    pallas_call x1, Pallas kernels: 7.33 us -> 6.39 us  [body(): call(functools.partial(tile_kernel, scale), (sent, f32(512, COLS), sent,...]
    ppermute x1, waiting for transfers between devices: 5.34 us -> 4.8 us  [body(): far = lax.ppermute(far, 'imgy', matching(row_count, 1))]
  transfers between devices with their start and end apart: 4 -> 4, of which waited for: 3 -> 3; matrix products, arithmetic and copies ran while one was open for 1% -> 2% of each run, Pallas kernels for 0% -> 0%
where the time goes in v7:
time: 43.5 us; the launch traced here: 43.4 us
  blocking collectives  17.4 us (40%)
  Pallas kernels  9.66 us (22%)
  waiting for transfers between devices  9.3 us (21%)
  starting transfers between devices  5.73 us (13%)
  local copies, waits for them, and re-layouts  0.66 us (2%)
  other arithmetic  0.47 us (1%)
    all_to_all x1, blocking collectives, body(): lax.all_to_all(pieces, 'depth', split_axis=0, concat_axis=0, tiled=True)  17.4 us
    pallas_call x1, Pallas kernels, body(): call(functools.partial(tile_kernel, scale), (sent, f32(512, COLS), sent,...  6.39 us
    ppermute x1, waiting for transfers between devices, body(): far = lax.ppermute(far, 'imgy', matching(row_count, 1))  4.8 us
    ppermute x1, waiting for transfers between devices, body(): far = lax.ppermute(far, 'imgx', matching(col_count, 1))  2.8 us
    ppermute x1, starting transfers between devices, body(): far = lax.ppermute(far, 'imgy', matching(row_count, 1))  2.45 us
    ppermute x1, starting transfers between devices, body(): far = lax.ppermute(far, 'imgx', matching(col_count, 1))  1.91 us
    ppermute x1, waiting for transfers between devices, body(): near = lax.ppermute(near, 'imgx', matching(col_count, 0))  1.71 us
    pallas_call x1, Pallas kernels, body(): call(functools.partial(rows_kernel, scale), (f32(4, ROWS, COLS), packed,...  1.44 us
  transfers between devices with their start and end apart: 4, of which 3 were waited for; matrix products, arithmetic and copies ran while one was open for 2% of the time, Pallas kernels for 0%

profile of v7, /device:TPU:20, one launch (start us, length us, event | category | flops | bytes accessed | tf_op | source)
XLA Modules:
  0.0 43.4 jit_solution(8185945852024028763)
XLA Ops:
  0.0 0.0 copy-start
  0.0 0.0 copy-start.2
  0.0 0.0 copy-start.1
  0.0 0.1 pad_add_fusion.edge_ref
  0.1 6.4 %shard_map.46 = (f32[640,128]{1,0:T(8,128)S(1)}, f32[512,128]{1,0:T(8,128)S(1)}, f32[640,128]{1,0:T(8,128)S(1)}, f32[128,128]{1,0:T(8,128)S(1)}, f32[64,128]{1,0:T(8,128)S(1)}) custom-call(s32[3]{0:T(128)S(1)} %pad_add_fusion.edge_ref, s32[2,64]{1,0:T(2,128)} %shift_ref.1, f32[2,64]{1,0:T(2,128)} %frac_hbm.1, f32[64]{0:T(128)} %absorb_hbm.1, ...), custom_call_target="tpu_custom_call" | custom-call | flops 300000000 | bytes 4194304 | tf_op jit(solution)/shard_map/pallas_call | solution.py:390
  6.5 0.1 collective-permute-start
  6.6 2.4 %collective-permute-start.1 = (f32[640,128]{1,0:T(8,128)S(1)}, f32[640,128]{1,0:T(8,128)S(1)}, u32[]{:S(2)}, u32[]{:S(2)}) collective-permute-start(f32[640,128]{1,0:T(8,128)S(1)} %get-tuple-element.16), channel_id=1, source_target_pairs={{4,8},{12,16},{20,24},{8,4},{16,12},{24,20},{5,9},{13,17},{21,25},... | collective-permute-start | bytes 983048 | tf_op jit(solution)/shard_map/ppermute | solution.py:399
  9.1 0.0 copy-done
  9.1 0.0 copy-done.2
  9.1 0.0 copy-done.1
  9.2 0.1 broadcast_in_dim.56
  9.2 0.1 broadcast_in_dim.57
  9.4 0.1 copy.29
  9.5 0.1 broadcast_in_dim.59
  9.5 0.1 broadcast_in_dim_reshape.4.fy_ref
  9.6 0.2 select_reduce_fusion.3
  9.8 0.1 copy.31.zrow_ref
  10.0 0.1 pad.16.clone
  10.0 0.1 select_reduce_fusion.1
  10.1 0.1 fusion.fvec_ref
  10.2 0.0 collective-permute-done.near_ref
  10.2 4.8 %collective-permute-done.1.far_ref = f32[640,128]{1,0:T(8,128)S(1)} collective-permute-done((f32[640,128]{1,0:T(8,128)S(1)}, f32[640,128]{1,0:T(8,128)S(1)}, u32[]{:S(2)}, u32[]{:S(2)}) %collective-permute-start.1) | collective-permute-done | bytes 327712 | tf_op jit(solution)/shard_map/ppermute | solution.py:399
  15.0 1.4 %shard_map.47 = (f32[4,64,128]{2,1,0:T(8,128)S(1)}, f32[160,128]{1,0:T(8,128)S(1)}, f32[160,128]{1,0:T(8,128)S(1)}, f32[128,128]{1,0:T(8,128)S(1)}) custom-call(s32[2,64]{1,0:T(2,128)S(1)} %copy-done, s32[3]{0:T(128)S(1)} %pad_add_fusion.edge_ref, f32[512,128]{1,0:T(8,128)S(1)} %get-tuple-element.14.own_ref, f32[640,128]{1,0:T(8,128)S(1)} %collective-permute-done.near_ref, ...), custom_call_target="tpu_custom_call" | custom-call | flops 1000 | bytes 1000 | tf_op jit(solution)/shard_map/pallas_call | solution.py:402
  16.4 1.3 %collective-permute-start.2 = (f32[160,128]{1,0:T(8,128)S(1)}, f32[160,128]{1,0:T(8,128)S(1)}, u32[]{:S(2)}, u32[]{:S(2)}) collective-permute-start(f32[160,128]{1,0:T(8,128)S(1)} %get-tuple-element.20), channel_id=1, source_target_pairs={{0,1},{2,3},{1,0},{3,2},{4,5},{6,7},{5,4},{7,6},{8,9},{10,11},{9,8... | collective-permute-start | bytes 245768 | tf_op jit(solution)/shard_map/ppermute | solution.py:408
  17.7 1.9 %collective-permute-start.3 = (f32[160,128]{1,0:T(8,128)S(1)}, f32[160,128]{1,0:T(8,128)S(1)}, u32[]{:S(2)}, u32[]{:S(2)}) collective-permute-start(f32[160,128]{1,0:T(8,128)S(1)} %get-tuple-element.21), channel_id=1, source_target_pairs={{1,2},{2,1},{5,6},{6,5},{9,10},{10,9},{13,14},{14,13},{17,18},{18,... | collective-permute-start | bytes 245768 | tf_op jit(solution)/shard_map/ppermute | solution.py:407
  19.7 1.7 %collective-permute-done.2.near_ref = f32[160,128]{1,0:T(8,128)S(1)} collective-permute-done((f32[160,128]{1,0:T(8,128)S(1)}, f32[160,128]{1,0:T(8,128)S(1)}, u32[]{:S(2)}, u32[]{:S(2)}) %collective-permute-start.2) | collective-permute-done | bytes 81952 | tf_op jit(solution)/shard_map/ppermute | solution.py:408
  21.4 2.8 %collective-permute-done.3.far_ref = f32[160,128]{1,0:T(8,128)S(1)} collective-permute-done((f32[160,128]{1,0:T(8,128)S(1)}, f32[160,128]{1,0:T(8,128)S(1)}, u32[]{:S(2)}, u32[]{:S(2)}) %collective-permute-start.3) | collective-permute-done | bytes 81952 | tf_op jit(solution)/shard_map/ppermute | solution.py:407
  24.2 1.2 %shard_map.48 = f32[8,4,8,128]{3,2,1,0:T(8,128)S(1)} custom-call(s32[3]{0:T(128)S(1)} %pad_add_fusion.edge_ref, f32[4,64,128]{2,1,0:T(8,128)S(1)} %get-tuple-element.19.mine_ref, f32[160,128]{1,0:T(8,128)S(1)} %collective-permute-done.2.near_ref, f32[160,128]{1,0:T(8,128)S(1)} %collective-permute-done.3.far_ref, f32[128,128]{1,0:T(8,128)S(1)} %get-tuple-element.22.u_ref, ...), custom_call_target="tpu_custom_call" | custom-call | flops 1000 | bytes 1000 | tf_op jit(solution)/shard_map/pallas_call | solution.py:421
  25.4 17.4 %all_to_all.5.in_ref = f32[8,4,8,128]{3,2,1,0:T(8,128)S(1)} all-to-all(f32[8,4,8,128]{3,2,1,0:T(8,128)S(1)} %shard_map.48), channel_id=1, replica_groups=mesh['depth'=8,'imgy'=8,'imgx'=4] {'depth'}, dimensions={0} | all-to-all | bytes 262144 | tf_op jit(solution)/shard_map/all_to_all | solution.py:426
  42.7 0.6 %shard_map.49 = f32[4,8,128]{2,1,0:T(8,128)} custom-call(f32[8,4,8,128]{3,2,1,0:T(8,128)S(1)} %all_to_all.5.in_ref), custom_call_target="tpu_custom_call" | custom-call | flops 1000 | bytes 1000 | tf_op jit(solution)/shard_map/pallas_call | solution.py:427
  (11 shorter events, 0.1 us)
Async XLA Ops:
  0.0 9.1 %copy-start = (s32[2,64]{1,0:T(2,128)S(1)}, s32[2,64]{1,0:T(2,128)}, u32[]{:S(2)}) copy-start(s32[2,64]{1,0:T(2,128)} %shift_ref.1) | copy-start | bytes 1540
  0.0 9.1 %copy-start.2 = (f32[2,64]{1,0:T(2,128)S(1)}, f32[2,64]{1,0:T(2,128)}, u32[]{:S(2)}) copy-start(f32[2,64]{1,0:T(2,128)} %frac_hbm.1) | copy-start | bytes 1540
  0.0 9.1 %copy-start.1 = (f32[64]{0:T(128)S(1)}, f32[64]{0:T(128)}, u32[]{:S(2)}) copy-start(f32[64]{0:T(128)} %absorb_hbm.1) | copy-start | bytes 772
  6.5 3.7 %collective-permute-start = (f32[640,128]{1,0:T(8,128)S(1)}, f32[640,128]{1,0:T(8,128)S(1)}, u32[]{:S(2)}, u32[]{:S(2)}) collective-permute-start(f32[640,128]{1,0:T(8,128)S(1)} %get-tuple-element.15), channel_id=1, source_target_pairs={{0,4},{8,12},{16,20},{24,28},{4,0},{12,8},{20,16},{28,24},{1,5},{9... | collective-permute-start | bytes 983048 | tf_op jit(solution)/shard_map/ppermute | solution.py:400
  6.6 8.4 %collective-permute-start.1 = (f32[640,128]{1,0:T(8,128)S(1)}, f32[640,128]{1,0:T(8,128)S(1)}, u32[]{:S(2)}, u32[]{:S(2)}) collective-permute-start(f32[640,128]{1,0:T(8,128)S(1)} %get-tuple-element.16), channel_id=1, source_target_pairs={{4,8},{12,16},{20,24},{8,4},{16,12},{24,20},{5,9},{13,17},{21,25},... | collective-permute-start | bytes 983048 | tf_op jit(solution)/shard_map/ppermute | solution.py:399
  16.4 4.9 %collective-permute-start.2 = (f32[160,128]{1,0:T(8,128)S(1)}, f32[160,128]{1,0:T(8,128)S(1)}, u32[]{:S(2)}, u32[]{:S(2)}) collective-permute-start(f32[160,128]{1,0:T(8,128)S(1)} %get-tuple-element.20), channel_id=1, source_target_pairs={{0,1},{2,3},{1,0},{3,2},{4,5},{6,7},{5,4},{7,6},{8,9},{10,11},{9,8... | collective-permute-start | bytes 245768 | tf_op jit(solution)/shard_map/ppermute | solution.py:408
  17.7 6.4 %collective-permute-start.3 = (f32[160,128]{1,0:T(8,128)S(1)}, f32[160,128]{1,0:T(8,128)S(1)}, u32[]{:S(2)}, u32[]{:S(2)}) collective-permute-start(f32[160,128]{1,0:T(8,128)S(1)} %get-tuple-element.21), channel_id=1, source_target_pairs={{1,2},{2,1},{5,6},{6,5},{9,10},{10,9},{13,14},{14,13},{17,18},{18,... | collective-permute-start | bytes 245768 | tf_op jit(solution)/shard_map/ppermute | solution.py:407

commit v8 on v7

--- a/solution.py
+++ b/solution.py
@@ -7,6 +7,7 @@
 from jax.experimental import pallas as pl
 from jax.experimental.pallas import tpu as pltpu
 from jax.sharding import PartitionSpec as P
+
 
 BRICK = 64
 SLAB = 64
@@ -19,7 +20,6 @@
 VMEM_SPEC = pl.BlockSpec(memory_space=pltpu.VMEM)
 SMEM_SPEC = pl.BlockSpec(memory_space=pltpu.SMEM)
 HBM_SPEC = pl.BlockSpec(memory_space=pltpu.HBM)
-CHUNK = 16
 INTERPRET = False
 
 
@@ -92,8 +92,10 @@
     lane = lax.broadcasted_iota(jnp.int32, (1, COLS), 1)
     sub = lax.broadcasted_iota(jnp.int32, (8, COLS), 0)
 
+    tables = {half: lane_table(half) for half in (8, 16, 32)}
+
     def level(half, below, out_ref, on_result, init, unroll, span=None):
-        table = lane_table(half)
+        table = tables[half]
 
         def step(i, carry):
             if below is None:
@@ -195,33 +197,30 @@
     return [ref[(*index, c)] for c in range(4)]
 
 
-def turn_rows(plane, amounts):
+def turn_rows(plane, amounts, share=1):
     sub = lax.broadcasted_iota(jnp.int32, (8, COLS), 0)
     tiles = []
     for t in range(plane.shape[0] // 8):
         tile = plane[8 * t : 8 * t + 8]
-        turned = pltpu.roll(tile, amounts(8 * t), 1)
-        for r in range(1, 8):
-            turned = jnp.where(sub == r, pltpu.roll(tile, amounts(8 * t + r), 1), turned)
+        turned = pltpu.roll(tile, amounts(8 * t // share), 1)
+        for r in range(1, 8 // share):
+            turned = jnp.where(sub // share == r, pltpu.roll(tile, amounts(8 * t // share + r), 1), turned)
         tiles.append(turned)
     return jnp.concatenate(tiles, axis=0)
 
 
 def select_dot(chosen, values):
     coarse = values.astype(jnp.bfloat16)
-    rest = values - coarse.astype(jnp.float32)
-    fine = rest.astype(jnp.bfloat16)
-    left = chosen.astype(jnp.bfloat16)
-    return jnp.dot(left, coarse, preferred_element_type=jnp.float32) + jnp.dot(
-        left, fine, preferred_element_type=jnp.float32
-    )
+    rest = (values - coarse.astype(jnp.float32)).astype(jnp.bfloat16)
+    both = jnp.concatenate([coarse, rest], axis=0)
+    return jnp.dot(chosen.astype(jnp.bfloat16), both, preferred_element_type=jnp.float32)
 
 
 def line_composite(sheared, opticals, key_row, key_col):
-    first = lax.broadcasted_iota(jnp.int32, (SLAB, SLAB), 0)
-    second = lax.broadcasted_iota(jnp.int32, (SLAB, SLAB), 1)
+    first = lax.broadcasted_iota(jnp.int32, (SLAB, 2 * SLAB), 0)
+    second = lax.broadcasted_iota(jnp.int32, (SLAB, 2 * SLAB), 1) % SLAB
     ahead = jnp.where((second < first) & (key_row == key_col), 1.0, 0.0)
-    target = lax.broadcasted_iota(jnp.int32, (2 * SLAB, SLAB), 0).astype(jnp.float32)
+    target = lax.broadcasted_iota(jnp.int32, (2 * SLAB, 2 * SLAB), 0).astype(jnp.float32)
     chosen = jnp.where(target == key_row + 64.0, 1.0, 0.0)
     before = select_dot(ahead, jnp.concatenate(opticals, axis=1))
     tints = tint(sheared)
@@ -256,7 +255,7 @@
     optical = rate * softplus(sheared)
     place = lane.astype(jnp.float32)
     opticals = [jnp.where(place > ox + 64.0, optical, 0.0), jnp.where(place < ox + 64.0, optical, 0.0)]
-    line = line_composite(sheared, opticals, fvec_ref[3:4, 0:SLAB], oy)
+    line = line_composite(sheared, opticals, fvec_ref[6:7, :], oy)
 
     halves = []
     for half in range(2):
@@ -282,10 +281,10 @@
     )
 
     def amount(z):
-        offset = shift_ref[0, z // 2]
+        offset = shift_ref[0, z]
         return jnp.where(offset < 0, offset + COLS, offset + 64)
 
-    here = turn_rows(jnp.transpose(pair), amount)
+    here = turn_rows(jnp.transpose(pair), amount, 2)
     u_ref[...] = here + fy_ref[:, 0:1] * (pltpu.roll(here, 1, 1) - here)
 
     def pack(column):
@@ -314,7 +313,7 @@
     sheared = here + fx * (behind - here)
     row = (lane + edge_ref[2]).astype(jnp.float32) - oy
     optical = jnp.where((row >= 0.0) & (row <= limit), rate * softplus(sheared), 0.0)
-    line = line_composite(sheared, [optical], fvec_ref[4:5, 0:SLAB], ox)
+    line = line_composite(sheared, [optical], fvec_ref[7:8, :], ox)
     line = [pltpu.roll(jnp.transpose(part)[:64], 64, 1) for part in line]
 
     front, behind = [], []
@@ -382,7 +381,8 @@
     edge = jnp.stack([iy % 2, ix % 2, iy * ROWS]).astype(jnp.int32)
     lines = jnp.concatenate([fraction, absorb[None], shifts.astype(jnp.float32)], axis=0)
     twice = jnp.repeat(lines[3:4], 2, axis=1)
-    vectors = jnp.concatenate([jnp.pad(lines, ((0, 0), (0, COLS - SLAB))), twice, jnp.zeros((2, COLS))], axis=0)
+    tiled = jnp.tile(lines[3:5], (1, 2))
+    vectors = jnp.concatenate([jnp.pad(lines, ((0, 0), (0, COLS - SLAB))), twice, tiled], axis=0)
     fy_twice = jnp.repeat(fraction[0], 2)[:, None]
     columns = jnp.pad(lines.T, ((0, 0), (0, 3)))
 

time: 43.5 us -> 43.4 us (level)
  no operation moved by 1% of the time
where the time goes in v8:
time: 43.4 us; the launch traced here: 43.2 us
  blocking collectives  17.3 us (40%)
  Pallas kernels  9.53 us (22%)
  waiting for transfers between devices  9.36 us (22%)
  starting transfers between devices  5.71 us (13%)
  local copies, waits for them, and re-layouts  0.67 us (2%)
    all_to_all x1, blocking collectives, body(): lax.all_to_all(pieces, 'depth', split_axis=0, concat_axis=0, tiled=True)  17.3 us
    pallas_call x1, Pallas kernels, body(): call(functools.partial(tile_kernel, scale), (sent, f32(512, COLS), sent,...  6.37 us
    ppermute x1, waiting for transfers between devices, body(): far = lax.ppermute(far, 'imgy', matching(row_count, 1))  4.85 us
    ppermute x1, waiting for transfers between devices, body(): far = lax.ppermute(far, 'imgx', matching(col_count, 1))  2.79 us
    ppermute x1, starting transfers between devices, body(): far = lax.ppermute(far, 'imgy', matching(row_count, 1))  2.43 us
    ppermute x1, starting transfers between devices, body(): far = lax.ppermute(far, 'imgx', matching(col_count, 1))  1.91 us
    ppermute x1, waiting for transfers between devices, body(): near = lax.ppermute(near, 'imgx', matching(col_count, 0))  1.71 us
    pallas_call x1, Pallas kernels, body(): call(functools.partial(rows_kernel, scale), (f32(4, ROWS, COLS), packed,...  1.37 us
  transfers between devices with their start and end apart: 4, of which 3 were waited for; matrix products, arithmetic and copies ran while one was open for 2% of the time, Pallas kernels for 0%

profile of v8, /device:TPU:20, one launch (start us, length us, event | category | flops | bytes accessed | tf_op | source)
XLA Modules:
  0.0 43.2 jit_solution(18011957304940091704)
XLA Ops:
  0.0 0.0 copy-start
  0.0 0.0 copy-start.2
  0.0 0.0 copy-start.1
  0.0 0.1 pad_add_fusion.edge_ref
  0.1 6.4 %shard_map.46 = (f32[640,128]{1,0:T(8,128)S(1)}, f32[512,128]{1,0:T(8,128)S(1)}, f32[640,128]{1,0:T(8,128)S(1)}, f32[128,128]{1,0:T(8,128)S(1)}, f32[64,128]{1,0:T(8,128)S(1)}) custom-call(s32[3]{0:T(128)S(1)} %pad_add_fusion.edge_ref, s32[2,64]{1,0:T(2,128)} %shift_ref.1, f32[2,64]{1,0:T(2,128)} %frac_hbm.1, f32[64]{0:T(128)} %absorb_hbm.1, ...), custom_call_target="tpu_custom_call" | custom-call | flops 300000000 | bytes 4194304 | tf_op jit(solution)/shard_map/pallas_call | solution.py:390
  6.5 0.1 collective-permute-start
  6.6 2.4 %collective-permute-start.1 = (f32[640,128]{1,0:T(8,128)S(1)}, f32[640,128]{1,0:T(8,128)S(1)}, u32[]{:S(2)}, u32[]{:S(2)}) collective-permute-start(f32[640,128]{1,0:T(8,128)S(1)} %get-tuple-element.16), channel_id=1, source_target_pairs={{4,8},{12,16},{20,24},{8,4},{16,12},{24,20},{5,9},{13,17},{21,25},... | collective-permute-start | bytes 983048 | tf_op jit(solution)/shard_map/ppermute | solution.py:399
  9.0 0.0 copy-done
  9.0 0.0 copy-done.2
  9.1 0.0 copy-done.1
  9.1 0.1 broadcast_in_dim.53
  9.2 0.1 broadcast_in_dim.54
  9.4 0.1 tile.10
  9.4 0.1 copy.29
  9.5 0.1 broadcast_in_dim.55
  9.6 0.1 broadcast_in_dim_reshape.4.fy_ref
  9.7 0.2 select_reduce_fusion.3
  9.9 0.1 copy.31.zrow_ref
  10.0 0.1 select_reduce_fusion.1
  10.1 0.0 collective-permute-done.near_ref
  10.1 4.9 %collective-permute-done.1.far_ref = f32[640,128]{1,0:T(8,128)S(1)} collective-permute-done((f32[640,128]{1,0:T(8,128)S(1)}, f32[640,128]{1,0:T(8,128)S(1)}, u32[]{:S(2)}, u32[]{:S(2)}) %collective-permute-start.1) | collective-permute-done | bytes 327712 | tf_op jit(solution)/shard_map/ppermute | solution.py:399
  15.0 1.4 %shard_map.47 = (f32[4,64,128]{2,1,0:T(8,128)S(1)}, f32[160,128]{1,0:T(8,128)S(1)}, f32[160,128]{1,0:T(8,128)S(1)}, f32[128,128]{1,0:T(8,128)S(1)}) custom-call(s32[2,64]{1,0:T(2,128)S(1)} %copy-done, s32[3]{0:T(128)S(1)} %pad_add_fusion.edge_ref, f32[512,128]{1,0:T(8,128)S(1)} %get-tuple-element.14.own_ref, f32[640,128]{1,0:T(8,128)S(1)} %collective-permute-done.near_ref, ...), custom_call_target="tpu_custom_call" | custom-call | flops 1000 | bytes 1000 | tf_op jit(solution)/shard_map/pallas_call | solution.py:402
  16.4 1.3 %collective-permute-start.2 = (f32[160,128]{1,0:T(8,128)S(1)}, f32[160,128]{1,0:T(8,128)S(1)}, u32[]{:S(2)}, u32[]{:S(2)}) collective-permute-start(f32[160,128]{1,0:T(8,128)S(1)} %get-tuple-element.20), channel_id=1, source_target_pairs={{0,1},{2,3},{1,0},{3,2},{4,5},{6,7},{5,4},{7,6},{8,9},{10,11},{9,8... | collective-permute-start | bytes 245768 | tf_op jit(solution)/shard_map/ppermute | solution.py:408
  17.6 1.9 %collective-permute-start.3 = (f32[160,128]{1,0:T(8,128)S(1)}, f32[160,128]{1,0:T(8,128)S(1)}, u32[]{:S(2)}, u32[]{:S(2)}) collective-permute-start(f32[160,128]{1,0:T(8,128)S(1)} %get-tuple-element.21), channel_id=1, source_target_pairs={{1,2},{2,1},{5,6},{6,5},{9,10},{10,9},{13,14},{14,13},{17,18},{18,... | collective-permute-start | bytes 245768 | tf_op jit(solution)/shard_map/ppermute | solution.py:407
  19.6 1.7 %collective-permute-done.2.near_ref = f32[160,128]{1,0:T(8,128)S(1)} collective-permute-done((f32[160,128]{1,0:T(8,128)S(1)}, f32[160,128]{1,0:T(8,128)S(1)}, u32[]{:S(2)}, u32[]{:S(2)}) %collective-permute-start.2) | collective-permute-done | bytes 81952 | tf_op jit(solution)/shard_map/ppermute | solution.py:408
  21.3 2.8 %collective-permute-done.3.far_ref = f32[160,128]{1,0:T(8,128)S(1)} collective-permute-done((f32[160,128]{1,0:T(8,128)S(1)}, f32[160,128]{1,0:T(8,128)S(1)}, u32[]{:S(2)}, u32[]{:S(2)}) %collective-permute-start.3) | collective-permute-done | bytes 81952 | tf_op jit(solution)/shard_map/ppermute | solution.py:407
  24.1 1.2 %shard_map.48 = f32[8,4,8,128]{3,2,1,0:T(8,128)S(1)} custom-call(s32[3]{0:T(128)S(1)} %pad_add_fusion.edge_ref, f32[4,64,128]{2,1,0:T(8,128)S(1)} %get-tuple-element.19.mine_ref, f32[160,128]{1,0:T(8,128)S(1)} %collective-permute-done.2.near_ref, f32[160,128]{1,0:T(8,128)S(1)} %collective-permute-done.3.far_ref, f32[128,128]{1,0:T(8,128)S(1)} %get-tuple-element.22.u_ref, ...), custom_call_target="tpu_custom_call" | custom-call | flops 1000 | bytes 1000 | tf_op jit(solution)/shard_map/pallas_call | solution.py:421
  25.2 17.3 %all_to_all.5.in_ref = f32[8,4,8,128]{3,2,1,0:T(8,128)S(1)} all-to-all(f32[8,4,8,128]{3,2,1,0:T(8,128)S(1)} %shard_map.48), channel_id=1, replica_groups=mesh['depth'=8,'imgy'=8,'imgx'=4] {'depth'}, dimensions={0} | all-to-all | bytes 262144 | tf_op jit(solution)/shard_map/all_to_all | solution.py:426
  42.6 0.6 %shard_map.49 = f32[4,8,128]{2,1,0:T(8,128)} custom-call(f32[8,4,8,128]{3,2,1,0:T(8,128)S(1)} %all_to_all.5.in_ref), custom_call_target="tpu_custom_call" | custom-call | flops 1000 | bytes 1000 | tf_op jit(solution)/shard_map/pallas_call | solution.py:427
  (12 shorter events, 0.1 us)
Async XLA Ops:
  0.0 9.0 %copy-start = (s32[2,64]{1,0:T(2,128)S(1)}, s32[2,64]{1,0:T(2,128)}, u32[]{:S(2)}) copy-start(s32[2,64]{1,0:T(2,128)} %shift_ref.1) | copy-start | bytes 1540
  0.0 9.0 %copy-start.2 = (f32[2,64]{1,0:T(2,128)S(1)}, f32[2,64]{1,0:T(2,128)}, u32[]{:S(2)}) copy-start(f32[2,64]{1,0:T(2,128)} %frac_hbm.1) | copy-start | bytes 1540
  0.0 9.1 %copy-start.1 = (f32[64]{0:T(128)S(1)}, f32[64]{0:T(128)}, u32[]{:S(2)}) copy-start(f32[64]{0:T(128)} %absorb_hbm.1) | copy-start | bytes 772
  6.5 3.6 %collective-permute-start = (f32[640,128]{1,0:T(8,128)S(1)}, f32[640,128]{1,0:T(8,128)S(1)}, u32[]{:S(2)}, u32[]{:S(2)}) collective-permute-start(f32[640,128]{1,0:T(8,128)S(1)} %get-tuple-element.15), channel_id=1, source_target_pairs={{0,4},{8,12},{16,20},{24,28},{4,0},{12,8},{20,16},{28,24},{1,5},{9... | collective-permute-start | bytes 983048 | tf_op jit(solution)/shard_map/ppermute | solution.py:400
  6.6 8.4 %collective-permute-start.1 = (f32[640,128]{1,0:T(8,128)S(1)}, f32[640,128]{1,0:T(8,128)S(1)}, u32[]{:S(2)}, u32[]{:S(2)}) collective-permute-start(f32[640,128]{1,0:T(8,128)S(1)} %get-tuple-element.16), channel_id=1, source_target_pairs={{4,8},{12,16},{20,24},{8,4},{16,12},{24,20},{5,9},{13,17},{21,25},... | collective-permute-start | bytes 983048 | tf_op jit(solution)/shard_map/ppermute | solution.py:399
  16.4 4.9 %collective-permute-start.2 = (f32[160,128]{1,0:T(8,128)S(1)}, f32[160,128]{1,0:T(8,128)S(1)}, u32[]{:S(2)}, u32[]{:S(2)}) collective-permute-start(f32[160,128]{1,0:T(8,128)S(1)} %get-tuple-element.20), channel_id=1, source_target_pairs={{0,1},{2,3},{1,0},{3,2},{4,5},{6,7},{5,4},{7,6},{8,9},{10,11},{9,8... | collective-permute-start | bytes 245768 | tf_op jit(solution)/shard_map/ppermute | solution.py:408
  17.6 6.4 %collective-permute-start.3 = (f32[160,128]{1,0:T(8,128)S(1)}, f32[160,128]{1,0:T(8,128)S(1)}, u32[]{:S(2)}, u32[]{:S(2)}) collective-permute-start(f32[160,128]{1,0:T(8,128)S(1)} %get-tuple-element.21), channel_id=1, source_target_pairs={{1,2},{2,1},{5,6},{6,5},{9,10},{10,9},{13,14},{14,13},{17,18},{18,... | collective-permute-start | bytes 245768 | tf_op jit(solution)/shard_map/ppermute | solution.py:407

commit v9 on v8

--- a/solution.py
+++ b/solution.py
@@ -70,8 +70,8 @@
 
 
 def tile_kernel(
-    scale, edge_ref, shift_hbm, frac_hbm, absorb_hbm, c_hbm, near_ref, own_ref, far_ref, rows_ref, cols_ref,
-    shift_ref, frac_ref, absorb_ref, c_ref, s2_ref, s1_ref, d_ref, plane_ref, acc_ref, sems,
+    scale, edge_ref, shift_hbm, frac_hbm, absorb_hbm, c_hbm, near_ref, acc_ref, far_ref, rows_ref, cols_ref,
+    shift_ref, frac_ref, absorb_ref, c_ref, s2_ref, s1_ref, d_ref, plane_ref, sems,
 ):
     def load(index, planes, rows):
         block = (pl.ds(*planes), pl.ds(*rows))
@@ -176,7 +176,7 @@
     lax.fori_loop(0, SLAB, slice_step, 0, unroll=SLICE_UNROLL)
 
     odd = edge_ref[0]
-    for start, out_ref in ((128 - 128 * odd, near_ref), (64, own_ref), (128 * odd, far_ref)):
+    for start, out_ref in ((128 - 128 * odd, near_ref), (128 * odd, far_ref)):
         for half in range(2):
             for channel in range(4):
                 value = acc_ref[4 * half + channel, pl.ds(pl.multiple_of(start, 64), 64), :]
@@ -260,7 +260,8 @@
     halves = []
     for half in range(2):
         pairs = [received(64 * (4 * half + c), 64) for c in range(4)]
-        own = [own_ref[pl.ds(64 * (4 * half + c), 64), :] for c in range(4)]
+        own = [own_ref[4 * half + c, pl.ds(64, 64), :] for c in range(4)]
+        own[3] = 1.0 - own[3]
         lower = [line[4 * half + c][:64] for c in range(4)]
         upper = [line[4 * half + c][64:] for c in range(4)]
         merged = over(own, over(upper, [above for _, above in pairs]))
@@ -360,7 +361,6 @@
         pltpu.VMEM((32, 32, COLS), jnp.float32),
         pltpu.VMEM((64, 64, COLS), jnp.float32),
         pltpu.VMEM((64, COLS), jnp.float32),
-        pltpu.VMEM((8, EXT, COLS), jnp.float32),
         pltpu.SemaphoreType.DMA((10,)),
     ]
 
@@ -389,7 +389,7 @@
     sent = f32(640, COLS)
     near, own, far, row_planes, col_planes = call(
         functools.partial(tile_kernel, scale),
-        (sent, f32(512, COLS), sent, f32(128, COLS), f32(64, COLS)),
+        (sent, f32(8, EXT, COLS), sent, f32(128, COLS), f32(64, COLS)),
         [SMEM_SPEC] + [HBM_SPEC] * 4,
         tile_scratch(),
         flops=300_000_000,

time: 43.4 us -> 43.5 us (level)
  no operation moved by 1% of the time
where the time goes in v9:
time: 43.5 us; the launch traced here: 43.3 us
  blocking collectives  17.4 us (40%)
  Pallas kernels  9.63 us (22%)
  waiting for transfers between devices  9.33 us (21%)
  starting transfers between devices  5.73 us (13%)
  local copies, waits for them, and re-layouts  0.67 us (2%)
    all_to_all x1, blocking collectives, body(): lax.all_to_all(pieces, 'depth', split_axis=0, concat_axis=0, tiled=True)  17.4 us
    pallas_call x1, Pallas kernels, body(): call(functools.partial(tile_kernel, scale), (sent, f32(8, EXT, COLS), sen...  6.47 us
    ppermute x1, waiting for transfers between devices, body(): far = lax.ppermute(far, 'imgy', matching(row_count, 1))  4.83 us
    ppermute x1, waiting for transfers between devices, body(): far = lax.ppermute(far, 'imgx', matching(col_count, 1))  2.79 us
    ppermute x1, starting transfers between devices, body(): far = lax.ppermute(far, 'imgy', matching(row_count, 1))  2.46 us
    ppermute x1, starting transfers between devices, body(): far = lax.ppermute(far, 'imgx', matching(col_count, 1))  1.91 us
    ppermute x1, waiting for transfers between devices, body(): near = lax.ppermute(near, 'imgx', matching(col_count, 0))  1.71 us
    pallas_call x1, Pallas kernels, body(): call(functools.partial(rows_kernel, scale), (f32(4, ROWS, COLS), packed,...  1.37 us
  transfers between devices with their start and end apart: 4, of which 3 were waited for; matrix products, arithmetic and copies ran while one was open for 2% of the time, Pallas kernels for 0%

profile of v9, /device:TPU:20, one launch (start us, length us, event | category | flops | bytes accessed | tf_op | source)
XLA Modules:
  0.0 43.3 jit_solution(5057733828750401902)
XLA Ops:
  0.0 0.0 copy-start
  0.0 0.0 copy-start.2
  0.0 0.0 copy-start.1
  0.0 0.1 pad_add_fusion.edge_ref
  0.1 6.5 %shard_map.46 = (f32[640,128]{1,0:T(8,128)S(1)}, f32[8,208,128]{2,1,0:T(8,128)S(1)}, f32[640,128]{1,0:T(8,128)S(1)}, f32[128,128]{1,0:T(8,128)S(1)}, f32[64,128]{1,0:T(8,128)S(1)}) custom-call(s32[3]{0:T(128)S(1)} %pad_add_fusion.edge_ref, s32[2,64]{1,0:T(2,128)} %shift_ref.1, f32[2,64]{1,0:T(2,128)} %frac_hbm.1, f32[64]{0:T(128)} %absorb_hbm.1, ...), custom_call_target="tpu_custom_call" | custom-call | flops 300000000 | bytes 4194304 | tf_op jit(solution)/shard_map/pallas_call | solution.py:390
  6.6 0.1 collective-permute-start
  6.7 2.5 %collective-permute-start.1 = (f32[640,128]{1,0:T(8,128)S(1)}, f32[640,128]{1,0:T(8,128)S(1)}, u32[]{:S(2)}, u32[]{:S(2)}) collective-permute-start(f32[640,128]{1,0:T(8,128)S(1)} %get-tuple-element.16), channel_id=1, source_target_pairs={{4,8},{12,16},{20,24},{8,4},{16,12},{24,20},{5,9},{13,17},{21,25},... | collective-permute-start | bytes 983048 | tf_op jit(solution)/shard_map/ppermute | solution.py:399
  9.1 0.0 copy-done
  9.2 0.0 copy-done.2
  9.2 0.0 copy-done.1
  9.2 0.1 broadcast_in_dim.53
  9.3 0.1 broadcast_in_dim.54
  9.5 0.1 tile.10
  9.6 0.1 copy.29
  9.7 0.1 broadcast_in_dim.55
  9.7 0.1 broadcast_in_dim_reshape.4.fy_ref
  9.8 0.2 select_reduce_fusion.3
  10.0 0.1 copy.31.zrow_ref
  10.1 0.1 select_reduce_fusion.1
  10.2 0.0 collective-permute-done.near_ref
  10.2 4.8 %collective-permute-done.1.far_ref = f32[640,128]{1,0:T(8,128)S(1)} collective-permute-done((f32[640,128]{1,0:T(8,128)S(1)}, f32[640,128]{1,0:T(8,128)S(1)}, u32[]{:S(2)}, u32[]{:S(2)}) %collective-permute-start.1) | collective-permute-done | bytes 327712 | tf_op jit(solution)/shard_map/ppermute | solution.py:399
  15.1 1.4 %shard_map.47 = (f32[4,64,128]{2,1,0:T(8,128)S(1)}, f32[160,128]{1,0:T(8,128)S(1)}, f32[160,128]{1,0:T(8,128)S(1)}, f32[128,128]{1,0:T(8,128)S(1)}) custom-call(s32[2,64]{1,0:T(2,128)S(1)} %copy-done, s32[3]{0:T(128)S(1)} %pad_add_fusion.edge_ref, f32[8,208,128]{2,1,0:T(8,128)S(1)} %get-tuple-element.14.own_ref, ...), custom_call_target="tpu_custom_call" | custom-call | flops 1000 | bytes 1000 | tf_op jit(solution)/shard_map/pallas_call | solution.py:402
  16.5 1.3 %collective-permute-start.2 = (f32[160,128]{1,0:T(8,128)S(1)}, f32[160,128]{1,0:T(8,128)S(1)}, u32[]{:S(2)}, u32[]{:S(2)}) collective-permute-start(f32[160,128]{1,0:T(8,128)S(1)} %get-tuple-element.20), channel_id=1, source_target_pairs={{0,1},{2,3},{1,0},{3,2},{4,5},{6,7},{5,4},{7,6},{8,9},{10,11},{9,8... | collective-permute-start | bytes 245768 | tf_op jit(solution)/shard_map/ppermute | solution.py:408
  17.7 1.9 %collective-permute-start.3 = (f32[160,128]{1,0:T(8,128)S(1)}, f32[160,128]{1,0:T(8,128)S(1)}, u32[]{:S(2)}, u32[]{:S(2)}) collective-permute-start(f32[160,128]{1,0:T(8,128)S(1)} %get-tuple-element.21), channel_id=1, source_target_pairs={{1,2},{2,1},{5,6},{6,5},{9,10},{10,9},{13,14},{14,13},{17,18},{18,... | collective-permute-start | bytes 245768 | tf_op jit(solution)/shard_map/ppermute | solution.py:407
  19.7 1.7 %collective-permute-done.2.near_ref = f32[160,128]{1,0:T(8,128)S(1)} collective-permute-done((f32[160,128]{1,0:T(8,128)S(1)}, f32[160,128]{1,0:T(8,128)S(1)}, u32[]{:S(2)}, u32[]{:S(2)}) %collective-permute-start.2) | collective-permute-done | bytes 81952 | tf_op jit(solution)/shard_map/ppermute | solution.py:408
  21.4 2.8 %collective-permute-done.3.far_ref = f32[160,128]{1,0:T(8,128)S(1)} collective-permute-done((f32[160,128]{1,0:T(8,128)S(1)}, f32[160,128]{1,0:T(8,128)S(1)}, u32[]{:S(2)}, u32[]{:S(2)}) %collective-permute-start.3) | collective-permute-done | bytes 81952 | tf_op jit(solution)/shard_map/ppermute | solution.py:407
  24.2 1.2 %shard_map.48 = f32[8,4,8,128]{3,2,1,0:T(8,128)S(1)} custom-call(s32[3]{0:T(128)S(1)} %pad_add_fusion.edge_ref, f32[4,64,128]{2,1,0:T(8,128)S(1)} %get-tuple-element.19.mine_ref, f32[160,128]{1,0:T(8,128)S(1)} %collective-permute-done.2.near_ref, f32[160,128]{1,0:T(8,128)S(1)} %collective-permute-done.3.far_ref, f32[128,128]{1,0:T(8,128)S(1)} %get-tuple-element.22.u_ref, ...), custom_call_target="tpu_custom_call" | custom-call | flops 1000 | bytes 1000 | tf_op jit(solution)/shard_map/pallas_call | solution.py:421
  25.3 17.4 %all_to_all.5.in_ref = f32[8,4,8,128]{3,2,1,0:T(8,128)S(1)} all-to-all(f32[8,4,8,128]{3,2,1,0:T(8,128)S(1)} %shard_map.48), channel_id=1, replica_groups=mesh['depth'=8,'imgy'=8,'imgx'=4] {'depth'}, dimensions={0} | all-to-all | bytes 262144 | tf_op jit(solution)/shard_map/all_to_all | solution.py:426
  42.7 0.6 %shard_map.49 = f32[4,8,128]{2,1,0:T(8,128)} custom-call(f32[8,4,8,128]{3,2,1,0:T(8,128)S(1)} %all_to_all.5.in_ref), custom_call_target="tpu_custom_call" | custom-call | flops 1000 | bytes 1000 | tf_op jit(solution)/shard_map/pallas_call | solution.py:427
  (12 shorter events, 0.1 us)
Async XLA Ops:
  0.0 9.1 %copy-start = (s32[2,64]{1,0:T(2,128)S(1)}, s32[2,64]{1,0:T(2,128)}, u32[]{:S(2)}) copy-start(s32[2,64]{1,0:T(2,128)} %shift_ref.1) | copy-start | bytes 1540
  0.0 9.2 %copy-start.2 = (f32[2,64]{1,0:T(2,128)S(1)}, f32[2,64]{1,0:T(2,128)}, u32[]{:S(2)}) copy-start(f32[2,64]{1,0:T(2,128)} %frac_hbm.1) | copy-start | bytes 1540
  0.0 9.2 %copy-start.1 = (f32[64]{0:T(128)S(1)}, f32[64]{0:T(128)}, u32[]{:S(2)}) copy-start(f32[64]{0:T(128)} %absorb_hbm.1) | copy-start | bytes 772
  6.6 3.7 %collective-permute-start = (f32[640,128]{1,0:T(8,128)S(1)}, f32[640,128]{1,0:T(8,128)S(1)}, u32[]{:S(2)}, u32[]{:S(2)}) collective-permute-start(f32[640,128]{1,0:T(8,128)S(1)} %get-tuple-element.15), channel_id=1, source_target_pairs={{0,4},{8,12},{16,20},{24,28},{4,0},{12,8},{20,16},{28,24},{1,5},{9... | collective-permute-start | bytes 983048 | tf_op jit(solution)/shard_map/ppermute | solution.py:400
  6.7 8.4 %collective-permute-start.1 = (f32[640,128]{1,0:T(8,128)S(1)}, f32[640,128]{1,0:T(8,128)S(1)}, u32[]{:S(2)}, u32[]{:S(2)}) collective-permute-start(f32[640,128]{1,0:T(8,128)S(1)} %get-tuple-element.16), channel_id=1, source_target_pairs={{4,8},{12,16},{20,24},{8,4},{16,12},{24,20},{5,9},{13,17},{21,25},... | collective-permute-start | bytes 983048 | tf_op jit(solution)/shard_map/ppermute | solution.py:399
  16.5 4.9 %collective-permute-start.2 = (f32[160,128]{1,0:T(8,128)S(1)}, f32[160,128]{1,0:T(8,128)S(1)}, u32[]{:S(2)}, u32[]{:S(2)}) collective-permute-start(f32[160,128]{1,0:T(8,128)S(1)} %get-tuple-element.20), channel_id=1, source_target_pairs={{0,1},{2,3},{1,0},{3,2},{4,5},{6,7},{5,4},{7,6},{8,9},{10,11},{9,8... | collective-permute-start | bytes 245768 | tf_op jit(solution)/shard_map/ppermute | solution.py:408
  17.7 6.4 %collective-permute-start.3 = (f32[160,128]{1,0:T(8,128)S(1)}, f32[160,128]{1,0:T(8,128)S(1)}, u32[]{:S(2)}, u32[]{:S(2)}) collective-permute-start(f32[160,128]{1,0:T(8,128)S(1)} %get-tuple-element.21), channel_id=1, source_target_pairs={{1,2},{2,1},{5,6},{6,5},{9,10},{10,9},{13,14},{14,13},{17,18},{18,... | collective-permute-start | bytes 245768 | tf_op jit(solution)/shard_map/ppermute | solution.py:407
